TPU v7x, 32 devices: a whole 2x2x4 slice. The times are simulated.
32 devices in a mesh: brick: 16 (over z, x, core), view: 2 (over y).
Axes of the slice: x: 2, y: 2, z: 4, core: 2. Of those that a mesh axis runs over, the one named last changes fastest.
Arguments:
- estimate: float32 [128, 64, 512], P('brick'), may hold values from 0.5 to 2
- camera_blocks: bfloat16 [2, 256, 8, 2048], P('view', 'brick'), may hold values from 0.099609375 to 2
- block_lists: int32 [2, 16, 16, 2], P('view'), may hold values from -1 to 15, as said below
- block_offsets: int32 [2, 256], P('view'), may hold values from 1 to 124, as said below
- psf_index: int32 [2, 64], P('view'), may hold values from 0 to 15
- psf_bank: float32 [2, 2, 16, 9], P('view'), may hold values from 0.03 to 0.3
Outputs:
- updated: float32 [128, 64, 512], P('brick')
Inputs may be any that keep to these rules, and one draw needn't show every extreme that they name: block_lists[v, d, s] names exactly the blocks of holder s that intersect brick d, each once; at most 2 of them, and 2 for some brick and holder. `block_offsets`: every block starts after its brick's first row by 1 to 4 rows.
All inputs are finite; a program needn't handle non-finite values.
Results may differ from a plain program's by a relative error of at most 0.0003.
Values may be sent and summed in bfloat16 or wider, within the bound.
No kernel may reach another device: no remote copies, remote signals or barrier semaphores. Data moves between devices by JAX's collectives and lax.ppermute only.
A program may use at most 128 MiB of HBM per device.

v0:
```python
import jax
import jax.numpy as jnp
from jax import lax
from jax.sharding import PartitionSpec as P


def with_halo(cells, sides, width):
    for axis, dim in sides:
        count = lax.axis_size(axis)
        ends = count - 1
        head = lax.slice_in_dim(cells, 0, width, axis=dim)
        tail = lax.slice_in_dim(cells, cells.shape[dim] - width, cells.shape[dim], axis=dim)
        cells = jnp.concatenate(
            [
                lax.ppermute(tail, axis, [(i, (i + 1) % count) for i in range(ends)]),
                cells,
                lax.ppermute(head, axis, [((i + 1) % count, i) for i in range(ends)]),
            ],
            axis=dim,
        )
    return cells


def joined(value, axis, join):
    pieces = lax.all_gather(value, axis)
    head = pieces[0]
    tail = pieces[1:]
    running, _ = lax.scan(lambda running, slab: (join(running, slab), None), head, tail)
    return running


def blur_cols(field, kern, reverse):
    tap_count = kern.shape[1]
    radius = tap_count // 2
    width = field.shape[2]
    padded = jnp.pad(field, ((0, 0), (0, 0), (radius, radius)))
    result = None
    for offset in range(tap_count):
        begin_at = 2 * radius - offset if reverse else offset
        term = kern[:, offset][None, :, None] * padded[:, :, begin_at : begin_at + width]
        result = term if result is None else result + term
    return result


def blur_rows(padded, kern, reverse, rows):
    tap_count = kern.shape[1]
    radius = tap_count // 2
    result = None
    for offset in range(tap_count):
        begin_at = 2 * radius - offset if reverse else offset
        term = kern[:, offset][None, :, None] * padded[begin_at : begin_at + rows]
        result = term if result is None else result + term
    return result


def place_blocks(blocks, column_ids, row_starts, is_valid, start_x, rows_dev, depth, column_count):
    block_rows = blocks.shape[1]
    block_cols = column_count // 1
    local_rows = row_starts[:, None] + jnp.arange(block_rows, dtype=jnp.int32)[None, :] - start_x
    row_hit = (
        local_rows[:, :, None] == jnp.arange(rows_dev, dtype=jnp.int32)[None, None, :]
    ) & is_valid[:, None, None]
    colhot = column_ids[:, None] == jnp.arange(column_count, dtype=jnp.int32)[None, :]
    weight = (row_hit[:, :, :, None] & colhot[:, None, None, :]).astype(jnp.bfloat16)
    summed = jnp.einsum("sabc,saf->bcf", weight, blocks, preferred_element_type=jnp.float32)
    block_width = blocks.shape[2] // depth
    summed = summed.reshape(rows_dev, block_cols, depth, block_width)
    return summed.transpose(0, 2, 1, 3).reshape(rows_dev, depth, block_cols * block_width)


def multiply(first_value, second_value):
    return first_value * second_value


def shards(estimate, camera_blocks, block_lists, block_offsets, psf_index, psf_bank):
    rows_dev, depth, columns = estimate.shape
    tile_count = camera_blocks.shape[1]
    block_rows = camera_blocks.shape[2]
    brick_here = lax.axis_index("brick")
    start_x = brick_here * rows_dev
    tap_count = psf_bank.shape[-1]
    radius = tap_count // 2
    kern_count = psf_bank.shape[2]
    kernel_pick = (
        psf_index[0][:, None] == jnp.arange(kern_count, dtype=jnp.int32)[None, :]
    ).astype(jnp.float32)
    kern_x = jnp.dot(kernel_pick, psf_bank[0, 0], precision=lax.Precision.HIGHEST)
    kern_y = jnp.dot(kernel_pick, psf_bank[0, 1], precision=lax.Precision.HIGHEST)
    offsets_view = block_offsets[0]
    route_table = block_lists[0]
    outgoing = lax.dynamic_index_in_dim(route_table, brick_here, 1, keepdims=False)
    chosen = jnp.take(camera_blocks[0], jnp.maximum(outgoing, 0), axis=0)
    chosen = chosen * (outgoing >= 0)[:, :, None, None].astype(jnp.bfloat16)
    arrived = lax.all_to_all(chosen, "brick", split_axis=0, concat_axis=0, tiled=True)
    incoming = lax.dynamic_index_in_dim(route_table, brick_here, 0, keepdims=False)
    brick_count, capacity = incoming.shape
    sources = (
        jnp.arange(brick_count, dtype=jnp.int32)[:, None] * tile_count + jnp.maximum(incoming, 0)
    ).reshape(-1)
    measured = place_blocks(
        arrived.reshape(brick_count * capacity, block_rows, -1),
        sources % tile_count,
        jnp.take(offsets_view, sources),
        (incoming >= 0).reshape(-1),
        start_x,
        rows_dev,
        depth,
        tile_count,
    )
    padded = with_halo(estimate, (("brick", 0),), radius)
    blurred = blur_rows(blur_cols(padded, kern_y, False), kern_x, False, rows_dev)
    ratio = measured / blurred
    padded_ratio = with_halo(ratio, (("brick", 0),), radius)
    correction = blur_rows(blur_cols(padded_ratio, kern_y, True), kern_x, True, rows_dev)
    product = joined(correction, "view", multiply)
    return estimate * product


def solution(mesh):
    placed = (
        P("brick", None, None),
        P("view", "brick", None, None),
        P("view", None, None, None),
        P("view", None),
        P("view", None),
        P("view", None, None, None),
    )
    return jax.shard_map(
        shards, mesh=mesh, in_specs=placed, out_specs=P("brick", None, None), check_vma=False
    )
```

profile of v0, /device:TPU:8, one launch (start us, length us, event | category | flops | bytes accessed | tf_op | source)
XLA Modules:
  0.0 151.4 jit_solution(978949546729310310)
XLA Ops:
  6.5 0.9 constant_dynamic-slice_fusion
  7.5 0.1 copy.76
  7.6 0.1 copy.59
  7.7 0.1 copy.57
  7.8 0.1 copy.58
  7.8 0.1 reshape.205
  8.0 0.0 copy-done
  8.0 0.0 copy-start.6
  8.0 0.0 copy-start.7
  8.0 0.0 copy-start.1
  8.0 0.6 gather_fusion.1
  8.6 1.2 select_multiply_fusion
  9.8 6.3 %all-to-all-start = ((bf16[16,2,8,2048]{3,2,1,0:T(8,128)(2,1)}), bf16[16,2,8,2048]{3,2,1,0:T(8,128)(2,1)}, u32[]{:S(2)}, u32[]{:S(2)}) async-start(bf16[16,2,8,2048]{3,2,1,0:T(8,128)(2,1)} %select_multiply_fusion), calls=%async_computation | async-start | bytes 2097152 | tf_op jit(solution)/shard_map/all_to_all | solution.py:94
  16.0 0.0 all-gather.3.cloned.1.call-start
  16.1 1.1 fusion.48
  17.2 2.0 %collective-permute-start = (f32[4,64,512]{2,1,0:T(8,128)}, f32[4,64,512]{2,1,0:T(8,128)}, u32[]{:S(2)}, u32[]{:S(2)}) collective-permute-start(f32[4,64,512]{2,1,0:T(8,128)} %get-tuple-element.16), channel_id=1, source_target_pairs={{0,2},{2,4},{4,6},{6,8},{8,10},{10,12},{12,14},{14,16},{16,18},{18... | collective-permute-start | bytes 1572872 | tf_op jit(solution)/shard_map/ppermute | solution.py:15
  19.2 4.4 %collective-permute-start.1 = (f32[4,64,512]{2,1,0:T(8,128)}, f32[4,64,512]{2,1,0:T(8,128)S(1)}, u32[]{:S(2)}, u32[]{:S(2)}) collective-permute-start(f32[4,64,512]{2,1,0:T(8,128)} %get-tuple-element.17), channel_id=1, source_target_pairs={{2,0},{4,2},{6,4},{8,6},{10,8},{12,10},{14,12},{16,14},{18,16},{20... | collective-permute-start | bytes 1572872 | tf_op jit(solution)/shard_map/ppermute | solution.py:17
  23.6 0.7 dynamic-slice_maximum_fusion
  24.3 0.1 copy.53
  24.4 0.1 max.43
  24.5 0.1 max.42
  24.6 0.1 add.195
  24.7 0.1 add.201
  24.8 0.1 add.196
  24.9 0.1 copy.75
  25.0 0.2 fusion.37
  25.2 0.0 copy-done.1
  25.2 0.7 gather_fusion
  26.0 1.9 %copy.64 = f32[8,64,512]{1,2,0:T(8,128)} copy(f32[8,64,512]{2,1,0:T(8,128)S(1)} %copy-done.3) | data formatting | bytes 2097152 | tf_op args[0]
  27.9 0.1 copy.74
  28.0 0.2 fusion.38
  28.2 0.9 dynamic-slice_compare_fusion
  29.1 0.1 copy.55
  29.2 0.1 ge.40
  29.3 13.4 %collective-permute-done = f32[4,64,512]{2,1,0:T(8,128)} collective-permute-done((f32[4,64,512]{2,1,0:T(8,128)}, f32[4,64,512]{2,1,0:T(8,128)}, u32[]{:S(2)}, u32[]{:S(2)}) %collective-permute-start) | collective-permute-done | bytes 524320 | tf_op jit(solution)/shard_map/ppermute | solution.py:15
  42.8 2.4 %copy.63 = f32[4,64,512]{1,2,0:T(8,128)} copy(f32[4,64,512]{2,1,0:T(8,128)} %collective-permute-done) | data formatting | bytes 1048576 | tf_op jit(solution)/shard_map/ppermute | solution.py:15
  45.1 0.0 collective-permute-done.1
  45.1 1.3 copy.65
  46.4 1.9 %pad_maximum_fusion = f32[16,64,512]{1,2,0:T(8,128)S(1)} fusion(f32[4,64,512]{1,2,0:T(8,128)} %copy.65, f32[8,64,512]{1,2,0:T(8,128)S(1)} %copy-done.5, f32[4,64,512]{1,2,0:T(8,128)} %copy.63), kind=kLoop, calls=%fused_computation.2 | loop fusion | flops 1048576 | bytes 4194304 | tf_op jit(solution)/shard_map/concatenate | solution.py:13
  48.3 6.1 %multiply_add_fusion.1 = f32[16,64,512]{1,2,0:T(8,128)} fusion(f32[16,64,512]{1,2,0:T(8,128)S(1)} %pad_maximum_fusion, f32[64]{0:T(128)S(1)} %get-tuple-element.30, f32[64]{0:T(128)S(1)} %get-tuple-element.31, f32[64]{0:T(128)S(1)} %get-tuple-element.32, f32[64]{0:T(128)S(1)} %get-tuple-element.33, f32[64]{0:T(128)S(1)} %get-tuple-element.34, ...), kind=kLoop, calls=%fused_computation.13 | loop fusion | flops 8912896 | bytes 4196608 | tf_op jit(solution)/shard_map/add | solution.py:41
  54.4 0.0 all-to-all-done
  54.4 1.8 %copy.78 = bf16[32,8,2048]{2,0,1:T(8,128)(2,1)S(1)} copy(bf16[32,8,2048]{2,1,0:T(8,128)(2,1)} %bitcast.13) | data formatting | bytes 2097152 | tf_op jit(solution)/shard_map/reshape | solution.py:101
  56.2 4.5 %dot_general.16 = bf16[64,32,8,32]{1,0,3,2:T(8,128)(2,1)} reshape(bf16[2048,8,32]{0,2,1:T(8,128)(2,1)S(1)} %bitcast.87) | data formatting | bytes 2097152 | tf_op jit(solution)/shard_map/sabc,saf->bcf/dot_general | solution.py:65
  60.7 5.1 %copy.61 = bf16[64,32,8,32]{0,3,2,1:T(8,128)(2,1)S(1)} copy(bf16[64,32,8,32]{1,0,3,2:T(8,128)(2,1)} %dot_general.16) | data formatting | bytes 2097152 | tf_op jit(solution)/shard_map/sabc,saf->bcf/dot_general | solution.py:65
  65.9 0.8 fusion.29
  66.6 0.6 copy.62
  67.3 0.8 copy-done.2
  68.0 1.7 %fusion.19 = f32[8,64,512]{1,2,0:T(8,128)S(1)} fusion(f32[16,64,512]{1,2,0:T(8,128)S(1)} %copy-done.2, f32[8,64,16,32]{1,3,2,0:T(8,128)S(1)} %copy.62, f32[64]{0:T(128)S(1)} %get-tuple-element.21, f32[64]{0:T(128)S(1)} %get-tuple-element.22, f32[64]{0:T(128)S(1)} %get-tuple-element.23, f32[64]{0:T(128)S(1)} %get-tuple-element.24, ...), kind=kLoop, calls=%fused_computation.41 | loop fusion | flops 4718592 | bytes 11536640 | tf_op jit(solution)/shard_map/div | solution.py:112
  69.8 1.5 fusion.47
  71.3 1.5 %copy.66 = f32[4,64,512]{2,1,0:T(8,128)S(1)} copy(f32[4,64,512]{1,2,0:T(8,128)} %get-tuple-element.12) | data formatting | bytes 1048576 | tf_op jit(solution)/shard_map/slice | solution.py:12
  72.8 1.9 %collective-permute-start.2 = (f32[4,64,512]{2,1,0:T(8,128)S(1)}, f32[4,64,512]{2,1,0:T(8,128)}, u32[]{:S(2)}, u32[]{:S(2)}) collective-permute-start(f32[4,64,512]{2,1,0:T(8,128)S(1)} %copy.66), channel_id=1, source_target_pairs={{0,2},{2,4},{4,6},{6,8},{8,10},{10,12},{12,14},{14,16},{16,18},{18... | collective-permute-start | bytes 1572872 | tf_op jit(solution)/shard_map/ppermute | solution.py:15
  74.8 2.3 %copy.67 = f32[4,64,512]{2,1,0:T(8,128)} copy(f32[4,64,512]{1,2,0:T(8,128)} %get-tuple-element.14) | data formatting | bytes 1048576 | tf_op jit(solution)/shard_map/slice | solution.py:11
  77.1 4.7 %collective-permute-start.3 = (f32[4,64,512]{2,1,0:T(8,128)}, f32[4,64,512]{2,1,0:T(8,128)}, u32[]{:S(2)}, u32[]{:S(2)}) collective-permute-start(f32[4,64,512]{2,1,0:T(8,128)} %copy.67), channel_id=1, source_target_pairs={{2,0},{4,2},{6,4},{8,6},{10,8},{12,10},{14,12},{16,14},{18,16},{20... | collective-permute-start | bytes 1572872 | tf_op jit(solution)/shard_map/ppermute | solution.py:17
  81.8 2.5 %collective-permute-done.2 = f32[4,64,512]{2,1,0:T(8,128)} collective-permute-done((f32[4,64,512]{2,1,0:T(8,128)S(1)}, f32[4,64,512]{2,1,0:T(8,128)}, u32[]{:S(2)}, u32[]{:S(2)}) %collective-permute-start.2) | collective-permute-done | bytes 524320 | tf_op jit(solution)/shard_map/ppermute | solution.py:15
  84.3 2.4 %copy.68 = f32[4,64,512]{1,2,0:T(8,128)} copy(f32[4,64,512]{2,1,0:T(8,128)} %collective-permute-done.2) | data formatting | bytes 1048576 | tf_op jit(solution)/shard_map/ppermute | solution.py:15
  86.7 1.9 %collective-permute-done.3 = f32[4,64,512]{2,1,0:T(8,128)} collective-permute-done((f32[4,64,512]{2,1,0:T(8,128)}, f32[4,64,512]{2,1,0:T(8,128)}, u32[]{:S(2)}, u32[]{:S(2)}) %collective-permute-start.3) | collective-permute-done | bytes 524320 | tf_op jit(solution)/shard_map/ppermute | solution.py:17
  88.6 2.4 %copy.69 = f32[4,64,512]{1,2,0:T(8,128)} copy(f32[4,64,512]{2,1,0:T(8,128)} %collective-permute-done.3) | data formatting | bytes 1048576 | tf_op jit(solution)/shard_map/ppermute | solution.py:17
  91.0 1.9 %pad_maximum_fusion.1 = f32[16,64,512]{1,2,0:T(8,128)S(1)} fusion(f32[4,64,512]{1,2,0:T(8,128)} %copy.69, f32[8,64,512]{1,2,0:T(8,128)S(1)} %fusion.19, f32[4,64,512]{1,2,0:T(8,128)} %copy.68), kind=kLoop, calls=%fused_computation.3 | loop fusion | flops 1048576 | bytes 4194304 | tf_op jit(solution)/shard_map/concatenate | solution.py:13
  92.9 5.3 %multiply_add_fusion = f32[16,64,512]{1,2,0:T(8,128)S(1)} fusion(f32[16,64,512]{1,2,0:T(8,128)S(1)} %pad_maximum_fusion.1, f32[64]{0:T(128)S(1)} %get-tuple-element.30, f32[64]{0:T(128)S(1)} %get-tuple-element.31, f32[64]{0:T(128)S(1)} %get-tuple-element.32, f32[64]{0:T(128)S(1)} %get-tuple-element.33, f32[64]{0:T(128)S(1)} %get-tuple-element.34, ...), kind=kLoop, calls=%fused_computation.4 | loop fusion | flops 8912896 | bytes 4196608 | tf_op jit(solution)/shard_map/add | solution.py:41
  98.2 2.3 %fusion.10 = f32[8,64,512]{1,2,0:T(8,128)} fusion(f32[16,64,512]{1,2,0:T(8,128)S(1)} %multiply_add_fusion, f32[64]{0:T(128)S(1)} %get-tuple-element.21, f32[64]{0:T(128)S(1)} %get-tuple-element.22, f32[64]{0:T(128)S(1)} %get-tuple-element.23, f32[64]{0:T(128)S(1)} %get-tuple-element.24, f32[64]{0:T(128)S(1)} %get-tuple-element.25, ...), kind=kLoop, calls=%fused_computation.23 | loop fusion | flops 4456448 | bytes 10488064 | tf_op jit(solution)/shard_map/add | solution.py:52
  100.4 3.2 %copy.70 = f32[8,64,512]{2,1,0:T(8,128)} copy(f32[8,64,512]{1,2,0:T(8,128)} %fusion.10) | data formatting | bytes 2097152 | tf_op jit(solution)/shard_map/add | solution.py:52
  103.7 0.0 all-gather.3.cloned.1.call-update
  103.7 38.0 %all-gather.3.cloned.1.call-done = f32[16,64,512]{2,1,0:T(8,128)} async-done(((f32[8,64,512]{2,1,0:T(8,128)}), f32[16,64,512]{2,1,0:T(8,128)}) %all-gather.3.cloned.1.call-update) | async-done | bytes 2097168 | tf_op jit(solution)/shard_map/all_gather | solution.py:25
  141.7 2.9 %fusion.32 = f32[8,64,512]{2,1,0:T(8,128)} fusion(f32[8,64,512]{2,1,0:T(8,128)S(1)} %copy-done.4, f32[16,64,512]{2,1,0:T(8,128)} %all-gather.3.cloned.1.call-done), kind=kLoop, calls=%fused_computation.61 | loop fusion | flops 524288 | bytes 4194304 | tf_op jit(solution)/shard_map/mul | solution.py:116
  (23 shorter events, 0.1 us)
Async XLA Ops:
  6.5 1.4 copy-start
  6.5 9.6 %copy-start.3 = (f32[8,64,512]{2,1,0:T(8,128)S(1)}, f32[8,64,512]{2,1,0:T(8,128)}, u32[]{:S(2)}) copy-start(f32[8,64,512]{2,1,0:T(8,128)} %param.6) | copy-start | bytes 3145732
  8.0 16.9 %copy-start.6 = (f32[1,2,16,9]{2,1,3,0:T(2,128)S(1)}, f32[1,2,16,9]{2,1,3,0:T(2,128)}, u32[]{:S(2)}) copy-start(f32[1,2,16,9]{2,1,3,0:T(2,128)} %param.11) | copy-start | bytes 3460
  8.0 17.0 %copy-start.7 = (s32[1,64]{1,0:T(1,128)S(1)}, s32[1,64]{1,0:T(1,128)}, u32[]{:S(2)}) copy-start(s32[1,64]{1,0:T(1,128)} %param.10) | copy-start | bytes 772
  8.0 17.2 %copy-start.1 = (s32[1,256]{1,0:T(1,128)S(1)}, s32[1,256]{1,0:T(1,128)}, u32[]{:S(2)}) copy-start(s32[1,256]{1,0:T(1,128)} %param.9) | copy-start | bytes 3076
  9.8 44.7 %all-to-all-start = ((bf16[16,2,8,2048]{3,2,1,0:T(8,128)(2,1)}), bf16[16,2,8,2048]{3,2,1,0:T(8,128)(2,1)}, u32[]{:S(2)}, u32[]{:S(2)}) async-start(bf16[16,2,8,2048]{3,2,1,0:T(8,128)(2,1)} %select_multiply_fusion), calls=%async_computation | async-start | bytes 2097152 | tf_op jit(solution)/shard_map/all_to_all | solution.py:94
  16.0 125.6 %all-gather.3.cloned.1.call-start = ((), (), s32[]{:S(2)}) async-start(), calls=%async_computation.1 | async-start | bytes 3145728 | tf_op jit(solution)/shard_map/all_gather | solution.py:25
  17.2 25.6 %collective-permute-start = (f32[4,64,512]{2,1,0:T(8,128)}, f32[4,64,512]{2,1,0:T(8,128)}, u32[]{:S(2)}, u32[]{:S(2)}) collective-permute-start(f32[4,64,512]{2,1,0:T(8,128)} %get-tuple-element.16), channel_id=1, source_target_pairs={{0,2},{2,4},{4,6},{6,8},{8,10},{10,12},{12,14},{14,16},{16,18},{18... | collective-permute-start | bytes 1572872 | tf_op jit(solution)/shard_map/ppermute | solution.py:15
  19.2 25.9 %collective-permute-start.1 = (f32[4,64,512]{2,1,0:T(8,128)}, f32[4,64,512]{2,1,0:T(8,128)S(1)}, u32[]{:S(2)}, u32[]{:S(2)}) collective-permute-start(f32[4,64,512]{2,1,0:T(8,128)} %get-tuple-element.17), channel_id=1, source_target_pairs={{2,0},{4,2},{6,4},{8,6},{10,8},{12,10},{14,12},{16,14},{18,16},{20... | collective-permute-start | bytes 1572872 | tf_op jit(solution)/shard_map/ppermute | solution.py:17
  27.9 18.5 %copy-start.5 = (f32[8,64,512]{1,2,0:T(8,128)S(1)}, f32[8,64,512]{1,2,0:T(8,128)}, u32[]{:S(2)}) copy-start(f32[8,64,512]{1,2,0:T(8,128)} %copy.64) | copy-start | bytes 3145732
  65.9 2.2 %copy-start.2 = (f32[16,64,512]{1,2,0:T(8,128)S(1)}, f32[16,64,512]{1,2,0:T(8,128)}, u32[]{:S(2)}) copy-start(f32[16,64,512]{1,2,0:T(8,128)} %multiply_add_fusion.1) | copy-start | bytes 6291460
  72.8 11.5 %collective-permute-start.2 = (f32[4,64,512]{2,1,0:T(8,128)S(1)}, f32[4,64,512]{2,1,0:T(8,128)}, u32[]{:S(2)}, u32[]{:S(2)}) collective-permute-start(f32[4,64,512]{2,1,0:T(8,128)S(1)} %copy.66), channel_id=1, source_target_pairs={{0,2},{2,4},{4,6},{6,8},{8,10},{10,12},{12,14},{14,16},{16,18},{18... | collective-permute-start | bytes 1572872 | tf_op jit(solution)/shard_map/ppermute | solution.py:15
  77.1 11.5 %collective-permute-start.3 = (f32[4,64,512]{2,1,0:T(8,128)}, f32[4,64,512]{2,1,0:T(8,128)}, u32[]{:S(2)}, u32[]{:S(2)}) collective-permute-start(f32[4,64,512]{2,1,0:T(8,128)} %copy.67), channel_id=1, source_target_pairs={{2,0},{4,2},{6,4},{8,6},{10,8},{12,10},{14,12},{16,14},{18,16},{20... | collective-permute-start | bytes 1572872 | tf_op jit(solution)/shard_map/ppermute | solution.py:17
  100.4 41.3 %copy-start.4 = (f32[8,64,512]{2,1,0:T(8,128)S(1)}, f32[8,64,512]{2,1,0:T(8,128)}, u32[]{:S(2)}) copy-start(f32[8,64,512]{2,1,0:T(8,128)} %param.6) | copy-start | bytes 3145732
Sparse Core Ops, SparseCore 0:
  103.8 37.8 all-gather.2
where the time goes:
time: 154 us; the launch traced here: 151 us
  waiting for transfers between devices  55.9 us (36%)
  local copies, waits for them, and re-layouts  36.4 us (24%)
  other arithmetic  24.8 us (16%)
  starting transfers between devices  19.4 us (13%)
  between operations  13.7 us (9%)
    all_gather x1, waiting for transfers between devices, joined(): pieces = lax.all_gather(value, axis)  38 us
    ppermute x2, waiting for transfers between devices, with_halo(): lax.ppermute(tail, axis, [(i, (i + 1) % count) for i in range(ends)])  16 us
    add x2, other arithmetic, blur_cols(): result = term if result is None else result + term  11.3 us
    dot_general x2, local copies, waits for them, and re-layouts, place_blocks(): jnp.einsum('sabc,saf->bcf', weight, blocks, preferred_element_type=jnp.fl...  9.61 us
    ppermute x2, starting transfers between devices, with_halo(): lax.ppermute(head, axis, [((i + 1) % count, i) for i in range(ends)])  9.15 us
    all_to_all x1, starting transfers between devices, shards(): lax.all_to_all(chosen, 'brick', split_axis=0, concat_axis=0, tiled=True)  6.27 us
    ppermute x2, local copies, waits for them, and re-layouts, with_halo(): lax.ppermute(tail, axis, [(i, (i + 1) % count) for i in range(ends)])  4.74 us
    slice x3, local copies, waits for them, and re-layouts, with_halo(): lax.slice_in_dim(cells, cells.shape[dim] - width, cells.shape[dim], axis=...  4.1 us
  transfers between devices with their start and end apart: 6, of which 4 were waited for; matrix products, arithmetic and copies ran while one was open for 15% of the time, Pallas kernels for 0%

commit v1 on v0

v1 whole, which is shorter than its diff:
```python
import functools

import jax
import jax.numpy as jnp
from jax import lax
from jax.experimental import pallas as pl
from jax.experimental.pallas import tpu as pltpu
from jax.sharding import PartitionSpec as P

LANES = 128
SUBLANES = 8
VMEM = pl.BlockSpec(memory_space=pltpu.VMEM)
SMEM = pl.BlockSpec(memory_space=pltpu.SMEM)


def tile(ref, row, group, col):
    return ref[row, pl.ds(group * SUBLANES, SUBLANES), pl.ds(col * LANES, LANES)]


def shifted(tiles, lane, shift):
    if shift == 0:
        return tiles
    zero = jnp.zeros_like(tiles[0])
    rolled = [pltpu.roll(t, (-shift) % LANES, 1) for t in tiles]
    if shift > 0:
        ahead = rolled[1:] + [zero]
        return [jnp.where(lane < LANES - shift, a, b) for a, b in zip(rolled, ahead)]
    behind = [zero] + rolled[:-1]
    return [jnp.where(lane >= -shift, a, b) for a, b in zip(rolled, behind)]


def blur_row(source, row, group, wx, wy, taps, reverse, lane, cols):
    radius = taps // 2
    planes = pl.ds(group * SUBLANES, SUBLANES)
    sums = None
    for tap in range(taps):
        at = row + (2 * radius - tap if reverse else tap)
        weight = wx[tap, planes, :]
        terms = [weight * tile(source, at, group, col) for col in range(cols)]
        sums = terms if sums is None else [a + b for a, b in zip(sums, terms)]
    result = None
    for tap in range(taps):
        weight = wy[tap, planes, :]
        moved = shifted(sums, lane, radius - tap if reverse else tap - radius)
        terms = [weight * m for m in moved]
        result = terms if result is None else [a + b for a, b in zip(result, terms)]
    return result


def pack_body(spot, lists, blocks, out):
    chips, cores, views, slots, _, width = out.shape
    bricks = chips * cores
    here = spot[0]

    def one_chip(chip, carry):
        for slot in range(slots):
            at = ((cores * chip + cores - 1) * bricks + here) * slots + slot
            block = jnp.maximum(lists[at], 0)
            for core in range(cores):
                for view in range(views):
                    begin = (view * cores + core) * width
                    out[chip, core, view, slot] = blocks[block, :, begin : begin + width]
        return carry

    lax.fori_loop(0, chips, one_chip, 0)


def blur_body(layout, spot, table, top, low, high, bottom, blurred, wx, wy, field):
    views, part, cores, taps, kernels = (
        layout["views"], layout["part"], layout["cores"], layout["taps"], layout["kernels"])
    where = spot[1] * cores + spot[2]
    for view in range(views):
        base = view * layout["table"]

        def one_plane(plane, carry):
            pick = table[base + layout["index_at"] + where * part + plane].astype(jnp.int32)
            for axis, target in enumerate((wx, wy)):
                begin = base + layout["bank_at"] + (axis * kernels + pick) * taps
                for tap in range(taps):
                    target[tap, pl.ds(view * part + plane, 1), :] = jnp.full(
                        (1, LANES), table[begin + tap], jnp.float32)
            return carry

        lax.fori_loop(0, part, one_plane, 0)
        planes = slice(view * part, (view + 1) * part)
        at = 0
        for piece in (top, low, high, bottom):
            rows = piece.shape[0]
            field[at : at + rows, planes, :] = piece[...]
            at += rows
    rows_out, planes, columns = blurred.shape
    lane = lax.broadcasted_iota(jnp.int32, (SUBLANES, LANES), 1)

    def one_row(row, carry):
        for group in range(planes // SUBLANES):
            tiles = blur_row(field, row, group, wx, wy, taps, False, lane, columns // LANES)
            for col, value in enumerate(tiles):
                blurred[row, pl.ds(group * SUBLANES, SUBLANES), pl.ds(col * LANES, LANES)] = value
        return carry

    lax.fori_loop(0, rows_out, one_row, 0)


def ratio_body(layout, spot, table, arrived, blurred, ratio, placed, turned):
    views, cores, slots = layout["views"], layout["cores"], layout["slots"]
    bricks, per_holder, rows_dev = layout["bricks"], layout["per_holder"], layout["rows_dev"]
    rows_out, planes, columns = ratio.shape
    per_tile = LANES // layout["block_width"]
    depth_tiles = layout["part"] // per_tile
    groups = views * depth_tiles
    pitch = layout["pitch"]
    chip = lax.div(spot[0], cores)
    first_row = chip * cores * rows_dev
    placed[...] = jnp.zeros_like(placed)

    def one_source(source, carry):
        adds = []
        for view in range(views):
            base = view * layout["table"]
            for slot in range(slots):
                at = ((cores * chip + cores - 1) * bricks + source) * slots + slot
                listed = table[base + at].astype(jnp.int32)
                named = listed >= 0
                block = jnp.maximum(listed, 0)
                start = table[base + layout["offset_at"] + source * per_holder + block]
                start = jnp.where(named, start.astype(jnp.int32) - first_row, 0)
                target = jnp.where(named, block, per_holder)
                values = arrived[source * views + view, slot].astype(jnp.float32)
                for z_tile in range(depth_tiles):
                    begin = (target * groups + view * depth_tiles + z_tile) * pitch + start
                    adds.append((begin, values[:, z_tile * LANES : (z_tile + 1) * LANES]))
        held = [placed[pl.ds(begin, rows_dev), :] for begin, _ in adds]
        for (begin, value), old in zip(adds, held):
            placed[pl.ds(begin, rows_dev), :] = old + value
        return carry

    lax.fori_loop(0, bricks, one_source, 0)

    lane = lax.broadcasted_iota(jnp.int32, (groups, LANES), 1)
    own_rows = cores * rows_dev
    keep_spill = (chip < bricks // cores - 1).astype(jnp.float32)

    def one_row(row, carry):
        for col in range(columns // LANES):
            tiles = [
                placed[pl.ds((col * per_tile + k) * groups * pitch + row, groups, stride=pitch), :]
                for k in range(per_tile)
            ]
            step = per_tile // 2
            while step:
                width = step * layout["block_width"]
                first_half = (lane // width) % 2 == 0
                mixed = list(tiles)
                for k in range(per_tile):
                    if (k // step) % 2 == 0:
                        a, b = tiles[k], tiles[k + step]
                        mixed[k] = jnp.where(first_half, a, pltpu.roll(b, width, 1))
                        mixed[k + step] = jnp.where(first_half, pltpu.roll(a, LANES - width, 1), b)
                tiles = mixed
                step //= 2
            for k, value in enumerate(tiles):
                turned[pl.ds(col * planes + k, groups, stride=per_tile), :] = value
        scale = jnp.where(row < own_rows, 1.0, keep_spill)
        for col in range(columns // LANES):
            for group in range(planes // SUBLANES):
                measured = turned[pl.ds(col * planes + group * SUBLANES, SUBLANES), :]
                ratio[row, pl.ds(group * SUBLANES, SUBLANES), pl.ds(col * LANES, LANES)] = (
                    measured * scale / tile(blurred, row, group, col))
        return carry

    lax.fori_loop(0, rows_out, one_row, 0)


def correct_body(layout, spot, ratio, before, after, wx, wy, low, high, keep, send, field, done):
    views, part, cores, taps = layout["views"], layout["part"], layout["cores"], layout["taps"]
    rows_all, planes, columns = ratio.shape
    spill = after.shape[0]
    own_rows = rows_all - spill
    rows_dev = own_rows // cores
    field[0:spill] = before[0:spill]
    field[spill : 2 * spill] = ratio[0:spill] + before[spill : 2 * spill]
    field[2 * spill : spill + own_rows] = ratio[spill:own_rows]
    field[spill + own_rows :] = ratio[own_rows:] + after[...]
    lane = lax.broadcasted_iota(jnp.int32, (SUBLANES, LANES), 1)

    def one_row(row, carry):
        for group in range(planes // SUBLANES):
            tiles = blur_row(field, row, group, wx, wy, taps, True, lane, columns // LANES)
            for col, value in enumerate(tiles):
                done[row, pl.ds(group * SUBLANES, SUBLANES), pl.ds(col * LANES, LANES)] = value
        return carry

    lax.fori_loop(0, own_rows, one_row, 0)
    core = spot[2]

    def finish(half, source, target):
        rows = pl.ds(half * rows_dev, rows_dev)
        product = done[rows, 0:part, :]
        for view in range(1, views):
            product = product * done[rows, view * part : (view + 1) * part, :]
        target[...] = source * product

    mine = jnp.where(core == 0, low[...], high[...])
    theirs = jnp.where(core == 0, high[...], low[...])
    finish(core, mine, keep)
    finish(1 - core, theirs, send)


def join_body(spot, keep, near, far, far_near, out):
    view, core = spot[1], spot[2]
    part = keep.shape[1]
    for v, c, piece in (
        (view, core, keep), (view, 1 - core, near), (1 - view, core, far), (1 - view, 1 - core, far_near)):
        out[:, pl.ds(pl.multiple_of((v * 2 + c) * part, part), part), :] = piece[...]


def shards(estimate, camera_blocks, block_lists, block_offsets, psf_index, psf_bank):
    rows_dev, depth, columns = estimate.shape
    _, per_holder, block_rows, block_lanes = camera_blocks.shape
    bricks, slots = block_lists.shape[1], block_lists.shape[3]
    views = lax.axis_size("view")
    kernels, taps = psf_bank.shape[2:]
    radius = taps // 2
    cores = 2
    chips = bricks // cores
    part = depth // (cores * views)
    planes = views * part
    block_width = block_lanes // depth
    brick = lax.axis_index("brick")
    view = lax.axis_index("view")
    core = lax.rem(brick, cores)
    spot = jnp.stack([brick, view, core]).astype(jnp.int32)
    f32 = jnp.float32

    lists = block_lists[0].reshape(-1)
    packed = pl.pallas_call(
        pack_body,
        out_shape=jax.ShapeDtypeStruct(
            (chips, cores, views, slots, block_rows, part * block_width), camera_blocks.dtype),
        in_specs=[SMEM, SMEM, VMEM],
        out_specs=VMEM,
        name="pack",
    )(spot, lists, camera_blocks[0])
    packed = packed.reshape(bricks * views, slots, block_rows, part * block_width)
    arrived = lax.all_to_all(packed, ("brick", "view"), 0, 0, tiled=True)

    pieces = [lists, block_offsets[0], psf_index[0], psf_bank[0].reshape(-1)]
    starts = [0]
    for piece in pieces:
        starts.append(starts[-1] + piece.shape[0])
    length = -(-starts[-1] // LANES) * LANES
    table = jnp.concatenate(
        [piece.astype(f32) for piece in pieces] + [jnp.zeros((length - starts[-1],), f32)])
    if views == 2:
        other = lax.ppermute(table, "view", [(0, 1), (1, 0)])
        table = jnp.concatenate(
            [jnp.where(view == 0, table, other), jnp.where(view == 0, other, table)])
    else:
        table = lax.all_gather(table, "view", tiled=True)
    layout = dict(
        views=views, part=part, cores=cores, taps=taps, kernels=kernels, slots=slots, bricks=bricks,
        per_holder=per_holder, rows_dev=rows_dev, block_width=block_width, table=length,
        offset_at=starts[1], index_at=starts[2], bank_at=starts[3],
        pitch=cores * rows_dev + 2 * radius)

    parts = estimate.reshape(rows_dev, views, cores, part, columns)
    mine = parts[:, view, core]
    theirs = parts[:, view, 1 - core]
    swap = [(i, i ^ 1) for i in range(bricks)]
    up = [(i, i + cores) for i in range(bricks - cores)]
    down = [(i + cores, i) for i in range(bricks - cores)]
    partner = lax.ppermute(theirs, "brick", swap)
    low = jnp.where(core == 0, mine, partner)
    high = jnp.where(core == 0, partner, mine)
    top = lax.ppermute(high[rows_dev - radius :], "brick", up)
    bottom = lax.ppermute(low[: 2 * radius], "brick", down)

    own_rows = cores * rows_dev
    rows_all = own_rows + radius
    blurred, wx, wy = pl.pallas_call(
        functools.partial(blur_body, layout),
        out_shape=[
            jax.ShapeDtypeStruct((rows_all, planes, columns), f32),
            jax.ShapeDtypeStruct((taps, planes, LANES), f32),
            jax.ShapeDtypeStruct((taps, planes, LANES), f32),
        ],
        in_specs=[SMEM, SMEM] + [VMEM] * 4,
        out_specs=[VMEM] * 3,
        scratch_shapes=[pltpu.VMEM((rows_all + 2 * radius, planes, columns), f32)],
        name="blur",
    )(spot, table, top, low, high, bottom)

    groups = planes * block_width // LANES
    ratio = pl.pallas_call(
        functools.partial(ratio_body, layout),
        out_shape=jax.ShapeDtypeStruct((rows_all, planes, columns), f32),
        in_specs=[SMEM, SMEM, VMEM, VMEM],
        out_specs=VMEM,
        scratch_shapes=[
            pltpu.VMEM(((per_holder + 1) * groups * layout["pitch"], LANES), f32),
            pltpu.VMEM((columns // LANES * planes, LANES), f32),
        ],
        name="ratio",
    )(spot, table, arrived, blurred)

    before = lax.ppermute(ratio[own_rows - radius :], "brick", up)
    after = lax.ppermute(ratio[:radius], "brick", down)
    piece = jax.ShapeDtypeStruct((rows_dev, part, columns), f32)
    keep, send = pl.pallas_call(
        functools.partial(correct_body, layout),
        out_shape=[piece, piece],
        in_specs=[SMEM] + [VMEM] * 7,
        out_specs=[VMEM] * 2,
        scratch_shapes=[
            pltpu.VMEM((own_rows + 2 * radius, planes, columns), f32),
            pltpu.VMEM((own_rows, planes, columns), f32),
        ],
        name="correct",
    )(spot, ratio, before, after, wx, wy, low, high)

    if views == 2:
        turn = [(0, 1), (1, 0)]
        far = lax.ppermute(keep, "view", turn)
        near = lax.ppermute(send, "brick", swap)
        far_near = lax.ppermute(near, "view", turn)
        return pl.pallas_call(
            join_body,
            out_shape=jax.ShapeDtypeStruct(estimate.shape, f32),
            in_specs=[SMEM] + [VMEM] * 4,
            out_specs=VMEM,
            name="join",
        )(spot, keep, near, far, far_near)
    near = lax.ppermute(send, "brick", swap)
    both = jnp.stack([jnp.where(core == 0, keep, near), jnp.where(core == 0, near, keep)], axis=1)
    everything = lax.all_gather(both, "view")
    return everything.transpose(1, 0, 2, 3, 4).reshape(estimate.shape)


def solution(mesh):
    placed = (
        P("brick", None, None),
        P("view", "brick", None, None),
        P("view", None, None, None),
        P("view", None),
        P("view", None),
        P("view", None, None, None),
    )
    return jax.shard_map(
        shards, mesh=mesh, in_specs=placed, out_specs=P("brick", None, None), check_vma=False
    )
```

time: 154 us -> 94 us (0.61); the launches traced: 151 us -> 93.5 us
  local copies, waits for them, and re-layouts: 36.4 us -> 7.16 us
  Pallas kernels: 0 us -> 24.6 us
  other arithmetic: 24.8 us -> 1.29 us
  waiting for transfers between devices: 55.9 us -> 38.5 us
  between operations: 13.7 us -> 0.2 us
  starting transfers between devices: 19.4 us -> 21.7 us
    all_gather x1 -> x0, waiting for transfers between devices: 38 us -> none  [joined(): pieces = lax.all_gather(value, axis)]
    pallas_call x0 -> x5, Pallas kernels: none -> 24.6 us  [the longest x1 7.47 us: shards(): pl.pallas_call(functools.partial(blur_body, layout), out_shape=[jax.Shape...]
    ppermute x4 -> x9, waiting for transfers between devices: 17.9 us -> 38.5 us  [the longest x1 14.2 us: shards(): after = lax.ppermute(ratio[:radius], 'brick', down)]
    add x3 -> x0, other arithmetic: 13.6 us -> none  [the longest x2 11.3 us: blur_cols(): result = term if result is None else result + term]
    dot_general x2 -> x0, local copies, waits for them, and re-layouts: 9.61 us -> none  [place_blocks(): jnp.einsum('sabc,saf->bcf', weight, blocks, preferred_element_type=jnp.fl...]
    ppermute x4 -> x0, local copies, waits for them, and re-layouts: 8.4 us -> none  [the longest x2 4.74 us: with_halo(): lax.ppermute(tail, axis, [(i, (i + 1) % count) for i in range(ends)])]
    slice x5 -> x3, local copies, waits for them, and re-layouts: 6.44 us -> 2.06 us  [the longest x1 1.08 us: shards(): before = lax.ppermute(ratio[own_rows - radius:], 'brick', up)]
    mul x3 -> x0, other arithmetic: 4.02 us -> none  [the longest x1 2.86 us: shards(): return estimate * product]
  transfers between devices with their start and end apart: 6 -> 10, of which waited for: 4 -> 6; matrix products, arithmetic and copies ran while one was open for 15% -> 2% of each run, Pallas kernels for 0% -> 8%
where the time goes in v1:
time: 94 us; the launch traced here: 93.5 us
  waiting for transfers between devices  38.5 us (41%)
  Pallas kernels  24.6 us (26%)
  starting transfers between devices  21.7 us (23%)
  local copies, waits for them, and re-layouts  7.16 us (8%)
  other arithmetic  1.29 us (1%)
    ppermute x1, waiting for transfers between devices, shards(): after = lax.ppermute(ratio[:radius], 'brick', down)  14.2 us
    pallas_call x1, Pallas kernels, shards(): pl.pallas_call(functools.partial(blur_body, layout), out_shape=[jax.Shape...  7.47 us
    ppermute x1, waiting for transfers between devices, shards(): far = lax.ppermute(keep, 'view', turn)  7.35 us
    pallas_call x1, Pallas kernels, shards(): pl.pallas_call(functools.partial(ratio_body, layout), out_shape=jax.Shape...  6.71 us
    pallas_call x1, Pallas kernels, shards(): pl.pallas_call(functools.partial(correct_body, layout), out_shape=[piece,...  6.22 us
    all_to_all x1, starting transfers between devices, shards(): arrived = lax.all_to_all(packed, ('brick', 'view'), 0, 0, tiled=True)  6.04 us
    ppermute x1, waiting for transfers between devices, shards(): far_near = lax.ppermute(near, 'view', turn)  5.14 us
    ppermute x1, waiting for transfers between devices, shards(): bottom = lax.ppermute(low[:2 * radius], 'brick', down)  5.13 us
  transfers between devices with their start and end apart: 10, of which 6 were waited for; matrix products, arithmetic and copies ran while one was open for 2% of the time, Pallas kernels for 8%

profile of v1, /device:TPU:8, one launch (start us, length us, event | category | flops | bytes accessed | tf_op | source)
XLA Modules:
  0.0 93.5 jit_solution(9273328679180531872)
XLA Ops:
  0.0 0.0 copy-start.9
  0.0 1.0 %copy.9 = s32[1,16,16,2]{3,2,1,0:T(8,128)S(1)} copy(s32[1,16,16,2]{2,3,1,0:T(2,128)} %param.8) | data formatting | bytes 4096 | tf_op args[2]
  1.0 0.7 reshape_squeeze.6.lists
  1.7 0.6 pad_add_fusion.spot
  2.3 0.0 copy-start.11
  2.3 0.0 copy-start.13
  2.3 0.0 copy-start.12
  2.3 0.0 copy-start.14
  2.3 2.0 %pack.1 = bf16[8,2,2,2,8,512]{5,4,3,2,1,0:T(8,128)(2,1)} custom-call(s32[3]{0:T(128)} %pad_add_fusion.spot, s32[512]{0:T(512)} %reshape_squeeze.6.lists, bf16[16,8,2048]{2,1,0:T(8,128)(2,1)} %bitcast.23), custom_call_target="tpu_custom_call" | custom-call | tf_op jit(solution)/shard_map/pack/pallas_call | solution.py:236
  4.3 6.0 %all-to-all-start = ((bf16[32,2,8,512]{3,2,1,0:T(8,128)(2,1)}), bf16[32,2,8,512]{3,2,1,0:T(8,128)(2,1)S(1)}, u32[]{:S(2)}, u32[]{:S(2)}) async-start(bf16[32,2,8,512]{3,2,1,0:T(8,128)(2,1)} %bitcast.22), calls=%async_computation | async-start | bytes 1048576 | tf_op jit(solution)/shard_map/all_to_all | solution.py:245
  10.4 0.0 copy-done.9
  10.4 0.2 collective-permute-start.1
  10.6 0.0 copy-done.11
  10.6 0.0 copy-done.13
  10.6 0.0 copy-done.12
  10.6 0.1 copy.10
  10.7 0.1 reshape_squeeze.7
  10.8 0.0 copy-done.14
  10.9 0.1 concatenate.6
  10.9 1.5 %collective-permute-start = (f32[1152]{0:T(1024)S(1)}, f32[1152]{0:T(1024)S(1)}, u32[]{:S(2)}, u32[]{:S(2)}) collective-permute-start(f32[1152]{0:T(1024)S(1)} %concatenate.6), channel_id=1, source_target_pairs={{0,1},{1,0},{2,3},{3,2},{4,5},{5,4},{6,7},{7,6},{8,9},{9,8},{10,11... | collective-permute-start | bytes 13832 | tf_op jit(solution)/shard_map/ppermute | solution.py:255
  12.4 0.0 collective-permute-done.1
  12.4 0.1 bitcast_select_fusion
  12.5 0.0 copy-start
  12.5 0.0 copy-start.1
  12.5 3.4 %collective-permute-start.2 = (f32[4,16,512]{2,1,0:T(8,128)S(1)}, f32[4,16,512]{2,1,0:T(8,128)S(1)}, u32[]{:S(2)}, u32[]{:S(2)}) collective-permute-start(f32[4,16,512]{2,1,0:T(8,128)S(1)} %slice.12), channel_id=1, source_target_pairs={{0,4},{2,6},{4,8},{6,10},{8,12},{10,14},{12,16},{14,18},{16,20},{1... | collective-permute-start | bytes 393224 | tf_op jit(solution)/shard_map/ppermute | solution.py:275
  15.9 3.4 %collective-permute-start.3 = (f32[8,16,512]{2,1,0:T(8,128)S(1)}, f32[8,16,512]{2,1,0:T(8,128)S(1)}, u32[]{:S(2)}, u32[]{:S(2)}) collective-permute-start(f32[8,16,512]{2,1,0:T(8,128)S(1)} %get-tuple-element.15.low), channel_id=1, source_target_pairs={{4,0},{6,2},{8,4},{10,6},{12,8},{14,10},{16,12},{18,14},{20,16},{2... | collective-permute-start | bytes 786440 | tf_op jit(solution)/shard_map/ppermute | solution.py:276
  19.3 0.0 collective-permute-done
  19.3 0.6 pad_maximum_fusion.table
  19.9 5.1 %collective-permute-done.2.top = f32[4,16,512]{2,1,0:T(8,128)S(1)} collective-permute-done((f32[4,16,512]{2,1,0:T(8,128)S(1)}, f32[4,16,512]{2,1,0:T(8,128)S(1)}, u32[]{:S(2)}, u32[]{:S(2)}) %collective-permute-start.2) | collective-permute-done | bytes 131104 | tf_op jit(solution)/shard_map/ppermute | solution.py:275
  25.0 0.0 copy-start.10
  25.0 5.1 %collective-permute-done.3.bottom = f32[8,16,512]{2,1,0:T(8,128)S(1)} collective-permute-done((f32[8,16,512]{2,1,0:T(8,128)S(1)}, f32[8,16,512]{2,1,0:T(8,128)S(1)}, u32[]{:S(2)}, u32[]{:S(2)}) %collective-permute-start.3) | collective-permute-done | bytes 262176 | tf_op jit(solution)/shard_map/ppermute | solution.py:276
  30.1 0.0 copy-done
  30.1 0.0 copy-done.1
  30.1 0.0 copy-done.10
  30.1 0.0 copy-start.4
  30.2 0.7 copy-done.4
  30.8 7.5 %blur.1 = (f32[20,32,512]{2,1,0:T(8,128)}, f32[9,32,128]{2,1,0:T(8,128)}, f32[9,32,128]{2,1,0:T(8,128)}) custom-call(s32[3]{0:T(128)} %pad_add_fusion.spot, f32[2304]{0:T(1024)} %pad_maximum_fusion.table, f32[4,16,512]{2,1,0:T(8,128)} %copy-done.10, f32[8,16,512]{2,1,0:T(8,128)} %copy-done.1, f32[8,16,512]{2,1,0:T(8,128)} %copy-done, f32[8,16,512]{2,1,0:T(8,128)} %copy-done.4), custom_call_target="tpu_custom_call" | custom-call | tf_op jit(solution)/shard_map/blur/pallas_call | solution.py:280
  38.3 0.0 all-to-all-done.arrived
  38.3 0.0 copy-start.2
  38.3 0.8 copy-done.2
  39.1 6.7 %ratio.1 = f32[20,32,512]{2,1,0:T(8,128)} custom-call(s32[3]{0:T(128)} %pad_add_fusion.spot, f32[2304]{0:T(1024)} %pad_maximum_fusion.table, bf16[32,2,8,512]{3,2,1,0:T(8,128)(2,1)} %copy-done.2, f32[20,32,512]{2,1,0:T(8,128)} %get-tuple-element.10.blurred), custom_call_target="tpu_custom_call" | custom-call | tf_op jit(solution)/shard_map/ratio/pallas_call | solution.py:294
  45.8 1.1 %slice.13 = f32[8,32,512]{2,1,0:T(8,128)S(1)} slice(f32[20,32,512]{2,1,0:T(8,128)} %ratio.1), slice={[12:20], [0:32], [0:512]} | slice | bytes 1048576 | tf_op jit(solution)/shard_map/slice | solution.py:306
  46.9 3.0 %collective-permute-start.4 = (f32[8,32,512]{2,1,0:T(8,128)S(1)}, f32[8,32,512]{2,1,0:T(8,128)S(1)}, u32[]{:S(2)}, u32[]{:S(2)}) collective-permute-start(f32[8,32,512]{2,1,0:T(8,128)S(1)} %slice.13), channel_id=1, source_target_pairs={{0,4},{2,6},{4,8},{6,10},{8,12},{10,14},{12,16},{14,18},{16,20},{1... | collective-permute-start | bytes 1572872 | tf_op jit(solution)/shard_map/ppermute | solution.py:306
  49.9 1.0 %slice.14 = f32[4,32,512]{2,1,0:T(8,128)S(1)} slice(f32[20,32,512]{2,1,0:T(8,128)} %ratio.1), slice={[0:4], [0:32], [0:512]} | slice | bytes 524288 | tf_op jit(solution)/shard_map/slice | solution.py:307
  50.9 3.8 %collective-permute-start.5 = (f32[4,32,512]{2,1,0:T(8,128)S(1)}, f32[4,32,512]{2,1,0:T(8,128)S(1)}, u32[]{:S(2)}, u32[]{:S(2)}) collective-permute-start(f32[4,32,512]{2,1,0:T(8,128)S(1)} %slice.14), channel_id=1, source_target_pairs={{4,0},{6,2},{8,4},{10,6},{12,8},{14,10},{16,12},{18,14},{20,16},{2... | collective-permute-start | bytes 786440 | tf_op jit(solution)/shard_map/ppermute | solution.py:307
  54.6 14.2 %collective-permute-done.5.after = f32[4,32,512]{2,1,0:T(8,128)S(1)} collective-permute-done((f32[4,32,512]{2,1,0:T(8,128)S(1)}, f32[4,32,512]{2,1,0:T(8,128)S(1)}, u32[]{:S(2)}, u32[]{:S(2)}) %collective-permute-start.5) | collective-permute-done | bytes 262176 | tf_op jit(solution)/shard_map/ppermute | solution.py:307
  68.9 0.0 copy-start.6
  68.9 0.0 collective-permute-done.4.before
  68.9 0.7 copy-done.6
  69.6 0.2 copy-done.3
  69.8 6.2 %correct.1 = (f32[8,16,512]{2,1,0:T(8,128)}, f32[8,16,512]{2,1,0:T(8,128)}) custom-call(s32[3]{0:T(128)} %pad_add_fusion.spot, f32[20,32,512]{2,1,0:T(8,128)} %ratio.1, f32[8,32,512]{2,1,0:T(8,128)} %copy-done.3, f32[4,32,512]{2,1,0:T(8,128)} %copy-done.6, f32[9,32,128]{2,1,0:T(8,128)} %get-tuple-element.11.wx, f32[9,32,128]{2,1,0:T(8,128)} %get-tuple-element.12.wy, ...), custom_call_target="tpu_custom_call" | custom-call | tf_op jit(solution)/shard_map/correct/pallas_call | solution.py:309
  76.0 0.0 collective-permute-start.6
  76.0 0.2 collective-permute-start.7
  76.2 1.5 %collective-permute-done.6.near = f32[8,16,512]{2,1,0:T(8,128)S(1)} collective-permute-done((f32[8,16,512]{2,1,0:T(8,128)}, f32[8,16,512]{2,1,0:T(8,128)S(1)}, u32[]{:S(2)}, u32[]{:S(2)}) %collective-permute-start.6) | collective-permute-done | bytes 262176 | tf_op jit(solution)/shard_map/ppermute | solution.py:324
  77.7 0.0 copy-start.5
  77.7 0.3 collective-permute-start.8
  78.0 7.4 %collective-permute-done.7.far = f32[8,16,512]{2,1,0:T(8,128)S(1)} collective-permute-done((f32[8,16,512]{2,1,0:T(8,128)}, f32[8,16,512]{2,1,0:T(8,128)S(1)}, u32[]{:S(2)}, u32[]{:S(2)}) %collective-permute-start.7) | collective-permute-done | bytes 262176 | tf_op jit(solution)/shard_map/ppermute | solution.py:323
  85.4 0.0 copy-start.7
  85.4 5.1 %collective-permute-done.8.far_near = f32[8,16,512]{2,1,0:T(8,128)S(1)} collective-permute-done((f32[8,16,512]{2,1,0:T(8,128)S(1)}, f32[8,16,512]{2,1,0:T(8,128)S(1)}, u32[]{:S(2)}, u32[]{:S(2)}) %collective-permute-start.8) | collective-permute-done | bytes 262176 | tf_op jit(solution)/shard_map/ppermute | solution.py:325
  90.5 0.0 copy-done.5
  90.5 0.0 copy-done.7
  90.5 0.0 copy-start.8
  90.5 0.7 copy-done.8
  91.2 2.2 %join.1 = f32[8,64,512]{2,1,0:T(8,128)} custom-call(s32[3]{0:T(128)} %pad_add_fusion.spot, f32[8,16,512]{2,1,0:T(8,128)} %get-tuple-element.13.keep, f32[8,16,512]{2,1,0:T(8,128)} %copy-done.5, f32[8,16,512]{2,1,0:T(8,128)} %copy-done.7, f32[8,16,512]{2,1,0:T(8,128)} %copy-done.8), custom_call_target="tpu_custom_call" | custom-call | tf_op jit(solution)/shard_map/join/pallas_call | solution.py:326
  (8 shorter events, 0.1 us)
Async XLA Ops:
  0.0 10.4 %copy-start.9 = (f32[8,64,512]{2,1,0:T(8,128)S(1)}, f32[8,64,512]{2,1,0:T(8,128)}, u32[]{:S(2)}) copy-start(f32[8,64,512]{2,1,0:T(8,128)} %param.6) | copy-start | bytes 3145732
  2.3 8.3 %copy-start.11 = (s32[512]{0:T(512)S(1)}, s32[512]{0:T(512)}, u32[]{:S(2)}) copy-start(s32[512]{0:T(512)} %reshape_squeeze.6.lists) | copy-start | bytes 6148
  2.3 8.3 %copy-start.13 = (s32[1,256]{1,0:T(1,128)S(1)}, s32[1,256]{1,0:T(1,128)}, u32[]{:S(2)}) copy-start(s32[1,256]{1,0:T(1,128)} %param.9) | copy-start | bytes 3076
  2.3 8.3 %copy-start.12 = (f32[1,2,16,9]{2,1,3,0:T(2,128)S(1)}, f32[1,2,16,9]{2,1,3,0:T(2,128)}, u32[]{:S(2)}) copy-start(f32[1,2,16,9]{2,1,3,0:T(2,128)} %param.11) | copy-start | bytes 3460
  2.3 8.5 %copy-start.14 = (s32[1,64]{1,0:T(1,128)S(1)}, s32[1,64]{1,0:T(1,128)}, u32[]{:S(2)}) copy-start(s32[1,64]{1,0:T(1,128)} %param.10) | copy-start | bytes 772
  4.3 34.0 %all-to-all-start = ((bf16[32,2,8,512]{3,2,1,0:T(8,128)(2,1)}), bf16[32,2,8,512]{3,2,1,0:T(8,128)(2,1)S(1)}, u32[]{:S(2)}, u32[]{:S(2)}) async-start(bf16[32,2,8,512]{3,2,1,0:T(8,128)(2,1)} %bitcast.22), calls=%async_computation | async-start | bytes 1048576 | tf_op jit(solution)/shard_map/all_to_all | solution.py:245
  10.4 2.0 %collective-permute-start.1 = (f32[8,16,512]{2,1,0:T(8,128)S(1)}, f32[8,16,512]{2,1,0:T(8,128)S(1)}, u32[]{:S(2)}, u32[]{:S(2)}) collective-permute-start(f32[8,16,512]{2,1,0:T(8,128)S(1)} %dynamic-slice_bitcast_fusion), channel_id=1, source_target_pairs={{0,2},{2,0},{4,6},{6,4},{8,10},{10,8},{12,14},{14,12},{16,18},{18,... | collective-permute-start | bytes 786440 | tf_op jit(solution)/shard_map/ppermute | solution.py:272
  10.9 8.3 %collective-permute-start = (f32[1152]{0:T(1024)S(1)}, f32[1152]{0:T(1024)S(1)}, u32[]{:S(2)}, u32[]{:S(2)}) collective-permute-start(f32[1152]{0:T(1024)S(1)} %concatenate.6), channel_id=1, source_target_pairs={{0,1},{1,0},{2,3},{3,2},{4,5},{5,4},{6,7},{7,6},{8,9},{9,8},{10,11... | collective-permute-start | bytes 13832 | tf_op jit(solution)/shard_map/ppermute | solution.py:255
  12.5 17.7 %copy-start = (f32[8,16,512]{2,1,0:T(8,128)}, f32[8,16,512]{2,1,0:T(8,128)S(1)}, u32[]{:S(2)}) copy-start(f32[8,16,512]{2,1,0:T(8,128)S(1)} %get-tuple-element.16.high) | copy-start | bytes 786436
  12.5 17.7 %copy-start.1 = (f32[8,16,512]{2,1,0:T(8,128)}, f32[8,16,512]{2,1,0:T(8,128)S(1)}, u32[]{:S(2)}) copy-start(f32[8,16,512]{2,1,0:T(8,128)S(1)} %get-tuple-element.15.low) | copy-start | bytes 786436
  12.5 12.5 %collective-permute-start.2 = (f32[4,16,512]{2,1,0:T(8,128)S(1)}, f32[4,16,512]{2,1,0:T(8,128)S(1)}, u32[]{:S(2)}, u32[]{:S(2)}) collective-permute-start(f32[4,16,512]{2,1,0:T(8,128)S(1)} %slice.12), channel_id=1, source_target_pairs={{0,4},{2,6},{4,8},{6,10},{8,12},{10,14},{12,16},{14,18},{16,20},{1... | collective-permute-start | bytes 393224 | tf_op jit(solution)/shard_map/ppermute | solution.py:275
  15.9 14.2 %collective-permute-start.3 = (f32[8,16,512]{2,1,0:T(8,128)S(1)}, f32[8,16,512]{2,1,0:T(8,128)S(1)}, u32[]{:S(2)}, u32[]{:S(2)}) collective-permute-start(f32[8,16,512]{2,1,0:T(8,128)S(1)} %get-tuple-element.15.low), channel_id=1, source_target_pairs={{4,0},{6,2},{8,4},{10,6},{12,8},{14,10},{16,12},{18,14},{20,16},{2... | collective-permute-start | bytes 786440 | tf_op jit(solution)/shard_map/ppermute | solution.py:276
  25.0 5.1 %copy-start.10 = (f32[4,16,512]{2,1,0:T(8,128)}, f32[4,16,512]{2,1,0:T(8,128)S(1)}, u32[]{:S(2)}) copy-start(f32[4,16,512]{2,1,0:T(8,128)S(1)} %collective-permute-done.2.top) | copy-start | bytes 393220
  30.1 0.7 copy-start.4
  38.3 0.8 copy-start.2
  46.9 22.0 %collective-permute-start.4 = (f32[8,32,512]{2,1,0:T(8,128)S(1)}, f32[8,32,512]{2,1,0:T(8,128)S(1)}, u32[]{:S(2)}, u32[]{:S(2)}) collective-permute-start(f32[8,32,512]{2,1,0:T(8,128)S(1)} %slice.13), channel_id=1, source_target_pairs={{0,4},{2,6},{4,8},{6,10},{8,12},{10,14},{12,16},{14,18},{16,20},{1... | collective-permute-start | bytes 1572872 | tf_op jit(solution)/shard_map/ppermute | solution.py:306
  50.9 18.0 %collective-permute-start.5 = (f32[4,32,512]{2,1,0:T(8,128)S(1)}, f32[4,32,512]{2,1,0:T(8,128)S(1)}, u32[]{:S(2)}, u32[]{:S(2)}) collective-permute-start(f32[4,32,512]{2,1,0:T(8,128)S(1)} %slice.14), channel_id=1, source_target_pairs={{4,0},{6,2},{8,4},{10,6},{12,8},{14,10},{16,12},{18,14},{20,16},{2... | collective-permute-start | bytes 786440 | tf_op jit(solution)/shard_map/ppermute | solution.py:307
  68.9 0.7 copy-start.6
  68.9 0.9 copy-start.3
  76.0 1.7 %collective-permute-start.6 = (f32[8,16,512]{2,1,0:T(8,128)}, f32[8,16,512]{2,1,0:T(8,128)S(1)}, u32[]{:S(2)}, u32[]{:S(2)}) collective-permute-start(f32[8,16,512]{2,1,0:T(8,128)} %get-tuple-element.14), channel_id=1, source_target_pairs={{0,2},{2,0},{4,6},{6,4},{8,10},{10,8},{12,14},{14,12},{16,18},{18,... | collective-permute-start | bytes 786440 | tf_op jit(solution)/shard_map/ppermute | solution.py:324
  76.0 9.4 %collective-permute-start.7 = (f32[8,16,512]{2,1,0:T(8,128)}, f32[8,16,512]{2,1,0:T(8,128)S(1)}, u32[]{:S(2)}, u32[]{:S(2)}) collective-permute-start(f32[8,16,512]{2,1,0:T(8,128)} %get-tuple-element.13.keep), channel_id=1, source_target_pairs={{0,1},{1,0},{2,3},{3,2},{4,5},{5,4},{6,7},{7,6},{8,9},{9,8},{10,11... | collective-permute-start | bytes 786440 | tf_op jit(solution)/shard_map/ppermute | solution.py:323
  77.7 12.8 %copy-start.5 = (f32[8,16,512]{2,1,0:T(8,128)}, f32[8,16,512]{2,1,0:T(8,128)S(1)}, u32[]{:S(2)}) copy-start(f32[8,16,512]{2,1,0:T(8,128)S(1)} %collective-permute-done.6.near) | copy-start | bytes 786436
  77.7 12.8 %collective-permute-start.8 = (f32[8,16,512]{2,1,0:T(8,128)S(1)}, f32[8,16,512]{2,1,0:T(8,128)S(1)}, u32[]{:S(2)}, u32[]{:S(2)}) collective-permute-start(f32[8,16,512]{2,1,0:T(8,128)S(1)} %collective-permute-done.6.near), channel_id=1, source_target_pairs={{0,1},{1,0},{2,3},{3,2},{4,5},{5,4},{6,7},{7,6},{8,9},{9,8},{10,11... | collective-permute-start | bytes 786440 | tf_op jit(solution)/shard_map/ppermute | solution.py:325
  85.4 5.2 %copy-start.7 = (f32[8,16,512]{2,1,0:T(8,128)}, f32[8,16,512]{2,1,0:T(8,128)S(1)}, u32[]{:S(2)}) copy-start(f32[8,16,512]{2,1,0:T(8,128)S(1)} %collective-permute-done.7.far) | copy-start | bytes 786436
  90.5 0.7 copy-start.8

commit v2 on v1

--- a/solution.py
+++ b/solution.py
@@ -1,4 +1,5 @@
 import functools
+import math
 
 import jax
 import jax.numpy as jnp
@@ -7,9 +8,15 @@
 from jax.experimental.pallas import tpu as pltpu
 from jax.sharding import PartitionSpec as P
 
+CAMERA = (0.099609375, 2.0)
+PSF = (0.03, 0.3)
+ESTIMATE = (0.5, 2.0)
+CODE_TOP = 32767.0
 LANES = 128
 SUBLANES = 8
+GRANT = pltpu.CompilerParams(vmem_limit_bytes=12 << 20)
 VMEM = pl.BlockSpec(memory_space=pltpu.VMEM)
+HBM = pl.BlockSpec(memory_space=pl.ANY)
 SMEM = pl.BlockSpec(memory_space=pltpu.SMEM)
 
 
@@ -47,15 +54,56 @@
     return result
 
 
-def pack_body(spot, lists, blocks, out):
+def near_core(*values):
+    return [pltpu.with_memory_space_constraint(value, pltpu.VMEM) for value in values]
+
+
+def position(cores):
+    brick = lax.axis_index("brick")
+    return lax.div(brick, cores), lax.rem(brick, cores), lax.axis_index("view")
+
+
+def ratio_range(bricks, taps):
+    least = CAMERA[0] / (taps * taps * PSF[1] * PSF[1] * ESTIMATE[1])
+    inside = taps // 2 + 1
+    most = bricks * CAMERA[1] / (inside * inside * PSF[0] * PSF[0] * ESTIMATE[0])
+    low, high = math.log(least) - 0.01, math.log(most) + 0.01
+    return low, (high - low) / (2 * CODE_TOP - 1)
+
+
+def encode_ratio(value, bricks, taps):
+    low, step = ratio_range(bricks, taps)
+    tiny = math.exp(low)
+    code = jnp.round((jnp.log(jnp.maximum(value, tiny)) - low) * (1.0 / step)) + (1.0 - CODE_TOP)
+    code = jnp.where(value > 0, jnp.minimum(code, CODE_TOP), -CODE_TOP)
+    return code.astype(jnp.int32).astype(jnp.int16)
+
+
+def decode_ratio(code, bricks, taps):
+    low, step = ratio_range(bricks, taps)
+    code = code.astype(jnp.int32).astype(jnp.float32)
+    value = jnp.exp((code + (CODE_TOP - 1.0)) * step + low)
+    return jnp.where(code > -CODE_TOP, value, 0.0)
+
+
+def encode_estimate(value):
+    scale = 2 * CODE_TOP / (ESTIMATE[1] - ESTIMATE[0])
+    code = jnp.round((value - ESTIMATE[0]) * scale) - CODE_TOP
+    return jnp.clip(code, -CODE_TOP, CODE_TOP).astype(jnp.int16)
+
+
+def decode_estimate(code):
+    scale = (ESTIMATE[1] - ESTIMATE[0]) / (2 * CODE_TOP)
+    return (code.astype(jnp.int32).astype(jnp.float32) + CODE_TOP) * scale + ESTIMATE[0]
+
+
+def pack_body(lists, blocks, out):
     chips, cores, views, slots, _, width = out.shape
-    bricks = chips * cores
-    here = spot[0]
+    here = lax.axis_index("brick")
 
     def one_chip(chip, carry):
         for slot in range(slots):
-            at = ((cores * chip + cores - 1) * bricks + here) * slots + slot
-            block = jnp.maximum(lists[at], 0)
+            block = jnp.maximum(lists[cores * chip + cores - 1, slot, here], 0)
             for core in range(cores):
                 for view in range(views):
                     begin = (view * cores + core) * width
@@ -65,10 +113,15 @@
     lax.fori_loop(0, chips, one_chip, 0)
 
 
-def blur_body(layout, spot, table, top, low, high, bottom, blurred, wx, wy, field):
+def blur_body(layout, table, top, low, high, bottom, inverse, wx, wy, field):
     views, part, cores, taps, kernels = (
         layout["views"], layout["part"], layout["cores"], layout["taps"], layout["kernels"])
-    where = spot[1] * cores + spot[2]
+    chip, core, view_here = position(cores)
+    where = view_here * cores + core
+    has_top = (chip > 0).astype(jnp.float32)
+    has_bottom = (chip < layout["bricks"] // cores - 1).astype(jnp.float32)
+    rows = (decode_estimate(top[...]) * has_top, low[...], high[...],
+            decode_estimate(bottom[...]) * has_bottom)
     for view in range(views):
         base = view * layout["table"]
 
@@ -84,32 +137,34 @@
         lax.fori_loop(0, part, one_plane, 0)
         planes = slice(view * part, (view + 1) * part)
         at = 0
-        for piece in (top, low, high, bottom):
-            rows = piece.shape[0]
-            field[at : at + rows, planes, :] = piece[...]
-            at += rows
-    rows_out, planes, columns = blurred.shape
+        for piece in rows:
+            field[at : at + piece.shape[0], planes, :] = piece
+            at += piece.shape[0]
+    rows_out, planes, columns = inverse.shape
+    own_rows = cores * layout["rows_dev"]
     lane = lax.broadcasted_iota(jnp.int32, (SUBLANES, LANES), 1)
 
     def one_row(row, carry):
+        wanted = jnp.where(row < own_rows, 1.0, has_bottom)
         for group in range(planes // SUBLANES):
             tiles = blur_row(field, row, group, wx, wy, taps, False, lane, columns // LANES)
             for col, value in enumerate(tiles):
-                blurred[row, pl.ds(group * SUBLANES, SUBLANES), pl.ds(col * LANES, LANES)] = value
-        return carry
-
-    lax.fori_loop(0, rows_out, one_row, 0)
-
-
-def ratio_body(layout, spot, table, arrived, blurred, ratio, placed, turned):
-    views, cores, slots = layout["views"], layout["cores"], layout["slots"]
+                inverse[row, pl.ds(group * SUBLANES, SUBLANES), pl.ds(col * LANES, LANES)] = wanted / value
+        return carry
+
+    lax.fori_loop(0, rows_out, one_row, 0, unroll=2)
+
+
+def ratio_body(layout, table, arrived, inverse, field, upward, downward, placed, turned):
+    views, cores, slots, taps = layout["views"], layout["cores"], layout["slots"], layout["taps"]
     bricks, per_holder, rows_dev = layout["bricks"], layout["per_holder"], layout["rows_dev"]
-    rows_out, planes, columns = ratio.shape
+    rows_out, planes, columns = inverse.shape
+    radius = taps // 2
     per_tile = LANES // layout["block_width"]
     depth_tiles = layout["part"] // per_tile
     groups = views * depth_tiles
     pitch = layout["pitch"]
-    chip = lax.div(spot[0], cores)
+    chip, _, _ = position(cores)
     first_row = chip * cores * rows_dev
     placed[...] = jnp.zeros_like(placed)
 
@@ -118,8 +173,7 @@
         for view in range(views):
             base = view * layout["table"]
             for slot in range(slots):
-                at = ((cores * chip + cores - 1) * bricks + source) * slots + slot
-                listed = table[base + at].astype(jnp.int32)
+                listed = table[base + slot * bricks + source].astype(jnp.int32)
                 named = listed >= 0
                 block = jnp.maximum(listed, 0)
                 start = table[base + layout["offset_at"] + source * per_holder + block]
@@ -138,7 +192,6 @@
 
     lane = lax.broadcasted_iota(jnp.int32, (groups, LANES), 1)
     own_rows = cores * rows_dev
-    keep_spill = (chip < bricks // cores - 1).astype(jnp.float32)
 
     def one_row(row, carry):
         for col in range(columns // LANES):
@@ -160,44 +213,93 @@
                 step //= 2
             for k, value in enumerate(tiles):
                 turned[pl.ds(col * planes + k, groups, stride=per_tile), :] = value
-        scale = jnp.where(row < own_rows, 1.0, keep_spill)
         for col in range(columns // LANES):
             for group in range(planes // SUBLANES):
                 measured = turned[pl.ds(col * planes + group * SUBLANES, SUBLANES), :]
-                ratio[row, pl.ds(group * SUBLANES, SUBLANES), pl.ds(col * LANES, LANES)] = (
-                    measured * scale / tile(blurred, row, group, col))
+                planes_at = pl.ds(group * SUBLANES, SUBLANES)
+                field[row + radius, planes_at, pl.ds(col * LANES, LANES)] = (
+                    measured * tile(inverse, row, group, col))
         return carry
 
     lax.fori_loop(0, rows_out, one_row, 0)
-
-
-def correct_body(layout, spot, ratio, before, after, wx, wy, low, high, keep, send, field, done):
-    views, part, cores, taps = layout["views"], layout["part"], layout["cores"], layout["taps"]
-    rows_all, planes, columns = ratio.shape
-    spill = after.shape[0]
-    own_rows = rows_all - spill
-    rows_dev = own_rows // cores
-    field[0:spill] = before[0:spill]
-    field[spill : 2 * spill] = ratio[0:spill] + before[spill : 2 * spill]
-    field[2 * spill : spill + own_rows] = ratio[spill:own_rows]
-    field[spill + own_rows :] = ratio[own_rows:] + after[...]
+    field[0:radius] = jnp.zeros((radius, planes, columns), jnp.float32)
+    for target, begin in ((upward, own_rows), (downward, radius)):
+
+        def one_message_row(row, carry):
+            target[row] = encode_ratio(field[row + begin], bricks, taps)
+            return carry
+
+        lax.fori_loop(0, target.shape[0], one_message_row, 0)
+
+
+def own_body(layout, field, wx, wy, done):
+    rows, planes, columns = done.shape
     lane = lax.broadcasted_iota(jnp.int32, (SUBLANES, LANES), 1)
 
     def one_row(row, carry):
         for group in range(planes // SUBLANES):
-            tiles = blur_row(field, row, group, wx, wy, taps, True, lane, columns // LANES)
+            tiles = blur_row(field, row, group, wx, wy, layout["taps"], True, lane, columns // LANES)
             for col, value in enumerate(tiles):
                 done[row, pl.ds(group * SUBLANES, SUBLANES), pl.ds(col * LANES, LANES)] = value
         return carry
 
-    lax.fori_loop(0, own_rows, one_row, 0)
-    core = spot[2]
+    lax.fori_loop(0, rows, one_row, 0, unroll=2)
+
+
+def rest_body(layout, done, before, after, wx, wy, low, high, keep, send, ahead, behind, total):
+    views, part, cores, taps = layout["views"], layout["part"], layout["cores"], layout["taps"]
+    bricks = layout["bricks"]
+    own_rows, planes, columns = done.shape
+    radius = taps // 2
+    rows_dev = own_rows // cores
+    chip, core, _ = position(cores)
+    has_before = (chip > 0).astype(jnp.float32)
+    has_after = (chip < bricks // cores - 1).astype(jnp.float32)
+    for target, source, mask in ((ahead, before, has_before), (behind, after, has_after)):
+
+        def one_message_row(row, carry):
+            target[row] = decode_ratio(source[row], bricks, taps) * mask
+            return carry
+
+        lax.fori_loop(0, source.shape[0], one_message_row, 0)
+    lane = lax.broadcasted_iota(jnp.int32, (SUBLANES, LANES), 1)
+    cols = columns // LANES
+    reached = list(range(2 * radius)) + list(range(own_rows - radius, own_rows))
+
+    def one_group(group, carry):
+        planes_at = pl.ds(pl.multiple_of(group * SUBLANES, SUBLANES), SUBLANES)
+        for row in reached:
+            sums = None
+            for tap in range(taps):
+                at = row + 2 * radius - tap
+                if at < 2 * radius:
+                    source = ahead
+                elif at >= own_rows + radius:
+                    source, at = behind, at - own_rows - radius
+                else:
+                    continue
+                weight = wx[tap, planes_at, :]
+                terms = [weight * source[at, planes_at, pl.ds(col * LANES, LANES)] for col in range(cols)]
+                sums = terms if sums is None else [a + b for a, b in zip(sums, terms)]
+            result = [done[row, planes_at, pl.ds(col * LANES, LANES)] for col in range(cols)]
+            for tap in range(taps):
+                weight = wy[tap, planes_at, :]
+                moved = shifted(sums, lane, radius - tap)
+                result = [a + weight * m for a, m in zip(result, moved)]
+            for col, value in enumerate(result):
+                total[row, planes_at, pl.ds(col * LANES, LANES)] = value
+        for row in range(own_rows):
+            if row not in reached:
+                total[row, planes_at, :] = done[row, planes_at, :]
+        return carry
+
+    lax.fori_loop(0, planes // SUBLANES, one_group, 0)
 
     def finish(half, source, target):
         rows = pl.ds(half * rows_dev, rows_dev)
-        product = done[rows, 0:part, :]
+        product = total[rows, 0:part, :]
         for view in range(1, views):
-            product = product * done[rows, view * part : (view + 1) * part, :]
+            product = product * total[rows, view * part : (view + 1) * part, :]
         target[...] = source * product
 
     mine = jnp.where(core == 0, low[...], high[...])
@@ -206,12 +308,18 @@
     finish(1 - core, theirs, send)
 
 
-def join_body(spot, keep, near, far, far_near, out):
-    view, core = spot[1], spot[2]
+def join_body(keep, near, far, far_near, out, sems):
+    _, core, view = position(2)
     part = keep.shape[1]
-    for v, c, piece in (
-        (view, core, keep), (view, 1 - core, near), (1 - view, core, far), (1 - view, 1 - core, far_near)):
-        out[:, pl.ds(pl.multiple_of((v * 2 + c) * part, part), part), :] = piece[...]
+    copies = []
+    for index, (v, c, piece) in enumerate((
+        (view, core, keep), (view, 1 - core, near), (1 - view, core, far), (1 - view, 1 - core, far_near))):
+        begin = pl.multiple_of((v * 2 + c) * part, part)
+        copies.append(pltpu.make_async_copy(piece, out.at[:, pl.ds(begin, part), :], sems.at[index]))
+    for copy in copies:
+        copy.start()
+    for copy in copies:
+        copy.wait()
 
 
 def shards(estimate, camera_blocks, block_lists, block_offsets, psf_index, psf_bank):
@@ -229,22 +337,23 @@
     brick = lax.axis_index("brick")
     view = lax.axis_index("view")
     core = lax.rem(brick, cores)
-    spot = jnp.stack([brick, view, core]).astype(jnp.int32)
     f32 = jnp.float32
 
-    lists = block_lists[0].reshape(-1)
+    lists = block_lists[0].transpose(0, 2, 1)
     packed = pl.pallas_call(
         pack_body,
-        out_shape=jax.ShapeDtypeStruct(
+        out_shape=pltpu.VMEM(
             (chips, cores, views, slots, block_rows, part * block_width), camera_blocks.dtype),
-        in_specs=[SMEM, SMEM, VMEM],
+        in_specs=[SMEM, VMEM],
         out_specs=VMEM,
+        compiler_params=GRANT,
         name="pack",
-    )(spot, lists, camera_blocks[0])
+    )(lists, camera_blocks[0])
     packed = packed.reshape(bricks * views, slots, block_rows, part * block_width)
     arrived = lax.all_to_all(packed, ("brick", "view"), 0, 0, tiled=True)
 
-    pieces = [lists, block_offsets[0], psf_index[0], psf_bank[0].reshape(-1)]
+    route = lax.dynamic_index_in_dim(lists, brick - core + cores - 1, 0, keepdims=False)
+    pieces = [route.reshape(-1), block_offsets[0], psf_index[0], psf_bank[0].reshape(-1)]
     starts = [0]
     for piece in pieces:
         starts.append(starts[-1] + piece.shape[0])
@@ -261,7 +370,7 @@
         views=views, part=part, cores=cores, taps=taps, kernels=kernels, slots=slots, bricks=bricks,
         per_holder=per_holder, rows_dev=rows_dev, block_width=block_width, table=length,
         offset_at=starts[1], index_at=starts[2], bank_at=starts[3],
-        pitch=cores * rows_dev + 2 * radius)
+        pitch=cores * rows_dev + 2 * radius + 1)
 
     parts = estimate.reshape(rows_dev, views, cores, part, columns)
     mine = parts[:, view, core]
@@ -272,51 +381,67 @@
     partner = lax.ppermute(theirs, "brick", swap)
     low = jnp.where(core == 0, mine, partner)
     high = jnp.where(core == 0, partner, mine)
-    top = lax.ppermute(high[rows_dev - radius :], "brick", up)
-    bottom = lax.ppermute(low[: 2 * radius], "brick", down)
+    top = lax.ppermute(encode_estimate(high[rows_dev - radius :]), "brick", up)
+    bottom = lax.ppermute(encode_estimate(low[: 2 * radius]), "brick", down)
 
     own_rows = cores * rows_dev
     rows_all = own_rows + radius
-    blurred, wx, wy = pl.pallas_call(
+    inverse, wx, wy = pl.pallas_call(
         functools.partial(blur_body, layout),
         out_shape=[
-            jax.ShapeDtypeStruct((rows_all, planes, columns), f32),
-            jax.ShapeDtypeStruct((taps, planes, LANES), f32),
-            jax.ShapeDtypeStruct((taps, planes, LANES), f32),
+            pltpu.VMEM((rows_all, planes, columns), f32),
+            pltpu.VMEM((taps, planes, LANES), f32),
+            pltpu.VMEM((taps, planes, LANES), f32),
         ],
-        in_specs=[SMEM, SMEM] + [VMEM] * 4,
+        in_specs=[SMEM] + [VMEM] * 4,
         out_specs=[VMEM] * 3,
         scratch_shapes=[pltpu.VMEM((rows_all + 2 * radius, planes, columns), f32)],
+        compiler_params=GRANT,
         name="blur",
-    )(spot, table, top, low, high, bottom)
+    )(table, *near_core(top, low, high, bottom))
 
     groups = planes * block_width // LANES
-    ratio = pl.pallas_call(
+    field, upward, downward = pl.pallas_call(
         functools.partial(ratio_body, layout),
-        out_shape=jax.ShapeDtypeStruct((rows_all, planes, columns), f32),
-        in_specs=[SMEM, SMEM, VMEM, VMEM],
-        out_specs=VMEM,
+        out_shape=[
+            pltpu.VMEM((rows_all + radius, planes, columns), f32),
+            pltpu.VMEM((2 * radius, planes, columns), jnp.int16),
+            pltpu.VMEM((radius, planes, columns), jnp.int16),
+        ],
+        in_specs=[SMEM, VMEM, VMEM],
+        out_specs=[VMEM] * 3,
         scratch_shapes=[
             pltpu.VMEM(((per_holder + 1) * groups * layout["pitch"], LANES), f32),
             pltpu.VMEM((columns // LANES * planes, LANES), f32),
         ],
+        compiler_params=GRANT,
         name="ratio",
-    )(spot, table, arrived, blurred)
-
-    before = lax.ppermute(ratio[own_rows - radius :], "brick", up)
-    after = lax.ppermute(ratio[:radius], "brick", down)
-    piece = jax.ShapeDtypeStruct((rows_dev, part, columns), f32)
+    )(table, *near_core(arrived, inverse))
+
+    before = lax.ppermute(upward, "brick", up)
+    after = lax.ppermute(downward, "brick", down)
+    done = pl.pallas_call(
+        functools.partial(own_body, layout),
+        out_shape=pltpu.VMEM((own_rows, planes, columns), f32),
+        in_specs=[VMEM] * 3,
+        out_specs=VMEM,
+        compiler_params=GRANT,
+        name="own",
+    )(*near_core(field, wx, wy))
+    piece = pltpu.VMEM((rows_dev, part, columns), f32)
     keep, send = pl.pallas_call(
-        functools.partial(correct_body, layout),
+        functools.partial(rest_body, layout),
         out_shape=[piece, piece],
-        in_specs=[SMEM] + [VMEM] * 7,
+        in_specs=[VMEM] * 7,
         out_specs=[VMEM] * 2,
         scratch_shapes=[
-            pltpu.VMEM((own_rows + 2 * radius, planes, columns), f32),
+            pltpu.VMEM((2 * radius, planes, columns), f32),
+            pltpu.VMEM((radius, planes, columns), f32),
             pltpu.VMEM((own_rows, planes, columns), f32),
         ],
-        name="correct",
-    )(spot, ratio, before, after, wx, wy, low, high)
+        compiler_params=GRANT,
+        name="rest",
+    )(*near_core(done, before, after, wx, wy, low, high))
 
     if views == 2:
         turn = [(0, 1), (1, 0)]
@@ -326,10 +451,12 @@
         return pl.pallas_call(
             join_body,
             out_shape=jax.ShapeDtypeStruct(estimate.shape, f32),
-            in_specs=[SMEM] + [VMEM] * 4,
-            out_specs=VMEM,
+            in_specs=[VMEM] * 4,
+            out_specs=HBM,
+            scratch_shapes=[pltpu.SemaphoreType.DMA((4,))],
+            compiler_params=GRANT,
             name="join",
-        )(spot, keep, near, far, far_near)
+        )(*near_core(keep, near, far, far_near))
     near = lax.ppermute(send, "brick", swap)
     both = jnp.stack([jnp.where(core == 0, keep, near), jnp.where(core == 0, near, keep)], axis=1)
     everything = lax.all_gather(both, "view")

time: 94 us -> 69 us (0.73)
  waiting for transfers between devices: 38.5 us -> 21.9 us
  Pallas kernels: 24.6 us -> 18.2 us
  local copies, waits for them, and re-layouts: 7.16 us -> 3.04 us
    ppermute x4, waiting for transfers between devices: 24.5 us -> 7.59 us  [the longest x1 4.77 us: shards(): top = lax.ppermute(encode_estimate(high[rows_dev - radius:]), 'brick', up)]
    pallas_call x4 -> x5, Pallas kernels: 22.4 us -> 17.2 us  [the longest x1 5.13 us: shards(): pl.pallas_call(functools.partial(blur_body, layout), out_shape=[pltpu.VME...]
    unnamed x32 -> x11, local copies, waits for them, and re-layouts: 4.16 us -> 1.85 us
    ppermute x1, waiting for transfers between devices: 0.01 us -> 2.15 us  [shards(): other = lax.ppermute(table, 'view', [(0, 1), (1, 0)])]
    slice x3 -> x0, local copies, waits for them, and re-layouts: 2.06 us -> none  [the longest x1 1.08 us: shards(): before = lax.ppermute(ratio[own_rows - radius:], 'brick', up)]
    pallas_call x1, Pallas kernels: 2.24 us -> 0.99 us  [shards(): pl.pallas_call(join_body, out_shape=jax.ShapeDtypeStruct(estimate.shape,...]
    ppermute x1, waiting for transfers between devices: 1.5 us -> 0.39 us  [shards(): near = lax.ppermute(send, 'brick', swap)]
    convert_element_type x0 -> x2, other arithmetic: none -> 1.08 us  [encode_estimate(): return jnp.clip(code, -CODE_TOP, CODE_TOP).astype(jnp.int16)]
  transfers between devices with their start and end apart: 10 -> 10, of which waited for: 6 -> 6; matrix products, arithmetic and copies ran while one was open for 2% -> 3% of each run, Pallas kernels for 8% -> 14%
where the time goes in v2:
time: 69 us; the launch traced here: 67.8 us
  starting transfers between devices  22.6 us (33%)
  waiting for transfers between devices  21.9 us (32%)
  Pallas kernels  18.2 us (26%)
  local copies, waits for them, and re-layouts  3.04 us (4%)
  other arithmetic  1.94 us (3%)
    ppermute x1, waiting for transfers between devices, shards(): far = lax.ppermute(keep, 'view', turn)  6.65 us
    all_to_all x1, starting transfers between devices, shards(): arrived = lax.all_to_all(packed, ('brick', 'view'), 0, 0, tiled=True)  6.14 us
    pallas_call x1, Pallas kernels, shards(): pl.pallas_call(functools.partial(blur_body, layout), out_shape=[pltpu.VME...  5.13 us
    pallas_call x1, Pallas kernels, shards(): pl.pallas_call(functools.partial(ratio_body, layout), out_shape=[pltpu.VM...  5.13 us
    ppermute x1, waiting for transfers between devices, shards(): far_near = lax.ppermute(near, 'view', turn)  5.08 us
    ppermute x1, waiting for transfers between devices, shards(): top = lax.ppermute(encode_estimate(high[rows_dev - radius:]), 'brick', up)  4.77 us
    ppermute x1, starting transfers between devices, shards(): before = lax.ppermute(upward, 'brick', up)  3.86 us
    ppermute x1, starting transfers between devices, shards(): bottom = lax.ppermute(encode_estimate(low[:2 * radius]), 'brick', down)  3.57 us
  transfers between devices with their start and end apart: 10, of which 6 were waited for; matrix products, arithmetic and copies ran while one was open for 3% of the time, Pallas kernels for 14%

profile of v2, /device:TPU:8, one launch (start us, length us, event | category | flops | bytes accessed | tf_op | source)
XLA Modules:
  0.0 67.8 jit_solution(812037884646463447)
XLA Ops:
  0.0 0.0 copy-start.4
  0.0 0.0 copy-start.3
  0.0 0.0 copy-start.2
  0.0 1.0 %dynamic-slice_bitcast_fusion = f32[8,16,512]{2,1,0:T(8,128)S(1)} fusion(f32[8,2,2,16,512]{4,3,2,1,0:T(8,128)} %bitcast.27, s32[]{:T(128)S(6)} %select_n.43, s32[]{:T(128)S(6)} %select_n.44), kind=kLoop, calls=%fused_computation.3 | loop fusion | bytes 524296 | tf_op jit(solution)/shard_map/squeeze | solution.py:377
  1.0 0.1 collective-permute-start.1
  1.1 0.0 copy-start
  1.1 1.0 %copy-done = bf16[1,16,8,2048]{3,2,1,0:T(8,128)(2,1)S(1)} copy-done((bf16[1,16,8,2048]{3,2,1,0:T(8,128)(2,1)S(1)}, bf16[1,16,8,2048]{3,2,1,0:T(8,128)(2,1)}, u32[]{:S(2)}) %copy-start) | copy-done | bytes 524312
  2.1 0.0 copy-start.1
  2.1 0.7 %copy-done.1 = s32[1,16,16,2]{2,3,1,0:T(2,128)S(1)} copy-done((s32[1,16,16,2]{2,3,1,0:T(2,128)S(1)}, s32[1,16,16,2]{2,3,1,0:T(2,128)}, u32[]{:S(2)}) %copy-start.1) | copy-done | bytes 2072
  2.9 1.7 %pack.1 = bf16[8,2,2,2,8,512]{5,4,3,2,1,0:T(8,128)(2,1)} custom-call(s32[16,2,16]{2,1,0:T(2,128)S(1)} %bitcast.26, bf16[16,8,2048]{2,1,0:T(8,128)(2,1)S(1)} %bitcast.25), custom_call_target="tpu_custom_call" | custom-call | tf_op jit(solution)/shard_map/pack/pallas_call | solution.py:343
  4.6 6.1 %all-to-all-start = ((bf16[32,2,8,512]{3,2,1,0:T(8,128)(2,1)}), bf16[32,2,8,512]{3,2,1,0:T(8,128)(2,1)S(1)}, u32[]{:S(2)}, u32[]{:S(2)}) async-start(bf16[32,2,8,512]{3,2,1,0:T(8,128)(2,1)} %bitcast.7), calls=%async_computation | async-start | bytes 1048576 | tf_op jit(solution)/shard_map/all_to_all | solution.py:353
  10.7 0.0 copy-done.4
  10.8 0.7 %convert_bitcast_fusion = f32[1,2,16]{2,1,0:T(2,128)S(1)} fusion(s32[1,16,16,2]{2,3,1,0:T(2,128)} %param.8, s32[]{:T(128)S(6)} %select_n.39), kind=kLoop, calls=%fused_computation.14 | loop fusion | flops 32 | bytes 260 | tf_op jit(solution)/shard_map/convert_element_type | solution.py:362
  11.4 0.1 convert_element_type.33
  11.5 0.0 copy-done.3
  11.5 0.0 copy-done.2
  11.5 0.1 copy.9
  11.6 0.1 reshape_squeeze.3
  11.7 0.1 pad_maximum_fusion.1
  11.8 1.5 %collective-permute-start = (f32[640]{0:T(1024)S(1)}, f32[640]{0:T(1024)S(1)}, u32[]{:S(2)}, u32[]{:S(2)}) collective-permute-start(f32[640]{0:T(1024)S(1)} %pad_maximum_fusion.1), channel_id=1, source_target_pairs={{0,1},{1,0},{2,3},{3,2},{4,5},{5,4},{6,7},{7,6},{8,9},{9,8},{10,11... | collective-permute-start | bytes 7688 | tf_op jit(solution)/shard_map/ppermute | solution.py:364
  13.3 2.1 %collective-permute-done = f32[640]{0:T(1024)S(1)} collective-permute-done((f32[640]{0:T(1024)S(1)}, f32[640]{0:T(1024)S(1)}, u32[]{:S(2)}, u32[]{:S(2)}) %collective-permute-start) | collective-permute-done | bytes 2592 | tf_op jit(solution)/shard_map/ppermute | solution.py:364
  15.4 0.1 broadcast_select_fusion.1
  15.5 0.0 collective-permute-done.1
  15.5 1.0 %clamp_convert_fusion = (s16[8,16,512]{2,1,0:T(8,128)(2,1)S(1)}, f32[8,16,512]{2,1,0:T(8,128)S(1)}, f32[8,16,512]{2,1,0:T(8,128)S(1)}) fusion(f32[8,16,512]{2,1,0:T(8,128)S(1)} %collective-permute-done.1, f32[8,2,2,16,512]{4,3,2,1,0:T(8,128)} %bitcast.28, s32[]{:T(128)S(6)} %select_n.43, s32[]{:T(128)S(6)} %select_n.45, pred[]{:T(512)S(6)} %eq.9), kind=kLoop, calls=%fused_computation.2 | loop fusion | flops 524288 | bytes 1179657 | tf_op jit(solution)/shard_map/convert_element_type | solution.py:92
  16.6 3.6 %collective-permute-start.3 = (s16[8,16,512]{2,1,0:T(8,128)(2,1)S(1)}, s16[8,16,512]{2,1,0:T(8,128)(2,1)S(1)}, u32[]{:S(2)}, u32[]{:S(2)}) collective-permute-start(s16[8,16,512]{2,1,0:T(8,128)(2,1)S(1)} %get-tuple-element.21), channel_id=1, source_target_pairs={{4,0},{6,2},{8,4},{10,6},{12,8},{14,10},{16,12},{18,14},{20,16},{2... | collective-permute-start | bytes 393224 | tf_op jit(solution)/shard_map/ppermute | solution.py:385
  20.2 2.3 %collective-permute-start.2 = (s16[4,16,512]{2,1,0:T(8,128)(2,1)S(1)}, s16[4,16,512]{2,1,0:T(8,128)(2,1)S(1)}, u32[]{:S(2)}, u32[]{:S(2)}) collective-permute-start(s16[4,16,512]{2,1,0:T(8,128)(2,1)S(1)} %fusion.4), channel_id=1, source_target_pairs={{0,4},{2,6},{4,8},{6,10},{8,12},{10,14},{12,16},{14,18},{16,20},{1... | collective-permute-start | bytes 196616 | tf_op jit(solution)/shard_map/ppermute | solution.py:384
  22.5 4.8 %collective-permute-done.2.top = s16[4,16,512]{2,1,0:T(8,128)(2,1)S(1)} collective-permute-done((s16[4,16,512]{2,1,0:T(8,128)(2,1)S(1)}, s16[4,16,512]{2,1,0:T(8,128)(2,1)S(1)}, u32[]{:S(2)}, u32[]{:S(2)}) %collective-permute-start.2) | collective-permute-done | bytes 65568 | tf_op jit(solution)/shard_map/ppermute | solution.py:384
  27.2 0.0 collective-permute-done.3.bottom
  27.3 5.1 %blur.1 = (f32[20,32,512]{2,1,0:T(8,128)S(1)}, f32[9,32,128]{2,1,0:T(8,128)S(1)}, f32[9,32,128]{2,1,0:T(8,128)S(1)}) custom-call(f32[1280]{0:T(1024)S(1)} %pad_maximum_fusion.table, s16[4,16,512]{2,1,0:T(8,128)(2,1)S(1)} %collective-permute-done.2.top, f32[8,16,512]{2,1,0:T(8,128)S(1)} %get-tuple-element.22.low, f32[8,16,512]{2,1,0:T(8,128)S(1)} %get-tuple-element.23.high, ...), custom_call_target="tpu_custom_call" | custom-call | tf_op jit(solution)/shard_map/blur/pallas_call | solution.py:389
  32.4 0.0 all-to-all-done.arrived
  32.4 5.1 %ratio.1 = (f32[24,32,512]{2,1,0:T(8,128)S(1)}, s16[8,32,512]{2,1,0:T(8,128)(2,1)S(1)}, s16[4,32,512]{2,1,0:T(8,128)(2,1)S(1)}) custom-call(f32[1280]{0:T(1024)S(1)} %pad_maximum_fusion.table, bf16[32,2,8,512]{3,2,1,0:T(8,128)(2,1)S(1)} %all-to-all-done.arrived, f32[20,32,512]{2,1,0:T(8,128)S(1)} %get-tuple-element.13.inverse), custom_call_target="tpu_custom_call" | custom-call | tf_op jit(solution)/shard_map/ratio/pallas_call | solution.py:404
  37.5 3.9 %collective-permute-start.4 = (s16[8,32,512]{2,1,0:T(8,128)(2,1)S(1)}, s16[8,32,512]{2,1,0:T(8,128)(2,1)S(1)}, u32[]{:S(2)}, u32[]{:S(2)}) collective-permute-start(s16[8,32,512]{2,1,0:T(8,128)(2,1)S(1)} %get-tuple-element.17), channel_id=1, source_target_pairs={{0,4},{2,6},{4,8},{6,10},{8,12},{10,14},{12,16},{14,18},{16,20},{1... | collective-permute-start | bytes 786440 | tf_op jit(solution)/shard_map/ppermute | solution.py:421
  41.4 2.9 %collective-permute-start.5 = (s16[4,32,512]{2,1,0:T(8,128)(2,1)S(1)}, s16[4,32,512]{2,1,0:T(8,128)(2,1)S(1)}, u32[]{:S(2)}, u32[]{:S(2)}) collective-permute-start(s16[4,32,512]{2,1,0:T(8,128)(2,1)S(1)} %get-tuple-element.18), channel_id=1, source_target_pairs={{4,0},{6,2},{8,4},{10,6},{12,8},{14,10},{16,12},{18,14},{20,16},{2... | collective-permute-start | bytes 393224 | tf_op jit(solution)/shard_map/ppermute | solution.py:422
  44.3 2.8 %own.1.done = f32[16,32,512]{2,1,0:T(8,128)S(1)} custom-call(f32[24,32,512]{2,1,0:T(8,128)S(1)} %get-tuple-element.14.field, f32[9,32,128]{2,1,0:T(8,128)S(1)} %get-tuple-element.15.wx, f32[9,32,128]{2,1,0:T(8,128)S(1)} %get-tuple-element.16.wy), custom_call_target="tpu_custom_call" | custom-call | tf_op jit(solution)/shard_map/own/pallas_call | solution.py:423
  47.1 2.8 %collective-permute-done.5.after = s16[4,32,512]{2,1,0:T(8,128)(2,1)S(1)} collective-permute-done((s16[4,32,512]{2,1,0:T(8,128)(2,1)S(1)}, s16[4,32,512]{2,1,0:T(8,128)(2,1)S(1)}, u32[]{:S(2)}, u32[]{:S(2)}) %collective-permute-start.5) | collective-permute-done | bytes 131104 | tf_op jit(solution)/shard_map/ppermute | solution.py:422
  49.9 0.0 collective-permute-done.4.before
  49.9 2.4 %rest.1 = (f32[8,16,512]{2,1,0:T(8,128)S(1)}, f32[8,16,512]{2,1,0:T(8,128)S(1)}) custom-call(f32[16,32,512]{2,1,0:T(8,128)S(1)} %own.1.done, s16[8,32,512]{2,1,0:T(8,128)(2,1)S(1)} %collective-permute-done.4.before, s16[4,32,512]{2,1,0:T(8,128)(2,1)S(1)} %collective-permute-done.5.after, f32[9,32,128]{2,1,0:T(8,128)S(1)} %get-tuple-element.15.wx, ...), custom_call_target="tpu_custom_call" | custom-call | tf_op jit(solution)/shard_map/rest/pallas_call | solution.py:432
  52.4 0.1 collective-permute-start.6
  52.4 1.1 %collective-permute-start.7 = (f32[8,16,512]{2,1,0:T(8,128)S(1)}, f32[8,16,512]{2,1,0:T(8,128)S(1)}, u32[]{:S(2)}, u32[]{:S(2)}) collective-permute-start(f32[8,16,512]{2,1,0:T(8,128)S(1)} %get-tuple-element.19.keep), channel_id=1, source_target_pairs={{0,1},{1,0},{2,3},{3,2},{4,5},{5,4},{6,7},{7,6},{8,9},{9,8},{10,11... | collective-permute-start | bytes 786440 | tf_op jit(solution)/shard_map/ppermute | solution.py:448
  53.6 0.4 collective-permute-done.6.near
  54.0 1.1 %collective-permute-start.8 = (f32[8,16,512]{2,1,0:T(8,128)S(1)}, f32[8,16,512]{2,1,0:T(8,128)S(1)}, u32[]{:S(2)}, u32[]{:S(2)}) collective-permute-start(f32[8,16,512]{2,1,0:T(8,128)S(1)} %collective-permute-done.6.near), channel_id=1, source_target_pairs={{0,1},{1,0},{2,3},{3,2},{4,5},{5,4},{6,7},{7,6},{8,9},{9,8},{10,11... | collective-permute-start | bytes 786440 | tf_op jit(solution)/shard_map/ppermute | solution.py:450
  55.0 6.7 %collective-permute-done.7.far = f32[8,16,512]{2,1,0:T(8,128)S(1)} collective-permute-done((f32[8,16,512]{2,1,0:T(8,128)S(1)}, f32[8,16,512]{2,1,0:T(8,128)S(1)}, u32[]{:S(2)}, u32[]{:S(2)}) %collective-permute-start.7) | collective-permute-done | bytes 262176 | tf_op jit(solution)/shard_map/ppermute | solution.py:448
  61.7 5.1 %collective-permute-done.8.far_near = f32[8,16,512]{2,1,0:T(8,128)S(1)} collective-permute-done((f32[8,16,512]{2,1,0:T(8,128)S(1)}, f32[8,16,512]{2,1,0:T(8,128)S(1)}, u32[]{:S(2)}, u32[]{:S(2)}) %collective-permute-start.8) | collective-permute-done | bytes 262176 | tf_op jit(solution)/shard_map/ppermute | solution.py:450
  66.8 1.0 %join.1 = f32[8,64,512]{2,1,0:T(8,128)} custom-call(f32[8,16,512]{2,1,0:T(8,128)S(1)} %get-tuple-element.19.keep, f32[8,16,512]{2,1,0:T(8,128)S(1)} %collective-permute-done.6.near, f32[8,16,512]{2,1,0:T(8,128)S(1)} %collective-permute-done.7.far, f32[8,16,512]{2,1,0:T(8,128)S(1)} %collective-permute-done.8.far_near), custom_call_target="tpu_custom_call" | custom-call | tf_op jit(solution)/shard_map/join/pallas_call | solution.py:451
  (4 shorter events, 0.1 us)
Async XLA Ops:
  0.0 10.7 %copy-start.4 = (s32[1,64]{1,0:T(1,128)S(1)}, s32[1,64]{1,0:T(1,128)}, u32[]{:S(2)}) copy-start(s32[1,64]{1,0:T(1,128)} %param.10) | copy-start | bytes 772
  0.0 11.5 %copy-start.3 = (s32[1,256]{1,0:T(1,128)S(1)}, s32[1,256]{1,0:T(1,128)}, u32[]{:S(2)}) copy-start(s32[1,256]{1,0:T(1,128)} %param.9) | copy-start | bytes 3076
  0.0 11.5 %copy-start.2 = (f32[1,2,16,9]{2,1,3,0:T(2,128)S(1)}, f32[1,2,16,9]{2,1,3,0:T(2,128)}, u32[]{:S(2)}) copy-start(f32[1,2,16,9]{2,1,3,0:T(2,128)} %param.11) | copy-start | bytes 3460
  1.0 14.5 %collective-permute-start.1 = (f32[8,16,512]{2,1,0:T(8,128)S(1)}, f32[8,16,512]{2,1,0:T(8,128)S(1)}, u32[]{:S(2)}, u32[]{:S(2)}) collective-permute-start(f32[8,16,512]{2,1,0:T(8,128)S(1)} %dynamic-slice_bitcast_fusion), channel_id=1, source_target_pairs={{0,2},{2,0},{4,6},{6,4},{8,10},{10,8},{12,14},{14,12},{16,18},{18,... | collective-permute-start | bytes 786440 | tf_op jit(solution)/shard_map/ppermute | solution.py:381
  1.1 1.0 %copy-start = (bf16[1,16,8,2048]{3,2,1,0:T(8,128)(2,1)S(1)}, bf16[1,16,8,2048]{3,2,1,0:T(8,128)(2,1)}, u32[]{:S(2)}) copy-start(bf16[1,16,8,2048]{3,2,1,0:T(8,128)(2,1)} %param.7) | copy-start | bytes 1572868
  2.1 0.7 %copy-start.1 = (s32[1,16,16,2]{2,3,1,0:T(2,128)S(1)}, s32[1,16,16,2]{2,3,1,0:T(2,128)}, u32[]{:S(2)}) copy-start(s32[1,16,16,2]{2,3,1,0:T(2,128)} %param.8) | copy-start | bytes 6148
  4.6 27.8 %all-to-all-start = ((bf16[32,2,8,512]{3,2,1,0:T(8,128)(2,1)}), bf16[32,2,8,512]{3,2,1,0:T(8,128)(2,1)S(1)}, u32[]{:S(2)}, u32[]{:S(2)}) async-start(bf16[32,2,8,512]{3,2,1,0:T(8,128)(2,1)} %bitcast.7), calls=%async_computation | async-start | bytes 1048576 | tf_op jit(solution)/shard_map/all_to_all | solution.py:353
  11.8 3.6 %collective-permute-start = (f32[640]{0:T(1024)S(1)}, f32[640]{0:T(1024)S(1)}, u32[]{:S(2)}, u32[]{:S(2)}) collective-permute-start(f32[640]{0:T(1024)S(1)} %pad_maximum_fusion.1), channel_id=1, source_target_pairs={{0,1},{1,0},{2,3},{3,2},{4,5},{5,4},{6,7},{7,6},{8,9},{9,8},{10,11... | collective-permute-start | bytes 7688 | tf_op jit(solution)/shard_map/ppermute | solution.py:364
  16.6 10.7 %collective-permute-start.3 = (s16[8,16,512]{2,1,0:T(8,128)(2,1)S(1)}, s16[8,16,512]{2,1,0:T(8,128)(2,1)S(1)}, u32[]{:S(2)}, u32[]{:S(2)}) collective-permute-start(s16[8,16,512]{2,1,0:T(8,128)(2,1)S(1)} %get-tuple-element.21), channel_id=1, source_target_pairs={{4,0},{6,2},{8,4},{10,6},{12,8},{14,10},{16,12},{18,14},{20,16},{2... | collective-permute-start | bytes 393224 | tf_op jit(solution)/shard_map/ppermute | solution.py:385
  20.2 7.1 %collective-permute-start.2 = (s16[4,16,512]{2,1,0:T(8,128)(2,1)S(1)}, s16[4,16,512]{2,1,0:T(8,128)(2,1)S(1)}, u32[]{:S(2)}, u32[]{:S(2)}) collective-permute-start(s16[4,16,512]{2,1,0:T(8,128)(2,1)S(1)} %fusion.4), channel_id=1, source_target_pairs={{0,4},{2,6},{4,8},{6,10},{8,12},{10,14},{12,16},{14,18},{16,20},{1... | collective-permute-start | bytes 196616 | tf_op jit(solution)/shard_map/ppermute | solution.py:384
  37.5 12.4 %collective-permute-start.4 = (s16[8,32,512]{2,1,0:T(8,128)(2,1)S(1)}, s16[8,32,512]{2,1,0:T(8,128)(2,1)S(1)}, u32[]{:S(2)}, u32[]{:S(2)}) collective-permute-start(s16[8,32,512]{2,1,0:T(8,128)(2,1)S(1)} %get-tuple-element.17), channel_id=1, source_target_pairs={{0,4},{2,6},{4,8},{6,10},{8,12},{10,14},{12,16},{14,18},{16,20},{1... | collective-permute-start | bytes 786440 | tf_op jit(solution)/shard_map/ppermute | solution.py:421
  41.4 8.5 %collective-permute-start.5 = (s16[4,32,512]{2,1,0:T(8,128)(2,1)S(1)}, s16[4,32,512]{2,1,0:T(8,128)(2,1)S(1)}, u32[]{:S(2)}, u32[]{:S(2)}) collective-permute-start(s16[4,32,512]{2,1,0:T(8,128)(2,1)S(1)} %get-tuple-element.18), channel_id=1, source_target_pairs={{4,0},{6,2},{8,4},{10,6},{12,8},{14,10},{16,12},{18,14},{20,16},{2... | collective-permute-start | bytes 393224 | tf_op jit(solution)/shard_map/ppermute | solution.py:422
  52.4 1.6 %collective-permute-start.6 = (f32[8,16,512]{2,1,0:T(8,128)S(1)}, f32[8,16,512]{2,1,0:T(8,128)S(1)}, u32[]{:S(2)}, u32[]{:S(2)}) collective-permute-start(f32[8,16,512]{2,1,0:T(8,128)S(1)} %get-tuple-element.20), channel_id=1, source_target_pairs={{0,2},{2,0},{4,6},{6,4},{8,10},{10,8},{12,14},{14,12},{16,18},{18,... | collective-permute-start | bytes 786440 | tf_op jit(solution)/shard_map/ppermute | solution.py:449
  52.4 9.2 %collective-permute-start.7 = (f32[8,16,512]{2,1,0:T(8,128)S(1)}, f32[8,16,512]{2,1,0:T(8,128)S(1)}, u32[]{:S(2)}, u32[]{:S(2)}) collective-permute-start(f32[8,16,512]{2,1,0:T(8,128)S(1)} %get-tuple-element.19.keep), channel_id=1, source_target_pairs={{0,1},{1,0},{2,3},{3,2},{4,5},{5,4},{6,7},{7,6},{8,9},{9,8},{10,11... | collective-permute-start | bytes 786440 | tf_op jit(solution)/shard_map/ppermute | solution.py:448
  54.0 12.8 %collective-permute-start.8 = (f32[8,16,512]{2,1,0:T(8,128)S(1)}, f32[8,16,512]{2,1,0:T(8,128)S(1)}, u32[]{:S(2)}, u32[]{:S(2)}) collective-permute-start(f32[8,16,512]{2,1,0:T(8,128)S(1)} %collective-permute-done.6.near), channel_id=1, source_target_pairs={{0,1},{1,0},{2,3},{3,2},{4,5},{5,4},{6,7},{7,6},{8,9},{9,8},{10,11... | collective-permute-start | bytes 786440 | tf_op jit(solution)/shard_map/ppermute | solution.py:450

commit v3 on v2

--- a/solution.py
+++ b/solution.py
@@ -8,10 +8,13 @@
 from jax.experimental.pallas import tpu as pltpu
 from jax.sharding import PartitionSpec as P
 
+
 CAMERA = (0.099609375, 2.0)
 PSF = (0.03, 0.3)
 ESTIMATE = (0.5, 2.0)
 CODE_TOP = 32767.0
+SCALE_STEPS = 64.0
+TINY = 1e-35
 LANES = 128
 SUBLANES = 8
 GRANT = pltpu.CompilerParams(vmem_limit_bytes=12 << 20)
@@ -58,6 +61,10 @@
     return [pltpu.with_memory_space_constraint(value, pltpu.VMEM) for value in values]
 
 
+def far_memory(*values):
+    return [pltpu.with_memory_space_constraint(value, pltpu.HBM) for value in values]
+
+
 def position(cores):
     brick = lax.axis_index("brick")
     return lax.div(brick, cores), lax.rem(brick, cores), lax.axis_index("view")
@@ -89,7 +96,7 @@
 def encode_estimate(value):
     scale = 2 * CODE_TOP / (ESTIMATE[1] - ESTIMATE[0])
     code = jnp.round((value - ESTIMATE[0]) * scale) - CODE_TOP
-    return jnp.clip(code, -CODE_TOP, CODE_TOP).astype(jnp.int16)
+    return code.astype(jnp.int32).astype(jnp.int16)
 
 
 def decode_estimate(code):
@@ -97,31 +104,68 @@
     return (code.astype(jnp.int32).astype(jnp.float32) + CODE_TOP) * scale + ESTIMATE[0]
 
 
-def pack_body(lists, blocks, out):
+def encode_rows(value):
+    most = jnp.maximum(jnp.max(value, axis=-1, keepdims=True), TINY)
+    level = jnp.ceil(jnp.log(most) * (SCALE_STEPS / math.log(2.0))) + 1.0
+    factor = jnp.exp(level * (-math.log(2.0) / SCALE_STEPS)) * (2 * CODE_TOP)
+    code = jnp.minimum(jnp.round(value * factor), 2 * CODE_TOP) - CODE_TOP
+    return code.astype(jnp.int32).astype(jnp.int16), level
+
+
+def decode_row(code, levels, row):
+    levels = levels[:, row : row + 1].astype(jnp.int32).astype(jnp.float32)
+    factor = jnp.exp(levels * (math.log(2.0) / SCALE_STEPS)) * (1.0 / (2 * CODE_TOP))
+    return (code.astype(jnp.int32).astype(jnp.float32) + CODE_TOP) * factor
+
+
+def pack_body(listed, blocks, estimate, out, edges, mine, theirs, held, lists, sems):
     chips, cores, views, slots, _, width = out.shape
     here = lax.axis_index("brick")
+    _, core, view = position(cores)
+    part = mine.shape[1]
+    copies = [
+        pltpu.make_async_copy(blocks, held, sems.at[0]),
+        pltpu.make_async_copy(listed, lists, sems.at[3]),
+    ]
+    for index, (half, target) in enumerate(((core, mine), (1 - core, theirs))):
+        begin = pl.multiple_of((view * cores + half) * part, part)
+        copies.append(pltpu.make_async_copy(
+            estimate.at[:, pl.ds(begin, part), :], target, sems.at[1 + index]))
+    for copy in reversed(copies):
+        copy.start()
+    copies[2].wait()
+    edges[core] = encode_estimate(mine[...])
+    copies[3].wait()
+    edges[1 - core] = encode_estimate(theirs[...])
+    copies[1].wait()
+    copies[0].wait()
 
     def one_chip(chip, carry):
         for slot in range(slots):
             block = jnp.maximum(lists[cores * chip + cores - 1, slot, here], 0)
-            for core in range(cores):
-                for view in range(views):
-                    begin = (view * cores + core) * width
-                    out[chip, core, view, slot] = blocks[block, :, begin : begin + width]
+            for half in range(cores):
+                for other in range(views):
+                    begin = (other * cores + half) * width
+                    out[chip, half, other, slot] = held[block, :, begin : begin + width]
         return carry
 
-    lax.fori_loop(0, chips, one_chip, 0)
-
-
-def blur_body(layout, table, top, low, high, bottom, inverse, wx, wy, field):
+    lax.fori_loop(0, chips, one_chip, 0, unroll=2)
+
+
+def blur_body(layout, table, mine, partner, across, passed, inverse, wx, wy, field):
     views, part, cores, taps, kernels = (
         layout["views"], layout["part"], layout["cores"], layout["taps"], layout["kernels"])
     chip, core, view_here = position(cores)
     where = view_here * cores + core
     has_top = (chip > 0).astype(jnp.float32)
     has_bottom = (chip < layout["bricks"] // cores - 1).astype(jnp.float32)
-    rows = (decode_estimate(top[...]) * has_top, low[...], high[...],
-            decode_estimate(bottom[...]) * has_bottom)
+    first = core == 0
+    radius = taps // 2
+    direct = decode_estimate(across[core])
+    relayed = decode_estimate(passed[...])
+    rows = (jnp.where(first, direct, relayed)[mine.shape[0] - radius :] * has_top,
+            jnp.where(first, mine[...], partner[...]), jnp.where(first, partner[...], mine[...]),
+            jnp.where(first, relayed, direct)[: 2 * radius] * has_bottom)
     for view in range(views):
         base = view * layout["table"]
 
@@ -246,7 +290,7 @@
     lax.fori_loop(0, rows, one_row, 0, unroll=2)
 
 
-def rest_body(layout, done, before, after, wx, wy, low, high, keep, send, ahead, behind, total):
+def rest_body(layout, done, before, after, wx, wy, mine, partner, keep, send, ahead, behind, total):
     views, part, cores, taps = layout["views"], layout["part"], layout["cores"], layout["taps"]
     bricks = layout["bricks"]
     own_rows, planes, columns = done.shape
@@ -295,29 +339,41 @@
 
     lax.fori_loop(0, planes // SUBLANES, one_group, 0)
 
+    wide = lax.broadcasted_iota(jnp.int32, (part, LANES), 1)
+
     def finish(half, source, target):
-        rows = pl.ds(half * rows_dev, rows_dev)
-        product = total[rows, 0:part, :]
-        for view in range(1, views):
-            product = product * total[rows, view * part : (view + 1) * part, :]
-        target[...] = source * product
-
-    mine = jnp.where(core == 0, low[...], high[...])
-    theirs = jnp.where(core == 0, high[...], low[...])
+        def one_row(row, levels):
+            at = half * rows_dev + row
+            value = source[row]
+            for view in range(views):
+                value = value * total[at, view * part : (view + 1) * part, :]
+            begin = row * columns if isinstance(row, int) else pl.multiple_of(row * columns, LANES)
+            target[:, pl.ds(begin, columns)], level = encode_rows(value)
+            return jnp.where(wide == row, level, levels)
+
+        levels = lax.fori_loop(
+            0, rows_dev, one_row, jnp.zeros((part, LANES), jnp.float32), unroll=True)
+        target[:, rows_dev * columns :] = levels.astype(jnp.int32).astype(jnp.int16)
+
     finish(core, mine, keep)
-    finish(1 - core, theirs, send)
-
-
-def join_body(keep, near, far, far_near, out, sems):
+    finish(1 - core, partner, send)
+
+
+def join_body(keep, near, far, far_near, out, pieces, sems):
     _, core, view = position(2)
-    part = keep.shape[1]
+    rows, columns = out.shape[0], out.shape[2]
+    part = keep.shape[0]
     copies = []
     for index, (v, c, piece) in enumerate((
         (view, core, keep), (view, 1 - core, near), (1 - view, core, far), (1 - view, 1 - core, far_near))):
+        levels = piece[:, rows * columns :]
+        for row in range(rows):
+            pieces[index, row] = decode_row(
+                piece[:, row * columns : (row + 1) * columns], levels, row)
         begin = pl.multiple_of((v * 2 + c) * part, part)
-        copies.append(pltpu.make_async_copy(piece, out.at[:, pl.ds(begin, part), :], sems.at[index]))
-    for copy in copies:
-        copy.start()
+        copies.append(pltpu.make_async_copy(
+            pieces.at[index], out.at[:, pl.ds(begin, part), :], sems.at[index]))
+        copies[-1].start()
     for copy in copies:
         copy.wait()
 
@@ -340,16 +396,29 @@
     f32 = jnp.float32
 
     lists = block_lists[0].transpose(0, 2, 1)
-    packed = pl.pallas_call(
+    outgoing = pltpu.VMEM(
+        (chips, cores, views, slots, block_rows, part * block_width), camera_blocks.dtype)
+    piece = pltpu.VMEM((rows_dev, part, columns), f32)
+    coded = pltpu.VMEM((cores, rows_dev, part, columns), jnp.int16)
+    packed, edges, mine, theirs = pl.pallas_call(
         pack_body,
-        out_shape=pltpu.VMEM(
-            (chips, cores, views, slots, block_rows, part * block_width), camera_blocks.dtype),
-        in_specs=[SMEM, VMEM],
-        out_specs=VMEM,
+        out_shape=[outgoing, coded, piece, piece],
+        in_specs=[HBM] * 3,
+        out_specs=[VMEM] * 4,
+        scratch_shapes=[
+            pltpu.VMEM(camera_blocks.shape[1:], camera_blocks.dtype),
+            pltpu.SMEM(lists.shape, jnp.int32),
+            pltpu.SemaphoreType.DMA((4,)),
+        ],
         compiler_params=GRANT,
         name="pack",
-    )(lists, camera_blocks[0])
+    )(*far_memory(lists, camera_blocks[0], estimate))
+    swap = [(i, i ^ 1) for i in range(bricks)]
     packed = packed.reshape(bricks * views, slots, block_rows, part * block_width)
+    across = lax.ppermute(edges, "brick", [
+        (i, j) for i in range(bricks) for j in [i + 1 if i % cores else i - 1]
+        if 0 <= j < bricks])
+    partner = lax.ppermute(theirs, "brick", swap)
     arrived = lax.all_to_all(packed, ("brick", "view"), 0, 0, tiled=True)
 
     route = lax.dynamic_index_in_dim(lists, brick - core + cores - 1, 0, keepdims=False)
@@ -362,27 +431,21 @@
         [piece.astype(f32) for piece in pieces] + [jnp.zeros((length - starts[-1],), f32)])
     if views == 2:
         other = lax.ppermute(table, "view", [(0, 1), (1, 0)])
-        table = jnp.concatenate(
-            [jnp.where(view == 0, table, other), jnp.where(view == 0, other, table)])
-    else:
-        table = lax.all_gather(table, "view", tiled=True)
     layout = dict(
         views=views, part=part, cores=cores, taps=taps, kernels=kernels, slots=slots, bricks=bricks,
         per_holder=per_holder, rows_dev=rows_dev, block_width=block_width, table=length,
         offset_at=starts[1], index_at=starts[2], bank_at=starts[3],
         pitch=cores * rows_dev + 2 * radius + 1)
 
-    parts = estimate.reshape(rows_dev, views, cores, part, columns)
-    mine = parts[:, view, core]
-    theirs = parts[:, view, 1 - core]
-    swap = [(i, i ^ 1) for i in range(bricks)]
     up = [(i, i + cores) for i in range(bricks - cores)]
     down = [(i + cores, i) for i in range(bricks - cores)]
-    partner = lax.ppermute(theirs, "brick", swap)
-    low = jnp.where(core == 0, mine, partner)
-    high = jnp.where(core == 0, partner, mine)
-    top = lax.ppermute(encode_estimate(high[rows_dev - radius :]), "brick", up)
-    bottom = lax.ppermute(encode_estimate(low[: 2 * radius]), "brick", down)
+    passed = lax.ppermute(
+        lax.dynamic_index_in_dim(across, 1 - core, 0, keepdims=False), "brick", swap)
+    if views == 2:
+        table = jnp.concatenate(
+            [jnp.where(view == 0, table, other), jnp.where(view == 0, other, table)])
+    else:
+        table = lax.all_gather(table, "view", tiled=True)
 
     own_rows = cores * rows_dev
     rows_all = own_rows + radius
@@ -398,7 +461,7 @@
         scratch_shapes=[pltpu.VMEM((rows_all + 2 * radius, planes, columns), f32)],
         compiler_params=GRANT,
         name="blur",
-    )(table, *near_core(top, low, high, bottom))
+    )(table, *near_core(mine, partner, across, passed))
 
     groups = planes * block_width // LANES
     field, upward, downward = pl.pallas_call(
@@ -428,7 +491,7 @@
         compiler_params=GRANT,
         name="own",
     )(*near_core(field, wx, wy))
-    piece = pltpu.VMEM((rows_dev, part, columns), f32)
+    piece = pltpu.VMEM((part, rows_dev * columns + LANES), jnp.int16)
     keep, send = pl.pallas_call(
         functools.partial(rest_body, layout),
         out_shape=[piece, piece],
@@ -441,7 +504,7 @@
         ],
         compiler_params=GRANT,
         name="rest",
-    )(*near_core(done, before, after, wx, wy, low, high))
+    )(*near_core(done, before, after, wx, wy, mine, partner))
 
     if views == 2:
         turn = [(0, 1), (1, 0)]
@@ -453,14 +516,20 @@
             out_shape=jax.ShapeDtypeStruct(estimate.shape, f32),
             in_specs=[VMEM] * 4,
             out_specs=HBM,
-            scratch_shapes=[pltpu.SemaphoreType.DMA((4,))],
+            scratch_shapes=[
+                pltpu.VMEM((4, rows_dev, part, columns), f32), pltpu.SemaphoreType.DMA((4,))],
             compiler_params=GRANT,
             name="join",
         )(*near_core(keep, near, far, far_near))
     near = lax.ppermute(send, "brick", swap)
-    both = jnp.stack([jnp.where(core == 0, keep, near), jnp.where(core == 0, near, keep)], axis=1)
-    everything = lax.all_gather(both, "view")
-    return everything.transpose(1, 0, 2, 3, 4).reshape(estimate.shape)
+    both = jnp.stack([jnp.where(core == 0, keep, near), jnp.where(core == 0, near, keep)])
+    coded = lax.all_gather(both, "view").reshape((-1,) + keep.shape)
+    rows = [
+        jax.vmap(lambda piece, row=row: decode_row(
+            piece[:, row * columns : (row + 1) * columns], piece[:, rows_dev * columns :], row))(coded)
+        for row in range(rows_dev)
+    ]
+    return jnp.stack(rows).reshape(estimate.shape)
 
 
 def solution(mesh):

time: 69 us -> 63.4 us (0.919)
  the two profiles are of different devices: /device:TPU:8 before, /device:TPU:16 now
where the time goes in v3:
time: 63.4 us; the launch traced here: 63.1 us
  waiting for transfers between devices  22.3 us (35%)
  starting transfers between devices  20.3 us (32%)
  Pallas kernels  19.2 us (30%)
  other arithmetic  0.86 us (1%)
    ppermute x1, waiting for transfers between devices, shards(): lax.ppermute(edges, 'brick', [(i, j) for i in range(bricks) for j in [i +...  10.8 us
    all_to_all x1, starting transfers between devices, shards(): arrived = lax.all_to_all(packed, ('brick', 'view'), 0, 0, tiled=True)  5.94 us
    pallas_call x1, Pallas kernels, shards(): pl.pallas_call(functools.partial(blur_body, layout), out_shape=[pltpu.VME...  5.23 us
    pallas_call x1, Pallas kernels, shards(): pl.pallas_call(functools.partial(ratio_body, layout), out_shape=[pltpu.VM...  5.14 us
    ppermute x1, starting transfers between devices, shards(): after = lax.ppermute(downward, 'brick', down)  4.82 us
    ppermute x1, waiting for transfers between devices, shards(): after = lax.ppermute(downward, 'brick', down)  4.24 us
    ppermute x1, waiting for transfers between devices, shards(): far = lax.ppermute(keep, 'view', turn)  3.72 us
    ppermute x1, starting transfers between devices, shards(): lax.ppermute(edges, 'brick', [(i, j) for i in range(bricks) for j in [i +...  3.09 us
  transfers between devices with their start and end apart: 10, of which 5 were waited for; matrix products, arithmetic and copies ran while one was open for 2% of the time, Pallas kernels for 13%

profile of v3, /device:TPU:16, one launch (start us, length us, event | category | flops | bytes accessed | tf_op | source)
XLA Modules:
  0.0 63.1 jit_solution(5790970575993187569)
XLA Ops:
  0.0 0.0 copy-start.1
  0.0 0.0 copy-start
  0.0 0.0 copy-start.2
  0.0 2.1 %pack.1 = (bf16[8,2,2,2,8,512]{5,4,3,2,1,0:T(8,128)(2,1)}, s16[2,8,16,512]{3,2,1,0:T(8,128)(2,1)S(1)}, f32[8,16,512]{2,1,0:T(8,128)S(1)}, f32[8,16,512]{2,1,0:T(8,128)S(1)}) custom-call(s32[16,2,16]{2,1,0:T(2,128)} %bitcast.17, bf16[16,8,2048]{2,1,0:T(8,128)(2,1)} %bitcast.16, f32[8,64,512]{2,1,0:T(8,128)} %estimate.1), custom_call_target="tpu_custom_call" | custom-call | tf_op jit(solution)/shard_map/pack/pallas_call | solution.py:403
  2.1 5.9 %all-to-all-start = ((bf16[32,2,8,512]{3,2,1,0:T(8,128)(2,1)}), bf16[32,2,8,512]{3,2,1,0:T(8,128)(2,1)S(1)}, u32[]{:S(2)}, u32[]{:S(2)}) async-start(bf16[32,2,8,512]{3,2,1,0:T(8,128)(2,1)} %bitcast.7), calls=%async_computation | async-start | bytes 1048576 | tf_op jit(solution)/shard_map/all_to_all | solution.py:422
  8.1 3.1 %collective-permute-start.2 = (s16[2,8,16,512]{3,2,1,0:T(8,128)(2,1)S(1)}, s16[2,8,16,512]{3,2,1,0:T(8,128)(2,1)S(1)}, u32[]{:S(2)}, u32[]{:S(2)}) collective-permute-start(s16[2,8,16,512]{3,2,1,0:T(8,128)(2,1)S(1)} %get-tuple-element.20), channel_id=1, source_target_pairs={{2,4},{4,2},{6,8},{8,6},{10,12},{12,10},{14,16},{16,14},{18,20},{2... | collective-permute-start | bytes 786440 | tf_op jit(solution)/shard_map/ppermute | solution.py:418
  11.2 0.7 %convert_bitcast_fusion = f32[1,2,16]{2,1,0:T(2,128)S(1)} fusion(s32[1,16,16,2]{2,3,1,0:T(2,128)} %param.8, s32[]{:T(128)S(6)} %select_n.21), kind=kLoop, calls=%fused_computation.5 | loop fusion | flops 32 | bytes 260 | tf_op jit(solution)/shard_map/convert_element_type | solution.py:431
  11.9 0.1 convert_element_type.27
  12.0 0.0 copy-done.1
  12.0 0.0 copy-done
  12.0 0.1 copy.7
  12.1 0.1 reshape_squeeze.3
  12.2 0.0 copy-done.2
  12.2 0.1 pad_maximum_fusion.1
  12.3 1.5 %collective-permute-start = (f32[640]{0:T(1024)S(1)}, f32[640]{0:T(1024)S(1)}, u32[]{:S(2)}, u32[]{:S(2)}) collective-permute-start(f32[640]{0:T(1024)S(1)} %pad_maximum_fusion.1), channel_id=1, source_target_pairs={{0,1},{1,0},{2,3},{3,2},{4,5},{5,4},{6,7},{7,6},{8,9},{9,8},{10,11... | collective-permute-start | bytes 7688 | tf_op jit(solution)/shard_map/ppermute | solution.py:433
  13.7 0.1 collective-permute-start.1
  13.9 10.8 %collective-permute-done.2.across = s16[2,8,16,512]{3,2,1,0:T(8,128)(2,1)S(1)} collective-permute-done((s16[2,8,16,512]{3,2,1,0:T(8,128)(2,1)S(1)}, s16[2,8,16,512]{3,2,1,0:T(8,128)(2,1)S(1)}, u32[]{:S(2)}, u32[]{:S(2)}) %collective-permute-start.2) | collective-permute-done | bytes 262176 | tf_op jit(solution)/shard_map/ppermute | solution.py:418
  24.7 0.1 collective-permute-start.3
  24.7 0.0 collective-permute-done
  24.7 0.1 broadcast_select_fusion.1
  24.8 0.0 collective-permute-done.1.partner
  24.8 1.2 %collective-permute-done.3.passed = s16[8,16,512]{2,1,0:T(8,128)(2,1)S(1)} collective-permute-done((s16[8,16,512]{2,1,0:T(8,128)(2,1)S(1)}, s16[8,16,512]{2,1,0:T(8,128)(2,1)S(1)}, u32[]{:S(2)}, u32[]{:S(2)}) %collective-permute-start.3) | collective-permute-done | bytes 131104 | tf_op jit(solution)/shard_map/ppermute | solution.py:442
  26.1 5.2 %blur.1 = (f32[20,32,512]{2,1,0:T(8,128)S(1)}, f32[9,32,128]{2,1,0:T(8,128)S(1)}, f32[9,32,128]{2,1,0:T(8,128)S(1)}) custom-call(f32[1280]{0:T(1024)S(1)} %pad_maximum_fusion.table, f32[8,16,512]{2,1,0:T(8,128)S(1)} %get-tuple-element.18.mine, f32[8,16,512]{2,1,0:T(8,128)S(1)} %collective-permute-done.1.partner, ...), custom_call_target="tpu_custom_call" | custom-call | tf_op jit(solution)/shard_map/blur/pallas_call | solution.py:452
  31.3 0.0 all-to-all-done.arrived
  31.3 5.1 %ratio.1 = (f32[24,32,512]{2,1,0:T(8,128)S(1)}, s16[8,32,512]{2,1,0:T(8,128)(2,1)S(1)}, s16[4,32,512]{2,1,0:T(8,128)(2,1)S(1)}) custom-call(f32[1280]{0:T(1024)S(1)} %pad_maximum_fusion.table, bf16[32,2,8,512]{3,2,1,0:T(8,128)(2,1)S(1)} %all-to-all-done.arrived, f32[20,32,512]{2,1,0:T(8,128)S(1)} %get-tuple-element.21.inverse), custom_call_target="tpu_custom_call" | custom-call | tf_op jit(solution)/shard_map/ratio/pallas_call | solution.py:467
  36.5 1.9 %collective-permute-start.4 = (s16[8,32,512]{2,1,0:T(8,128)(2,1)S(1)}, s16[8,32,512]{2,1,0:T(8,128)(2,1)S(1)}, u32[]{:S(2)}, u32[]{:S(2)}) collective-permute-start(s16[8,32,512]{2,1,0:T(8,128)(2,1)S(1)} %get-tuple-element.25), channel_id=1, source_target_pairs={{0,4},{2,6},{4,8},{6,10},{8,12},{10,14},{12,16},{14,18},{16,20},{1... | collective-permute-start | bytes 786440 | tf_op jit(solution)/shard_map/ppermute | solution.py:484
  38.4 4.8 %collective-permute-start.5 = (s16[4,32,512]{2,1,0:T(8,128)(2,1)S(1)}, s16[4,32,512]{2,1,0:T(8,128)(2,1)S(1)}, u32[]{:S(2)}, u32[]{:S(2)}) collective-permute-start(s16[4,32,512]{2,1,0:T(8,128)(2,1)S(1)} %get-tuple-element.26), channel_id=1, source_target_pairs={{4,0},{6,2},{8,4},{10,6},{12,8},{14,10},{16,12},{18,14},{20,16},{2... | collective-permute-start | bytes 393224 | tf_op jit(solution)/shard_map/ppermute | solution.py:485
  43.2 3.0 %own.1.done = f32[16,32,512]{2,1,0:T(8,128)S(1)} custom-call(f32[24,32,512]{2,1,0:T(8,128)S(1)} %get-tuple-element.22.field, f32[9,32,128]{2,1,0:T(8,128)S(1)} %get-tuple-element.23.wx, f32[9,32,128]{2,1,0:T(8,128)S(1)} %get-tuple-element.24.wy), custom_call_target="tpu_custom_call" | custom-call | tf_op jit(solution)/shard_map/own/pallas_call | solution.py:486
  46.2 4.2 %collective-permute-done.5.after = s16[4,32,512]{2,1,0:T(8,128)(2,1)S(1)} collective-permute-done((s16[4,32,512]{2,1,0:T(8,128)(2,1)S(1)}, s16[4,32,512]{2,1,0:T(8,128)(2,1)S(1)}, u32[]{:S(2)}, u32[]{:S(2)}) %collective-permute-start.5) | collective-permute-done | bytes 131104 | tf_op jit(solution)/shard_map/ppermute | solution.py:485
  50.4 0.0 collective-permute-done.4.before
  50.4 2.6 %rest.1 = (s16[16,4224]{1,0:T(8,128)(2,1)S(1)}, s16[16,4224]{1,0:T(8,128)(2,1)S(1)}) custom-call(f32[16,32,512]{2,1,0:T(8,128)S(1)} %own.1.done, s16[8,32,512]{2,1,0:T(8,128)(2,1)S(1)} %collective-permute-done.4.before, s16[4,32,512]{2,1,0:T(8,128)(2,1)S(1)} %collective-permute-done.5.after, f32[9,32,128]{2,1,0:T(8,128)S(1)} %get-tuple-element.23.wx, ...), custom_call_target="tpu_custom_call" | custom-call | tf_op jit(solution)/shard_map/rest/pallas_call | solution.py:495
  53.0 0.1 collective-permute-start.6
  53.1 1.5 %collective-permute-start.7 = (s16[16,4224]{1,0:T(8,128)(2,1)S(1)}, s16[16,4224]{1,0:T(8,128)(2,1)S(1)}, u32[]{:S(2)}, u32[]{:S(2)}) collective-permute-start(s16[16,4224]{1,0:T(8,128)(2,1)S(1)} %get-tuple-element.27.keep), channel_id=1, source_target_pairs={{0,1},{1,0},{2,3},{3,2},{4,5},{5,4},{6,7},{7,6},{8,9},{9,8},{10,11... | collective-permute-start | bytes 405512 | tf_op jit(solution)/shard_map/ppermute | solution.py:511
  54.6 0.0 collective-permute-done.6.near
  54.6 1.3 %collective-permute-start.8 = (s16[16,4224]{1,0:T(8,128)(2,1)S(1)}, s16[16,4224]{1,0:T(8,128)(2,1)S(1)}, u32[]{:S(2)}, u32[]{:S(2)}) collective-permute-start(s16[16,4224]{1,0:T(8,128)(2,1)S(1)} %collective-permute-done.6.near), channel_id=1, source_target_pairs={{0,1},{1,0},{2,3},{3,2},{4,5},{5,4},{6,7},{7,6},{8,9},{9,8},{10,11... | collective-permute-start | bytes 405512 | tf_op jit(solution)/shard_map/ppermute | solution.py:513
  55.9 3.7 %collective-permute-done.7.far = s16[16,4224]{1,0:T(8,128)(2,1)S(1)} collective-permute-done((s16[16,4224]{1,0:T(8,128)(2,1)S(1)}, s16[16,4224]{1,0:T(8,128)(2,1)S(1)}, u32[]{:S(2)}, u32[]{:S(2)}) %collective-permute-start.7) | collective-permute-done | bytes 135200 | tf_op jit(solution)/shard_map/ppermute | solution.py:511
  59.6 2.4 %collective-permute-done.8.far_near = s16[16,4224]{1,0:T(8,128)(2,1)S(1)} collective-permute-done((s16[16,4224]{1,0:T(8,128)(2,1)S(1)}, s16[16,4224]{1,0:T(8,128)(2,1)S(1)}, u32[]{:S(2)}, u32[]{:S(2)}) %collective-permute-start.8) | collective-permute-done | bytes 135200 | tf_op jit(solution)/shard_map/ppermute | solution.py:513
  62.0 1.1 %join.1 = f32[8,64,512]{2,1,0:T(8,128)} custom-call(s16[16,4224]{1,0:T(8,128)(2,1)S(1)} %get-tuple-element.27.keep, s16[16,4224]{1,0:T(8,128)(2,1)S(1)} %collective-permute-done.6.near, s16[16,4224]{1,0:T(8,128)(2,1)S(1)} %collective-permute-done.7.far, s16[16,4224]{1,0:T(8,128)(2,1)S(1)} %collective-permute-done.8.far_near), custom_call_target="tpu_custom_call" | custom-call | tf_op jit(solution)/shard_map/join/pallas_call | solution.py:514
  (4 shorter events, 0.0 us)
Async XLA Ops:
  0.0 12.0 %copy-start.1 = (s32[1,256]{1,0:T(1,128)S(1)}, s32[1,256]{1,0:T(1,128)}, u32[]{:S(2)}) copy-start(s32[1,256]{1,0:T(1,128)} %param.9) | copy-start | bytes 3076
  0.0 12.0 %copy-start = (f32[1,2,16,9]{2,1,3,0:T(2,128)S(1)}, f32[1,2,16,9]{2,1,3,0:T(2,128)}, u32[]{:S(2)}) copy-start(f32[1,2,16,9]{2,1,3,0:T(2,128)} %param.11) | copy-start | bytes 3460
  0.0 12.2 %copy-start.2 = (s32[1,64]{1,0:T(1,128)S(1)}, s32[1,64]{1,0:T(1,128)}, u32[]{:S(2)}) copy-start(s32[1,64]{1,0:T(1,128)} %param.10) | copy-start | bytes 772
  2.1 29.2 %all-to-all-start = ((bf16[32,2,8,512]{3,2,1,0:T(8,128)(2,1)}), bf16[32,2,8,512]{3,2,1,0:T(8,128)(2,1)S(1)}, u32[]{:S(2)}, u32[]{:S(2)}) async-start(bf16[32,2,8,512]{3,2,1,0:T(8,128)(2,1)} %bitcast.7), calls=%async_computation | async-start | bytes 1048576 | tf_op jit(solution)/shard_map/all_to_all | solution.py:422
  8.1 16.6 %collective-permute-start.2 = (s16[2,8,16,512]{3,2,1,0:T(8,128)(2,1)S(1)}, s16[2,8,16,512]{3,2,1,0:T(8,128)(2,1)S(1)}, u32[]{:S(2)}, u32[]{:S(2)}) collective-permute-start(s16[2,8,16,512]{3,2,1,0:T(8,128)(2,1)S(1)} %get-tuple-element.20), channel_id=1, source_target_pairs={{2,4},{4,2},{6,8},{8,6},{10,12},{12,10},{14,16},{16,14},{18,20},{2... | collective-permute-start | bytes 786440 | tf_op jit(solution)/shard_map/ppermute | solution.py:418
  12.3 12.5 %collective-permute-start = (f32[640]{0:T(1024)S(1)}, f32[640]{0:T(1024)S(1)}, u32[]{:S(2)}, u32[]{:S(2)}) collective-permute-start(f32[640]{0:T(1024)S(1)} %pad_maximum_fusion.1), channel_id=1, source_target_pairs={{0,1},{1,0},{2,3},{3,2},{4,5},{5,4},{6,7},{7,6},{8,9},{9,8},{10,11... | collective-permute-start | bytes 7688 | tf_op jit(solution)/shard_map/ppermute | solution.py:433
  13.7 11.1 %collective-permute-start.1 = (f32[8,16,512]{2,1,0:T(8,128)S(1)}, f32[8,16,512]{2,1,0:T(8,128)S(1)}, u32[]{:S(2)}, u32[]{:S(2)}) collective-permute-start(f32[8,16,512]{2,1,0:T(8,128)S(1)} %get-tuple-element.19), channel_id=1, source_target_pairs={{0,2},{2,0},{4,6},{6,4},{8,10},{10,8},{12,14},{14,12},{16,18},{18,... | collective-permute-start | bytes 786440 | tf_op jit(solution)/shard_map/ppermute | solution.py:421
  24.7 1.4 %collective-permute-start.3 = (s16[8,16,512]{2,1,0:T(8,128)(2,1)S(1)}, s16[8,16,512]{2,1,0:T(8,128)(2,1)S(1)}, u32[]{:S(2)}, u32[]{:S(2)}) collective-permute-start(s16[8,16,512]{2,1,0:T(8,128)(2,1)S(1)} %dynamic-slice_bitcast_fusion), channel_id=1, source_target_pairs={{0,2},{2,0},{4,6},{6,4},{8,10},{10,8},{12,14},{14,12},{16,18},{18,... | collective-permute-start | bytes 393224 | tf_op jit(solution)/shard_map/ppermute | solution.py:442
  36.5 14.0 %collective-permute-start.4 = (s16[8,32,512]{2,1,0:T(8,128)(2,1)S(1)}, s16[8,32,512]{2,1,0:T(8,128)(2,1)S(1)}, u32[]{:S(2)}, u32[]{:S(2)}) collective-permute-start(s16[8,32,512]{2,1,0:T(8,128)(2,1)S(1)} %get-tuple-element.25), channel_id=1, source_target_pairs={{0,4},{2,6},{4,8},{6,10},{8,12},{10,14},{12,16},{14,18},{16,20},{1... | collective-permute-start | bytes 786440 | tf_op jit(solution)/shard_map/ppermute | solution.py:484
  38.4 12.0 %collective-permute-start.5 = (s16[4,32,512]{2,1,0:T(8,128)(2,1)S(1)}, s16[4,32,512]{2,1,0:T(8,128)(2,1)S(1)}, u32[]{:S(2)}, u32[]{:S(2)}) collective-permute-start(s16[4,32,512]{2,1,0:T(8,128)(2,1)S(1)} %get-tuple-element.26), channel_id=1, source_target_pairs={{4,0},{6,2},{8,4},{10,6},{12,8},{14,10},{16,12},{18,14},{20,16},{2... | collective-permute-start | bytes 393224 | tf_op jit(solution)/shard_map/ppermute | solution.py:485
  53.0 1.6 %collective-permute-start.6 = (s16[16,4224]{1,0:T(8,128)(2,1)S(1)}, s16[16,4224]{1,0:T(8,128)(2,1)S(1)}, u32[]{:S(2)}, u32[]{:S(2)}) collective-permute-start(s16[16,4224]{1,0:T(8,128)(2,1)S(1)} %get-tuple-element.28), channel_id=1, source_target_pairs={{0,2},{2,0},{4,6},{6,4},{8,10},{10,8},{12,14},{14,12},{16,18},{18,... | collective-permute-start | bytes 405512 | tf_op jit(solution)/shard_map/ppermute | solution.py:512
  53.1 6.5 %collective-permute-start.7 = (s16[16,4224]{1,0:T(8,128)(2,1)S(1)}, s16[16,4224]{1,0:T(8,128)(2,1)S(1)}, u32[]{:S(2)}, u32[]{:S(2)}) collective-permute-start(s16[16,4224]{1,0:T(8,128)(2,1)S(1)} %get-tuple-element.27.keep), channel_id=1, source_target_pairs={{0,1},{1,0},{2,3},{3,2},{4,5},{5,4},{6,7},{7,6},{8,9},{9,8},{10,11... | collective-permute-start | bytes 405512 | tf_op jit(solution)/shard_map/ppermute | solution.py:511
  54.6 7.3 %collective-permute-start.8 = (s16[16,4224]{1,0:T(8,128)(2,1)S(1)}, s16[16,4224]{1,0:T(8,128)(2,1)S(1)}, u32[]{:S(2)}, u32[]{:S(2)}) collective-permute-start(s16[16,4224]{1,0:T(8,128)(2,1)S(1)} %collective-permute-done.6.near), channel_id=1, source_target_pairs={{0,1},{1,0},{2,3},{3,2},{4,5},{5,4},{6,7},{7,6},{8,9},{9,8},{10,11... | collective-permute-start | bytes 405512 | tf_op jit(solution)/shard_map/ppermute | solution.py:513

commit v4 on v3

--- a/solution.py
+++ b/solution.py
@@ -17,6 +17,7 @@
 TINY = 1e-35
 LANES = 128
 SUBLANES = 8
+UNROLL = 4
 GRANT = pltpu.CompilerParams(vmem_limit_bytes=12 << 20)
 VMEM = pl.BlockSpec(memory_space=pltpu.VMEM)
 HBM = pl.BlockSpec(memory_space=pl.ANY)
@@ -152,7 +153,7 @@
     lax.fori_loop(0, chips, one_chip, 0, unroll=2)
 
 
-def blur_body(layout, table, mine, partner, across, passed, inverse, wx, wy, field):
+def blur_body(layout, table, mine, partner, across, passed, inverse, wx, wy, cleared, field):
     views, part, cores, taps, kernels = (
         layout["views"], layout["part"], layout["cores"], layout["taps"], layout["kernels"])
     chip, core, view_here = position(cores)
@@ -185,6 +186,7 @@
             field[at : at + piece.shape[0], planes, :] = piece
             at += piece.shape[0]
     rows_out, planes, columns = inverse.shape
+    cleared[...] = jnp.zeros_like(cleared)
     own_rows = cores * layout["rows_dev"]
     lane = lax.broadcasted_iota(jnp.int32, (SUBLANES, LANES), 1)
 
@@ -199,10 +201,43 @@
     lax.fori_loop(0, rows_out, one_row, 0, unroll=2)
 
 
-def ratio_body(layout, table, arrived, inverse, field, upward, downward, placed, turned):
+def ratio_row(layout, placed, inverse, field, turned, row):
+    _, planes, columns = field.shape
+    radius = layout["taps"] // 2
+    block_width, pitch = layout["block_width"], layout["pitch"]
+    per_tile = LANES // block_width
+    groups = planes // per_tile
+    lane = lax.broadcasted_iota(jnp.int32, (groups, LANES), 1)
+    for col in range(columns // LANES):
+        tiles = [
+            placed[pl.ds((col * per_tile + k) * groups * pitch + row, groups, stride=pitch), :]
+            for k in range(per_tile)
+        ]
+        step = per_tile // 2
+        while step:
+            width = step * block_width
+            first_half = (lane // width) % 2 == 0
+            mixed = list(tiles)
+            for k in range(per_tile):
+                if (k // step) % 2 == 0:
+                    a, b = tiles[k], tiles[k + step]
+                    mixed[k] = jnp.where(first_half, a, pltpu.roll(b, width, 1))
+                    mixed[k + step] = jnp.where(first_half, pltpu.roll(a, LANES - width, 1), b)
+            tiles = mixed
+            step //= 2
+        for k, value in enumerate(tiles):
+            turned[pl.ds(col * planes + k, groups, stride=per_tile), :] = value
+    for col in range(columns // LANES):
+        for group in range(planes // SUBLANES):
+            measured = turned[pl.ds(col * planes + group * SUBLANES, SUBLANES), :]
+            planes_at = pl.ds(group * SUBLANES, SUBLANES)
+            field[row + radius, planes_at, pl.ds(col * LANES, LANES)] = (
+                measured * tile(inverse, row, group, col))
+
+
+def ratio_body(layout, table, arrived, inverse, cleared, placed, field, upward, downward, turned):
     views, cores, slots, taps = layout["views"], layout["cores"], layout["slots"], layout["taps"]
     bricks, per_holder, rows_dev = layout["bricks"], layout["per_holder"], layout["rows_dev"]
-    rows_out, planes, columns = inverse.shape
     radius = taps // 2
     per_tile = LANES // layout["block_width"]
     depth_tiles = layout["part"] // per_tile
@@ -210,7 +245,6 @@
     pitch = layout["pitch"]
     chip, _, _ = position(cores)
     first_row = chip * cores * rows_dev
-    placed[...] = jnp.zeros_like(placed)
 
     def one_source(source, carry):
         adds = []
@@ -232,53 +266,30 @@
             placed[pl.ds(begin, rows_dev), :] = old + value
         return carry
 
-    lax.fori_loop(0, bricks, one_source, 0)
-
-    lane = lax.broadcasted_iota(jnp.int32, (groups, LANES), 1)
+    lax.fori_loop(0, bricks, one_source, 0, unroll=UNROLL)
+
     own_rows = cores * rows_dev
-
-    def one_row(row, carry):
-        for col in range(columns // LANES):
-            tiles = [
-                placed[pl.ds((col * per_tile + k) * groups * pitch + row, groups, stride=pitch), :]
-                for k in range(per_tile)
-            ]
-            step = per_tile // 2
-            while step:
-                width = step * layout["block_width"]
-                first_half = (lane // width) % 2 == 0
-                mixed = list(tiles)
-                for k in range(per_tile):
-                    if (k // step) % 2 == 0:
-                        a, b = tiles[k], tiles[k + step]
-                        mixed[k] = jnp.where(first_half, a, pltpu.roll(b, width, 1))
-                        mixed[k + step] = jnp.where(first_half, pltpu.roll(a, LANES - width, 1), b)
-                tiles = mixed
-                step //= 2
-            for k, value in enumerate(tiles):
-                turned[pl.ds(col * planes + k, groups, stride=per_tile), :] = value
-        for col in range(columns // LANES):
-            for group in range(planes // SUBLANES):
-                measured = turned[pl.ds(col * planes + group * SUBLANES, SUBLANES), :]
-                planes_at = pl.ds(group * SUBLANES, SUBLANES)
-                field[row + radius, planes_at, pl.ds(col * LANES, LANES)] = (
-                    measured * tile(inverse, row, group, col))
+    for target, begin in ((upward, own_rows - radius), (downward, 0)):
+
+        def one_row(row, carry):
+            ratio_row(layout, placed, inverse, field, turned, row + begin)
+            target[row] = encode_ratio(field[row + begin + radius], bricks, taps)
+            return carry
+
+        lax.fori_loop(0, target.shape[0], one_row, 0, unroll=2)
+
+
+def own_body(layout, placed, inverse, edges, wx, wy, field, done, turned):
+    rows, planes, columns = done.shape
+    radius = layout["taps"] // 2
+    lane = lax.broadcasted_iota(jnp.int32, (SUBLANES, LANES), 1)
+    field[0:radius] = jnp.zeros((radius, planes, columns), jnp.float32)
+
+    def inner_row(row, carry):
+        ratio_row(layout, placed, inverse, field, turned, row)
         return carry
 
-    lax.fori_loop(0, rows_out, one_row, 0)
-    field[0:radius] = jnp.zeros((radius, planes, columns), jnp.float32)
-    for target, begin in ((upward, own_rows), (downward, radius)):
-
-        def one_message_row(row, carry):
-            target[row] = encode_ratio(field[row + begin], bricks, taps)
-            return carry
-
-        lax.fori_loop(0, target.shape[0], one_message_row, 0)
-
-
-def own_body(layout, field, wx, wy, done):
-    rows, planes, columns = done.shape
-    lane = lax.broadcasted_iota(jnp.int32, (SUBLANES, LANES), 1)
+    lax.fori_loop(radius, rows - radius, inner_row, 0)
 
     def one_row(row, carry):
         for group in range(planes // SUBLANES):
@@ -290,92 +301,102 @@
     lax.fori_loop(0, rows, one_row, 0, unroll=2)
 
 
-def rest_body(layout, done, before, after, wx, wy, mine, partner, keep, send, ahead, behind, total):
+def rest_body(layout, flip, done, before, after, wx, wy, source, target, reach, total):
     views, part, cores, taps = layout["views"], layout["part"], layout["cores"], layout["taps"]
-    bricks = layout["bricks"]
-    own_rows, planes, columns = done.shape
+    bricks, rows_dev = layout["bricks"], layout["rows_dev"]
+    _, planes, columns = done.shape
     radius = taps // 2
-    rows_dev = own_rows // cores
     chip, core, _ = position(cores)
-    has_before = (chip > 0).astype(jnp.float32)
-    has_after = (chip < bricks // cores - 1).astype(jnp.float32)
-    for target, source, mask in ((ahead, before, has_before), (behind, after, has_after)):
-
-        def one_message_row(row, carry):
-            target[row] = decode_ratio(source[row], bricks, taps) * mask
-            return carry
-
-        lax.fori_loop(0, source.shape[0], one_message_row, 0)
     lane = lax.broadcasted_iota(jnp.int32, (SUBLANES, LANES), 1)
     cols = columns // LANES
-    reached = list(range(2 * radius)) + list(range(own_rows - radius, own_rows))
-
-    def one_group(group, carry):
-        planes_at = pl.ds(pl.multiple_of(group * SUBLANES, SUBLANES), SUBLANES)
-        for row in reached:
-            sums = None
-            for tap in range(taps):
-                at = row + 2 * radius - tap
-                if at < 2 * radius:
-                    source = ahead
-                elif at >= own_rows + radius:
-                    source, at = behind, at - own_rows - radius
-                else:
-                    continue
-                weight = wx[tap, planes_at, :]
-                terms = [weight * source[at, planes_at, pl.ds(col * LANES, LANES)] for col in range(cols)]
-                sums = terms if sums is None else [a + b for a, b in zip(sums, terms)]
-            result = [done[row, planes_at, pl.ds(col * LANES, LANES)] for col in range(cols)]
-            for tap in range(taps):
-                weight = wy[tap, planes_at, :]
-                moved = shifted(sums, lane, radius - tap)
-                result = [a + weight * m for a, m in zip(result, moved)]
-            for col, value in enumerate(result):
-                total[row, planes_at, pl.ds(col * LANES, LANES)] = value
-        for row in range(own_rows):
-            if row not in reached:
-                total[row, planes_at, :] = done[row, planes_at, :]
-        return carry
-
-    lax.fori_loop(0, planes // SUBLANES, one_group, 0)
-
+
+    def add_received(half):
+        message, there = (
+            (after, chip < bricks // cores - 1) if half else (before, chip > 0))
+        mask = there.astype(jnp.float32)
+
+        def one_message_row(row, carry):
+            reach[row] = decode_ratio(message[row], bricks, taps) * mask
+            return carry
+
+        lax.fori_loop(0, message.shape[0], one_message_row, 0, unroll=UNROLL)
+        first = rows_dev if half else -radius
+
+        def one_group(group, carry):
+            planes_at = pl.ds(pl.multiple_of(group * SUBLANES, SUBLANES), SUBLANES)
+            for row in range(rows_dev):
+                result = [
+                    done[half * rows_dev + row, planes_at, pl.ds(col * LANES, LANES)]
+                    for col in range(cols)
+                ]
+                sums = None
+                for tap in range(taps):
+                    at = row + radius - tap - first
+                    if not 0 <= at < message.shape[0]:
+                        continue
+                    weight = wx[tap, planes_at, :]
+                    terms = [
+                        weight * reach[at, planes_at, pl.ds(col * LANES, LANES)] for col in range(cols)]
+                    sums = terms if sums is None else [a + b for a, b in zip(sums, terms)]
+                for tap in range(taps if sums else 0):
+                    weight = wy[tap, planes_at, :]
+                    moved = shifted(sums, lane, radius - tap)
+                    result = [a + weight * m for a, m in zip(result, moved)]
+                for col, value in enumerate(result):
+                    total[row, planes_at, pl.ds(col * LANES, LANES)] = value
+            return carry
+
+        lax.fori_loop(0, planes // SUBLANES, one_group, 0)
+
+    this = 1 - core if flip else core
+    for half in range(cores):
+        pl.when(this == half)(functools.partial(add_received, half))
     wide = lax.broadcasted_iota(jnp.int32, (part, LANES), 1)
-
-    def finish(half, source, target):
-        def one_row(row, levels):
-            at = half * rows_dev + row
-            value = source[row]
-            for view in range(views):
-                value = value * total[at, view * part : (view + 1) * part, :]
-            begin = row * columns if isinstance(row, int) else pl.multiple_of(row * columns, LANES)
-            target[:, pl.ds(begin, columns)], level = encode_rows(value)
-            return jnp.where(wide == row, level, levels)
-
-        levels = lax.fori_loop(
-            0, rows_dev, one_row, jnp.zeros((part, LANES), jnp.float32), unroll=True)
-        target[:, rows_dev * columns :] = levels.astype(jnp.int32).astype(jnp.int16)
-
-    finish(core, mine, keep)
-    finish(1 - core, partner, send)
-
-
-def join_body(keep, near, far, far_near, out, pieces, sems):
+    levels = jnp.zeros((part, LANES), jnp.float32)
+    for row in range(rows_dev):
+        value = source[row]
+        for view in range(views):
+            value = value * total[row, view * part : (view + 1) * part, :]
+        target[:, row * columns : (row + 1) * columns], level = encode_rows(value)
+        levels = jnp.where(wide == row, level, levels)
+    target[:, rows_dev * columns :] = levels.astype(jnp.int32).astype(jnp.int16)
+
+
+def join_body(places, *refs):
     _, core, view = position(2)
+    count = len(places)
+    sources, (out, held, sems) = refs[:count], refs[-3:]
     rows, columns = out.shape[0], out.shape[2]
-    part = keep.shape[0]
+    part = sources[0].shape[0]
     copies = []
-    for index, (v, c, piece) in enumerate((
-        (view, core, keep), (view, 1 - core, near), (1 - view, core, far), (1 - view, 1 - core, far_near))):
+    for index, (piece, (turn, flip)) in enumerate(zip(sources, places)):
+        v = 1 - view if turn else view
+        c = 1 - core if flip else core
         levels = piece[:, rows * columns :]
         for row in range(rows):
-            pieces[index, row] = decode_row(
-                piece[:, row * columns : (row + 1) * columns], levels, row)
+            held[index, row] = decode_row(piece[:, row * columns : (row + 1) * columns], levels, row)
         begin = pl.multiple_of((v * 2 + c) * part, part)
         copies.append(pltpu.make_async_copy(
-            pieces.at[index], out.at[:, pl.ds(begin, part), :], sems.at[index]))
+            held.at[index], out.at[:, pl.ds(begin, part), :], sems.at[index]))
         copies[-1].start()
     for copy in copies:
         copy.wait()
+
+
+def join(shape, part, places, pieces, out=None):
+    rows, _, columns = shape
+    count = len(pieces)
+    return pl.pallas_call(
+        functools.partial(join_body, places),
+        out_shape=jax.ShapeDtypeStruct(shape, jnp.float32),
+        in_specs=[VMEM] * count + ([] if out is None else [HBM]),
+        out_specs=HBM,
+        input_output_aliases={} if out is None else {count: 0},
+        scratch_shapes=[
+            pltpu.VMEM((count, rows, part, columns), jnp.float32), pltpu.SemaphoreType.DMA((count,))],
+        compiler_params=GRANT,
+        name="join",
+    )(*near_core(*pieces), *([] if out is None else [out]))
 
 
 def shards(estimate, camera_blocks, block_lists, block_offsets, psf_index, psf_bank):
@@ -449,79 +470,80 @@
 
     own_rows = cores * rows_dev
     rows_all = own_rows + radius
-    inverse, wx, wy = pl.pallas_call(
+    groups = planes * block_width // LANES
+    placing = pltpu.VMEM(((per_holder + 1) * groups * layout["pitch"], LANES), f32)
+    inverse, wx, wy, cleared = pl.pallas_call(
         functools.partial(blur_body, layout),
         out_shape=[
             pltpu.VMEM((rows_all, planes, columns), f32),
             pltpu.VMEM((taps, planes, LANES), f32),
             pltpu.VMEM((taps, planes, LANES), f32),
+            placing,
         ],
         in_specs=[SMEM] + [VMEM] * 4,
-        out_specs=[VMEM] * 3,
+        out_specs=[VMEM] * 4,
         scratch_shapes=[pltpu.VMEM((rows_all + 2 * radius, planes, columns), f32)],
         compiler_params=GRANT,
         name="blur",
     )(table, *near_core(mine, partner, across, passed))
 
-    groups = planes * block_width // LANES
-    field, upward, downward = pl.pallas_call(
+    edged = pltpu.VMEM((rows_all + radius, planes, columns), f32)
+    turning = pltpu.VMEM((columns // LANES * planes, LANES), f32)
+    placed, field, upward, downward = pl.pallas_call(
         functools.partial(ratio_body, layout),
         out_shape=[
-            pltpu.VMEM((rows_all + radius, planes, columns), f32),
+            placing,
+            edged,
             pltpu.VMEM((2 * radius, planes, columns), jnp.int16),
             pltpu.VMEM((radius, planes, columns), jnp.int16),
         ],
-        in_specs=[SMEM, VMEM, VMEM],
-        out_specs=[VMEM] * 3,
-        scratch_shapes=[
-            pltpu.VMEM(((per_holder + 1) * groups * layout["pitch"], LANES), f32),
-            pltpu.VMEM((columns // LANES * planes, LANES), f32),
-        ],
+        in_specs=[SMEM] + [VMEM] * 3,
+        out_specs=[VMEM] * 4,
+        input_output_aliases={3: 0},
+        scratch_shapes=[turning],
         compiler_params=GRANT,
         name="ratio",
-    )(table, *near_core(arrived, inverse))
+    )(table, *near_core(arrived, inverse, cleared))
 
     before = lax.ppermute(upward, "brick", up)
     after = lax.ppermute(downward, "brick", down)
-    done = pl.pallas_call(
+    _, done = pl.pallas_call(
         functools.partial(own_body, layout),
-        out_shape=pltpu.VMEM((own_rows, planes, columns), f32),
-        in_specs=[VMEM] * 3,
-        out_specs=VMEM,
+        out_shape=[edged, pltpu.VMEM((own_rows, planes, columns), f32)],
+        in_specs=[VMEM] * 5,
+        out_specs=[VMEM] * 2,
+        input_output_aliases={2: 0},
+        scratch_shapes=[turning],
         compiler_params=GRANT,
         name="own",
-    )(*near_core(field, wx, wy))
-    piece = pltpu.VMEM((part, rows_dev * columns + LANES), jnp.int16)
-    keep, send = pl.pallas_call(
-        functools.partial(rest_body, layout),
-        out_shape=[piece, piece],
-        in_specs=[VMEM] * 7,
-        out_specs=[VMEM] * 2,
-        scratch_shapes=[
-            pltpu.VMEM((2 * radius, planes, columns), f32),
-            pltpu.VMEM((radius, planes, columns), f32),
-            pltpu.VMEM((own_rows, planes, columns), f32),
-        ],
-        compiler_params=GRANT,
-        name="rest",
-    )(*near_core(done, before, after, wx, wy, mine, partner))
+    )(*near_core(placed, inverse, field, wx, wy))
+
+    def finished(flip, source):
+        return pl.pallas_call(
+            functools.partial(rest_body, layout, flip),
+            out_shape=pltpu.VMEM((part, rows_dev * columns + LANES), jnp.int16),
+            in_specs=[VMEM] * 6,
+            out_specs=VMEM,
+            scratch_shapes=[
+                pltpu.VMEM((2 * radius, planes, columns), f32),
+                pltpu.VMEM((rows_dev, planes, columns), f32),
+            ],
+            compiler_params=GRANT,
+            name="rest",
+        )(*near_core(done, before, after, wx, wy, source))
 
     if views == 2:
         turn = [(0, 1), (1, 0)]
+        keep = finished(False, mine)
         far = lax.ppermute(keep, "view", turn)
+        send = finished(True, partner)
         near = lax.ppermute(send, "brick", swap)
         far_near = lax.ppermute(near, "view", turn)
-        return pl.pallas_call(
-            join_body,
-            out_shape=jax.ShapeDtypeStruct(estimate.shape, f32),
-            in_specs=[VMEM] * 4,
-            out_specs=HBM,
-            scratch_shapes=[
-                pltpu.VMEM((4, rows_dev, part, columns), f32), pltpu.SemaphoreType.DMA((4,))],
-            compiler_params=GRANT,
-            name="join",
-        )(*near_core(keep, near, far, far_near))
-    near = lax.ppermute(send, "brick", swap)
+        out = join(estimate.shape, part, ((False, False), (False, True)), (keep, near))
+        out = join(estimate.shape, part, ((True, False),), (far,), out)
+        return join(estimate.shape, part, ((True, True),), (far_near,), out)
+    keep = finished(False, mine)
+    near = lax.ppermute(finished(True, partner), "brick", swap)
     both = jnp.stack([jnp.where(core == 0, keep, near), jnp.where(core == 0, near, keep)])
     coded = lax.all_gather(both, "view").reshape((-1,) + keep.shape)
     rows = [

time: 63.4 us -> 64.7 us (1.021)
  local copies, waits for them, and re-layouts: 0.3 us -> 4.54 us
  waiting for transfers between devices: 22.3 us -> 18.1 us
  Pallas kernels: 19.2 us -> 20.2 us
    unnamed x7 -> x23, local copies, waits for them, and re-layouts: 0.1 us -> 4.35 us
    ppermute x1, waiting for transfers between devices: 2.36 us -> 0.63 us  [shards(): far_near = lax.ppermute(near, 'view', turn)]
    ppermute x1, waiting for transfers between devices: 4.24 us -> 2.89 us  [shards(): after = lax.ppermute(downward, 'brick', down)]
    pallas_call x4 -> x7, Pallas kernels: 11.8 us -> 12.6 us  [the longest x1 4.29 us: shards(): pl.pallas_call(functools.partial(own_body, layout), out_shape=[edged, plt...]
    ppermute x1, starting transfers between devices: 1.27 us -> 0.56 us  [shards(): far_near = lax.ppermute(near, 'view', turn)]
    ppermute x1, waiting for transfers between devices: 1.22 us -> 0.51 us  [shards(): lax.ppermute(lax.dynamic_index_in_dim(across, 1 - core, 0, keepdims=False...]
    ppermute x1, starting transfers between devices: 0.1 us -> 0.77 us  [shards(): near = lax.ppermute(send, 'brick', swap)]
  transfers between devices with their start and end apart: 10 -> 10, of which waited for: 5 -> 5; matrix products, arithmetic and copies ran while one was open for 2% -> 2% of each run, Pallas kernels for 13% -> 21%
where the time goes in v4:
time: 64.7 us; the launch traced here: 64.3 us
  starting transfers between devices  20.4 us (32%)
  Pallas kernels  20.2 us (31%)
  waiting for transfers between devices  18.1 us (28%)
  local copies, waits for them, and re-layouts  4.54 us (7%)
  other arithmetic  0.86 us (1%)
    ppermute x1, waiting for transfers between devices, shards(): lax.ppermute(edges, 'brick', [(i, j) for i in range(bricks) for j in [i +...  10.7 us
    all_to_all x1, starting transfers between devices, shards(): arrived = lax.all_to_all(packed, ('brick', 'view'), 0, 0, tiled=True)  5.99 us
    pallas_call x1, Pallas kernels, shards(): pl.pallas_call(functools.partial(blur_body, layout), out_shape=[pltpu.VME...  5.48 us
    ppermute x1, starting transfers between devices, shards(): after = lax.ppermute(downward, 'brick', down)  4.82 us
    unnamed x23, local copies, waits for them, and re-layouts  4.35 us
    pallas_call x1, Pallas kernels, shards(): pl.pallas_call(functools.partial(own_body, layout), out_shape=[edged, plt...  4.29 us
    ppermute x1, waiting for transfers between devices, shards(): far = lax.ppermute(keep, 'view', turn)  3.36 us
    ppermute x1, starting transfers between devices, shards(): lax.ppermute(edges, 'brick', [(i, j) for i in range(bricks) for j in [i +...  3.09 us
  transfers between devices with their start and end apart: 10, of which 5 were waited for; matrix products, arithmetic and copies ran while one was open for 2% of the time, Pallas kernels for 21%

profile of v4, /device:TPU:16, one launch (start us, length us, event | category | flops | bytes accessed | tf_op | source)
XLA Modules:
  0.0 64.3 jit_solution(5462279081147218928)
XLA Ops:
  0.0 0.0 copy-start.9
  0.0 0.0 copy-start.8
  0.0 0.0 copy-start.10
  0.0 2.1 %pack.1 = (bf16[8,2,2,2,8,512]{5,4,3,2,1,0:T(8,128)(2,1)}, s16[2,8,16,512]{3,2,1,0:T(8,128)(2,1)S(1)}, f32[8,16,512]{2,1,0:T(8,128)S(1)}, f32[8,16,512]{2,1,0:T(8,128)S(1)}) custom-call(s32[16,2,16]{2,1,0:T(2,128)} %bitcast.17, bf16[16,8,2048]{2,1,0:T(8,128)(2,1)} %bitcast.16, f32[8,64,512]{2,1,0:T(8,128)} %estimate.1), custom_call_target="tpu_custom_call" | custom-call | tf_op jit(solution)/shard_map/pack/pallas_call | solution.py:424
  2.1 0.0 copy-start
  2.1 0.7 %copy-done = f32[8,16,512]{2,1,0:T(8,128)} copy-done((f32[8,16,512]{2,1,0:T(8,128)}, f32[8,16,512]{2,1,0:T(8,128)S(1)}, u32[]{:S(2)}) %copy-start) | copy-done | bytes 262168
  2.8 6.0 %all-to-all-start = ((bf16[32,2,8,512]{3,2,1,0:T(8,128)(2,1)}), bf16[32,2,8,512]{3,2,1,0:T(8,128)(2,1)}, u32[]{:S(2)}, u32[]{:S(2)}) async-start(bf16[32,2,8,512]{3,2,1,0:T(8,128)(2,1)} %bitcast.7), calls=%async_computation | async-start | bytes 1048576 | tf_op jit(solution)/shard_map/all_to_all | solution.py:443
  8.8 3.1 %collective-permute-start.2 = (s16[2,8,16,512]{3,2,1,0:T(8,128)(2,1)S(1)}, s16[2,8,16,512]{3,2,1,0:T(8,128)(2,1)S(1)}, u32[]{:S(2)}, u32[]{:S(2)}) collective-permute-start(s16[2,8,16,512]{3,2,1,0:T(8,128)(2,1)S(1)} %get-tuple-element.21), channel_id=1, source_target_pairs={{2,4},{4,2},{6,8},{8,6},{10,12},{12,10},{14,16},{16,14},{18,20},{2... | collective-permute-start | bytes 786440 | tf_op jit(solution)/shard_map/ppermute | solution.py:439
  11.9 0.7 %convert_bitcast_fusion = f32[1,2,16]{2,1,0:T(2,128)S(1)} fusion(s32[1,16,16,2]{2,3,1,0:T(2,128)} %param.8, s32[]{:T(128)S(6)} %select_n.21), kind=kLoop, calls=%fused_computation.5 | loop fusion | flops 32 | bytes 260 | tf_op jit(solution)/shard_map/convert_element_type | solution.py:452
  12.6 0.1 convert_element_type.27
  12.7 0.0 copy-done.9
  12.7 0.0 copy-done.8
  12.7 0.1 copy.11
  12.8 0.1 reshape_squeeze.3
  12.9 0.0 copy-done.10
  12.9 0.1 pad_maximum_fusion.1
  13.0 1.5 %collective-permute-start = (f32[640]{0:T(1024)S(1)}, f32[640]{0:T(1024)S(1)}, u32[]{:S(2)}, u32[]{:S(2)}) collective-permute-start(f32[640]{0:T(1024)S(1)} %pad_maximum_fusion.1), channel_id=1, source_target_pairs={{0,1},{1,0},{2,3},{3,2},{4,5},{5,4},{6,7},{7,6},{8,9},{9,8},{10,11... | collective-permute-start | bytes 7688 | tf_op jit(solution)/shard_map/ppermute | solution.py:454
  14.5 0.1 collective-permute-start.1
  14.6 10.7 %collective-permute-done.2.across = s16[2,8,16,512]{3,2,1,0:T(8,128)(2,1)S(1)} collective-permute-done((s16[2,8,16,512]{3,2,1,0:T(8,128)(2,1)S(1)}, s16[2,8,16,512]{3,2,1,0:T(8,128)(2,1)S(1)}, u32[]{:S(2)}, u32[]{:S(2)}) %collective-permute-start.2) | collective-permute-done | bytes 262176 | tf_op jit(solution)/shard_map/ppermute | solution.py:439
  25.3 0.0 copy-start.6
  25.3 0.1 collective-permute-start.3
  25.4 0.0 collective-permute-done
  25.4 0.1 broadcast_select_fusion.1
  25.5 0.0 collective-permute-done.1.partner.source
  25.5 0.0 copy-start.3
  25.5 0.7 %copy-done.3 = f32[8,16,512]{2,1,0:T(8,128)} copy-done((f32[8,16,512]{2,1,0:T(8,128)}, f32[8,16,512]{2,1,0:T(8,128)S(1)}, u32[]{:S(2)}) %copy-start.3) | copy-done | bytes 262168
  26.2 0.5 collective-permute-done.3.passed
  26.8 0.0 copy-done.6
  26.8 0.0 copy-start.1
  26.8 0.9 %copy-done.1 = f32[8,16,512]{2,1,0:T(8,128)S(1)} copy-done((f32[8,16,512]{2,1,0:T(8,128)S(1)}, f32[8,16,512]{2,1,0:T(8,128)}, u32[]{:S(2)}) %copy-start.1) | copy-done | bytes 262168
  27.7 0.0 copy-start.4
  27.7 0.9 %copy-done.4 = f32[8,16,512]{2,1,0:T(8,128)S(1)} copy-done((f32[8,16,512]{2,1,0:T(8,128)S(1)}, f32[8,16,512]{2,1,0:T(8,128)}, u32[]{:S(2)}) %copy-start.4) | copy-done | bytes 262168
  28.7 0.0 copy-start.7
  28.7 0.9 %copy-done.7 = s16[2,8,16,512]{3,2,1,0:T(8,128)(2,1)S(1)} copy-done((s16[2,8,16,512]{3,2,1,0:T(8,128)(2,1)S(1)}, s16[2,8,16,512]{3,2,1,0:T(8,128)(2,1)}, u32[]{:S(2)}) %copy-start.7) | copy-done | bytes 262168
  29.6 5.5 %blur.1 = (f32[20,32,512]{2,1,0:T(8,128)S(1)}, f32[9,32,128]{2,1,0:T(8,128)S(1)}, f32[9,32,128]{2,1,0:T(8,128)S(1)}, f32[3400,128]{1,0:T(8,128)S(1)}) custom-call(f32[1280]{0:T(1024)S(1)} %pad_maximum_fusion.table, f32[8,16,512]{2,1,0:T(8,128)S(1)} %copy-done.1, f32[8,16,512]{2,1,0:T(8,128)S(1)} %copy-done.4, s16[2,8,16,512]{3,2,1,0:T(8,128)(2,1)S(1)} %copy-done.7, ...), custom_call_target="tpu_custom_call" | custom-call | tf_op jit(solution)/shard_map/blur/pallas_call | solution.py:475
  35.1 0.0 all-to-all-done.arrived
  35.1 2.9 %ratio.1 = (f32[3400,128]{1,0:T(8,128)S(1)}, f32[24,32,512]{2,1,0:T(8,128)S(1)}, s16[8,32,512]{2,1,0:T(8,128)(2,1)S(1)}, s16[4,32,512]{2,1,0:T(8,128)(2,1)S(1)}) custom-call(f32[1280]{0:T(1024)S(1)} %pad_maximum_fusion.table, bf16[32,2,8,512]{3,2,1,0:T(8,128)(2,1)} %all-to-all-done.arrived, ...), custom_call_target="tpu_custom_call", output_to_operand_aliasing={{0}: (3, {})} | custom-call | tf_op jit(solution)/shard_map/ratio/pallas_call | solution.py:492
  38.0 1.9 %collective-permute-start.4 = (s16[8,32,512]{2,1,0:T(8,128)(2,1)S(1)}, s16[8,32,512]{2,1,0:T(8,128)(2,1)S(1)}, u32[]{:S(2)}, u32[]{:S(2)}) collective-permute-start(s16[8,32,512]{2,1,0:T(8,128)(2,1)S(1)} %get-tuple-element.29), channel_id=1, source_target_pairs={{0,4},{2,6},{4,8},{6,10},{8,12},{10,14},{12,16},{14,18},{16,20},{1... | collective-permute-start | bytes 786440 | tf_op jit(solution)/shard_map/ppermute | solution.py:508
  39.9 4.8 %collective-permute-start.5 = (s16[4,32,512]{2,1,0:T(8,128)(2,1)S(1)}, s16[4,32,512]{2,1,0:T(8,128)(2,1)S(1)}, u32[]{:S(2)}, u32[]{:S(2)}) collective-permute-start(s16[4,32,512]{2,1,0:T(8,128)(2,1)S(1)} %get-tuple-element.30), channel_id=1, source_target_pairs={{4,0},{6,2},{8,4},{10,6},{12,8},{14,10},{16,12},{18,14},{20,16},{2... | collective-permute-start | bytes 393224 | tf_op jit(solution)/shard_map/ppermute | solution.py:509
  44.8 0.0 copy-start.5
  44.8 4.3 %own.1 = (f32[24,32,512]{2,1,0:T(8,128)S(1)}, f32[16,32,512]{2,1,0:T(8,128)S(1)}) custom-call(f32[3400,128]{1,0:T(8,128)S(1)} %get-tuple-element.24.placed, f32[20,32,512]{2,1,0:T(8,128)S(1)} %get-tuple-element.22.inverse, f32[24,32,512]{2,1,0:T(8,128)S(1)} %get-tuple-element.25.edges, ...), custom_call_target="tpu_custom_call", output_to_operand_aliasing={{0}: (2, {})} | custom-call | tf_op jit(solution)/shard_map/own/pallas_call | solution.py:510
  49.1 0.0 copy-start.2
  49.1 2.9 %collective-permute-done.5.after = s16[4,32,512]{2,1,0:T(8,128)(2,1)S(1)} collective-permute-done((s16[4,32,512]{2,1,0:T(8,128)(2,1)S(1)}, s16[4,32,512]{2,1,0:T(8,128)(2,1)S(1)}, u32[]{:S(2)}, u32[]{:S(2)}) %collective-permute-start.5) | collective-permute-done | bytes 131104 | tf_op jit(solution)/shard_map/ppermute | solution.py:509
  52.0 0.0 collective-permute-done.4.before
  52.0 0.0 copy-done.5
  52.0 1.1 %rest.2 = s16[16,4224]{1,0:T(8,128)(2,1)S(1)} custom-call(f32[16,32,512]{2,1,0:T(8,128)S(1)} %get-tuple-element.28.done, s16[8,32,512]{2,1,0:T(8,128)(2,1)S(1)} %collective-permute-done.4.before, s16[4,32,512]{2,1,0:T(8,128)(2,1)S(1)} %collective-permute-done.5.after, f32[9,32,128]{2,1,0:T(8,128)S(1)} %get-tuple-element.26.wx, ...), custom_call_target="tpu_custom_call" | custom-call | tf_op jit(solution)/shard_map/rest/pallas_call | solution.py:522
  53.1 0.8 %collective-permute-start.6 = (s16[16,4224]{1,0:T(8,128)(2,1)S(1)}, s16[16,4224]{1,0:T(8,128)(2,1)S(1)}, u32[]{:S(2)}, u32[]{:S(2)}) collective-permute-start(s16[16,4224]{1,0:T(8,128)(2,1)S(1)} %rest.2), channel_id=1, source_target_pairs={{0,2},{2,0},{4,6},{6,4},{8,10},{10,8},{12,14},{14,12},{16,18},{18,... | collective-permute-start | bytes 405512 | tf_op jit(solution)/shard_map/ppermute | solution.py:540
  53.9 0.0 copy-done.2
  53.9 1.8 %rest.3.refs_0_ = s16[16,4224]{1,0:T(8,128)(2,1)S(1)} custom-call(f32[16,32,512]{2,1,0:T(8,128)S(1)} %get-tuple-element.28.done, s16[8,32,512]{2,1,0:T(8,128)(2,1)S(1)} %collective-permute-done.4.before, s16[4,32,512]{2,1,0:T(8,128)(2,1)S(1)} %collective-permute-done.5.after, f32[9,32,128]{2,1,0:T(8,128)S(1)} %get-tuple-element.26.wx, ...), custom_call_target="tpu_custom_call" | custom-call | tf_op jit(solution)/shard_map/rest/pallas_call | solution.py:522
  55.7 1.5 %collective-permute-start.8 = (s16[16,4224]{1,0:T(8,128)(2,1)S(1)}, s16[16,4224]{1,0:T(8,128)(2,1)S(1)}, u32[]{:S(2)}, u32[]{:S(2)}) collective-permute-start(s16[16,4224]{1,0:T(8,128)(2,1)S(1)} %rest.3.refs_0_), channel_id=1, source_target_pairs={{0,1},{1,0},{2,3},{3,2},{4,5},{5,4},{6,7},{7,6},{8,9},{9,8},{10,11... | collective-permute-start | bytes 405512 | tf_op jit(solution)/shard_map/ppermute | solution.py:538
  57.2 0.0 collective-permute-done.6.refs_1_
  57.2 0.6 collective-permute-start.7
  57.8 0.9 %join.3.refs_1_ = f32[8,64,512]{2,1,0:T(8,128)} custom-call(s16[16,4224]{1,0:T(8,128)(2,1)S(1)} %rest.3.refs_0_, s16[16,4224]{1,0:T(8,128)(2,1)S(1)} %collective-permute-done.6.refs_1_), custom_call_target="tpu_custom_call" | custom-call | tf_op jit(solution)/shard_map/join/pallas_call | solution.py:389
  58.7 3.4 %collective-permute-done.8.refs_0_ = s16[16,4224]{1,0:T(8,128)(2,1)S(1)} collective-permute-done((s16[16,4224]{1,0:T(8,128)(2,1)S(1)}, s16[16,4224]{1,0:T(8,128)(2,1)S(1)}, u32[]{:S(2)}, u32[]{:S(2)}) %collective-permute-start.8) | collective-permute-done | bytes 135200 | tf_op jit(solution)/shard_map/ppermute | solution.py:538
  62.1 0.8 %join.4.refs_1_ = f32[8,64,512]{2,1,0:T(8,128)} custom-call(s16[16,4224]{1,0:T(8,128)(2,1)S(1)} %collective-permute-done.8.refs_0_, f32[8,64,512]{2,1,0:T(8,128)} %join.3.refs_1_), custom_call_target="tpu_custom_call", output_to_operand_aliasing={{}: (1, {})} | custom-call | tf_op jit(solution)/shard_map/join/pallas_call | solution.py:389
  62.9 0.6 collective-permute-done.7.refs_0_
  63.5 0.8 %join.5 = f32[8,64,512]{2,1,0:T(8,128)} custom-call(s16[16,4224]{1,0:T(8,128)(2,1)S(1)} %collective-permute-done.7.refs_0_, f32[8,64,512]{2,1,0:T(8,128)} %join.4.refs_1_), custom_call_target="tpu_custom_call", output_to_operand_aliasing={{}: (1, {})} | custom-call | tf_op jit(solution)/shard_map/join/pallas_call | solution.py:389
  (4 shorter events, 0.0 us)
Async XLA Ops:
  0.0 12.7 %copy-start.9 = (s32[1,256]{1,0:T(1,128)S(1)}, s32[1,256]{1,0:T(1,128)}, u32[]{:S(2)}) copy-start(s32[1,256]{1,0:T(1,128)} %param.9) | copy-start | bytes 3076
  0.0 12.7 %copy-start.8 = (f32[1,2,16,9]{2,1,3,0:T(2,128)S(1)}, f32[1,2,16,9]{2,1,3,0:T(2,128)}, u32[]{:S(2)}) copy-start(f32[1,2,16,9]{2,1,3,0:T(2,128)} %param.11) | copy-start | bytes 3460
  0.0 12.9 %copy-start.10 = (s32[1,64]{1,0:T(1,128)S(1)}, s32[1,64]{1,0:T(1,128)}, u32[]{:S(2)}) copy-start(s32[1,64]{1,0:T(1,128)} %param.10) | copy-start | bytes 772
  2.1 0.7 %copy-start = (f32[8,16,512]{2,1,0:T(8,128)}, f32[8,16,512]{2,1,0:T(8,128)S(1)}, u32[]{:S(2)}) copy-start(f32[8,16,512]{2,1,0:T(8,128)S(1)} %get-tuple-element.19.mine.source) | copy-start | bytes 786436
  2.8 32.3 %all-to-all-start = ((bf16[32,2,8,512]{3,2,1,0:T(8,128)(2,1)}), bf16[32,2,8,512]{3,2,1,0:T(8,128)(2,1)}, u32[]{:S(2)}, u32[]{:S(2)}) async-start(bf16[32,2,8,512]{3,2,1,0:T(8,128)(2,1)} %bitcast.7), calls=%async_computation | async-start | bytes 1048576 | tf_op jit(solution)/shard_map/all_to_all | solution.py:443
  8.8 16.5 %collective-permute-start.2 = (s16[2,8,16,512]{3,2,1,0:T(8,128)(2,1)S(1)}, s16[2,8,16,512]{3,2,1,0:T(8,128)(2,1)S(1)}, u32[]{:S(2)}, u32[]{:S(2)}) collective-permute-start(s16[2,8,16,512]{3,2,1,0:T(8,128)(2,1)S(1)} %get-tuple-element.21), channel_id=1, source_target_pairs={{2,4},{4,2},{6,8},{8,6},{10,12},{12,10},{14,16},{16,14},{18,20},{2... | collective-permute-start | bytes 786440 | tf_op jit(solution)/shard_map/ppermute | solution.py:439
  13.0 12.4 %collective-permute-start = (f32[640]{0:T(1024)S(1)}, f32[640]{0:T(1024)S(1)}, u32[]{:S(2)}, u32[]{:S(2)}) collective-permute-start(f32[640]{0:T(1024)S(1)} %pad_maximum_fusion.1), channel_id=1, source_target_pairs={{0,1},{1,0},{2,3},{3,2},{4,5},{5,4},{6,7},{7,6},{8,9},{9,8},{10,11... | collective-permute-start | bytes 7688 | tf_op jit(solution)/shard_map/ppermute | solution.py:454
  14.5 11.1 %collective-permute-start.1 = (f32[8,16,512]{2,1,0:T(8,128)S(1)}, f32[8,16,512]{2,1,0:T(8,128)S(1)}, u32[]{:S(2)}, u32[]{:S(2)}) collective-permute-start(f32[8,16,512]{2,1,0:T(8,128)S(1)} %get-tuple-element.20), channel_id=1, source_target_pairs={{0,2},{2,0},{4,6},{6,4},{8,10},{10,8},{12,14},{14,12},{16,18},{18,... | collective-permute-start | bytes 786440 | tf_op jit(solution)/shard_map/ppermute | solution.py:442
  25.3 1.4 %copy-start.6 = (s16[2,8,16,512]{3,2,1,0:T(8,128)(2,1)}, s16[2,8,16,512]{3,2,1,0:T(8,128)(2,1)S(1)}, u32[]{:S(2)}) copy-start(s16[2,8,16,512]{3,2,1,0:T(8,128)(2,1)S(1)} %collective-permute-done.2.across) | copy-start | bytes 786436
  25.3 1.4 %collective-permute-start.3 = (s16[8,16,512]{2,1,0:T(8,128)(2,1)S(1)}, s16[8,16,512]{2,1,0:T(8,128)(2,1)S(1)}, u32[]{:S(2)}, u32[]{:S(2)}) collective-permute-start(s16[8,16,512]{2,1,0:T(8,128)(2,1)S(1)} %dynamic-slice_bitcast_fusion), channel_id=1, source_target_pairs={{0,2},{2,0},{4,6},{6,4},{8,10},{10,8},{12,14},{14,12},{16,18},{18,... | collective-permute-start | bytes 393224 | tf_op jit(solution)/shard_map/ppermute | solution.py:463
  25.5 0.7 %copy-start.3 = (f32[8,16,512]{2,1,0:T(8,128)}, f32[8,16,512]{2,1,0:T(8,128)S(1)}, u32[]{:S(2)}) copy-start(f32[8,16,512]{2,1,0:T(8,128)S(1)} %collective-permute-done.1.partner.source) | copy-start | bytes 786436
  26.8 1.0 %copy-start.1 = (f32[8,16,512]{2,1,0:T(8,128)S(1)}, f32[8,16,512]{2,1,0:T(8,128)}, u32[]{:S(2)}) copy-start(f32[8,16,512]{2,1,0:T(8,128)} %copy-done) | copy-start | bytes 786436
  27.7 0.9 %copy-start.4 = (f32[8,16,512]{2,1,0:T(8,128)S(1)}, f32[8,16,512]{2,1,0:T(8,128)}, u32[]{:S(2)}) copy-start(f32[8,16,512]{2,1,0:T(8,128)} %copy-done.3) | copy-start | bytes 786436
  28.7 0.9 %copy-start.7 = (s16[2,8,16,512]{3,2,1,0:T(8,128)(2,1)S(1)}, s16[2,8,16,512]{3,2,1,0:T(8,128)(2,1)}, u32[]{:S(2)}) copy-start(s16[2,8,16,512]{3,2,1,0:T(8,128)(2,1)} %copy-done.6) | copy-start | bytes 786436
  38.0 14.0 %collective-permute-start.4 = (s16[8,32,512]{2,1,0:T(8,128)(2,1)S(1)}, s16[8,32,512]{2,1,0:T(8,128)(2,1)S(1)}, u32[]{:S(2)}, u32[]{:S(2)}) collective-permute-start(s16[8,32,512]{2,1,0:T(8,128)(2,1)S(1)} %get-tuple-element.29), channel_id=1, source_target_pairs={{0,4},{2,6},{4,8},{6,10},{8,12},{10,14},{12,16},{14,18},{16,20},{1... | collective-permute-start | bytes 786440 | tf_op jit(solution)/shard_map/ppermute | solution.py:508
  39.9 12.0 %collective-permute-start.5 = (s16[4,32,512]{2,1,0:T(8,128)(2,1)S(1)}, s16[4,32,512]{2,1,0:T(8,128)(2,1)S(1)}, u32[]{:S(2)}, u32[]{:S(2)}) collective-permute-start(s16[4,32,512]{2,1,0:T(8,128)(2,1)S(1)} %get-tuple-element.30), channel_id=1, source_target_pairs={{4,0},{6,2},{8,4},{10,6},{12,8},{14,10},{16,12},{18,14},{20,16},{2... | collective-permute-start | bytes 393224 | tf_op jit(solution)/shard_map/ppermute | solution.py:509
  44.8 7.2 %copy-start.5 = (f32[8,16,512]{2,1,0:T(8,128)S(1)}, f32[8,16,512]{2,1,0:T(8,128)}, u32[]{:S(2)}) copy-start(f32[8,16,512]{2,1,0:T(8,128)} %copy-done.3) | copy-start | bytes 786436
  49.1 4.8 %copy-start.2 = (f32[8,16,512]{2,1,0:T(8,128)S(1)}, f32[8,16,512]{2,1,0:T(8,128)}, u32[]{:S(2)}) copy-start(f32[8,16,512]{2,1,0:T(8,128)} %copy-done) | copy-start | bytes 786436
  53.1 4.1 %collective-permute-start.6 = (s16[16,4224]{1,0:T(8,128)(2,1)S(1)}, s16[16,4224]{1,0:T(8,128)(2,1)S(1)}, u32[]{:S(2)}, u32[]{:S(2)}) collective-permute-start(s16[16,4224]{1,0:T(8,128)(2,1)S(1)} %rest.2), channel_id=1, source_target_pairs={{0,2},{2,0},{4,6},{6,4},{8,10},{10,8},{12,14},{14,12},{16,18},{18,... | collective-permute-start | bytes 405512 | tf_op jit(solution)/shard_map/ppermute | solution.py:540
  55.7 6.4 %collective-permute-start.8 = (s16[16,4224]{1,0:T(8,128)(2,1)S(1)}, s16[16,4224]{1,0:T(8,128)(2,1)S(1)}, u32[]{:S(2)}, u32[]{:S(2)}) collective-permute-start(s16[16,4224]{1,0:T(8,128)(2,1)S(1)} %rest.3.refs_0_), channel_id=1, source_target_pairs={{0,1},{1,0},{2,3},{3,2},{4,5},{5,4},{6,7},{7,6},{8,9},{9,8},{10,11... | collective-permute-start | bytes 405512 | tf_op jit(solution)/shard_map/ppermute | solution.py:538
  57.2 6.3 %collective-permute-start.7 = (s16[16,4224]{1,0:T(8,128)(2,1)S(1)}, s16[16,4224]{1,0:T(8,128)(2,1)S(1)}, u32[]{:S(2)}, u32[]{:S(2)}) collective-permute-start(s16[16,4224]{1,0:T(8,128)(2,1)S(1)} %collective-permute-done.6.refs_1_), channel_id=1, source_target_pairs={{0,1},{1,0},{2,3},{3,2},{4,5},{5,4},{6,7},{7,6},{8,9},{9,8},{10,11... | collective-permute-start | bytes 405512 | tf_op jit(solution)/shard_map/ppermute | solution.py:541

commit v5 on v4

--- a/solution.py
+++ b/solution.py
@@ -153,7 +153,7 @@
     lax.fori_loop(0, chips, one_chip, 0, unroll=2)
 
 
-def blur_body(layout, table, mine, partner, across, passed, inverse, wx, wy, cleared, field):
+def blur_body(layout, table, mine, partner, across, passed, inverse, wx, wy, field):
     views, part, cores, taps, kernels = (
         layout["views"], layout["part"], layout["cores"], layout["taps"], layout["kernels"])
     chip, core, view_here = position(cores)
@@ -186,7 +186,6 @@
             field[at : at + piece.shape[0], planes, :] = piece
             at += piece.shape[0]
     rows_out, planes, columns = inverse.shape
-    cleared[...] = jnp.zeros_like(cleared)
     own_rows = cores * layout["rows_dev"]
     lane = lax.broadcasted_iota(jnp.int32, (SUBLANES, LANES), 1)
 
@@ -235,7 +234,7 @@
                 measured * tile(inverse, row, group, col))
 
 
-def ratio_body(layout, table, arrived, inverse, cleared, placed, field, upward, downward, turned):
+def ratio_body(layout, table, arrived, inverse, placed, field, upward, downward, turned):
     views, cores, slots, taps = layout["views"], layout["cores"], layout["slots"], layout["taps"]
     bricks, per_holder, rows_dev = layout["bricks"], layout["per_holder"], layout["rows_dev"]
     radius = taps // 2
@@ -245,6 +244,7 @@
     pitch = layout["pitch"]
     chip, _, _ = position(cores)
     first_row = chip * cores * rows_dev
+    placed[...] = jnp.zeros_like(placed)
 
     def one_source(source, carry):
         adds = []
@@ -472,16 +472,15 @@
     rows_all = own_rows + radius
     groups = planes * block_width // LANES
     placing = pltpu.VMEM(((per_holder + 1) * groups * layout["pitch"], LANES), f32)
-    inverse, wx, wy, cleared = pl.pallas_call(
+    inverse, wx, wy = pl.pallas_call(
         functools.partial(blur_body, layout),
         out_shape=[
             pltpu.VMEM((rows_all, planes, columns), f32),
             pltpu.VMEM((taps, planes, LANES), f32),
             pltpu.VMEM((taps, planes, LANES), f32),
-            placing,
         ],
         in_specs=[SMEM] + [VMEM] * 4,
-        out_specs=[VMEM] * 4,
+        out_specs=[VMEM] * 3,
         scratch_shapes=[pltpu.VMEM((rows_all + 2 * radius, planes, columns), f32)],
         compiler_params=GRANT,
         name="blur",
@@ -497,13 +496,12 @@
             pltpu.VMEM((2 * radius, planes, columns), jnp.int16),
             pltpu.VMEM((radius, planes, columns), jnp.int16),
         ],
-        in_specs=[SMEM] + [VMEM] * 3,
+        in_specs=[SMEM] + [VMEM] * 2,
         out_specs=[VMEM] * 4,
-        input_output_aliases={3: 0},
         scratch_shapes=[turning],
         compiler_params=GRANT,
         name="ratio",
-    )(table, *near_core(arrived, inverse, cleared))
+    )(table, *near_core(arrived, inverse))
 
     before = lax.ppermute(upward, "brick", up)
     after = lax.ppermute(downward, "brick", down)
@@ -530,15 +528,17 @@
             ],
             compiler_params=GRANT,
             name="rest",
-        )(*near_core(done, before, after, wx, wy, source))
+        )(*near_core(done, before, after, wx, wy), source)
 
     if views == 2:
         turn = [(0, 1), (1, 0)]
         keep = finished(False, mine)
         far = lax.ppermute(keep, "view", turn)
         send = finished(True, partner)
+        far_near = lax.ppermute(send, ("brick", "view"), [
+            (i * views + j, (i ^ 1) * views + 1 - j)
+            for i in range(bricks) for j in range(views)])
         near = lax.ppermute(send, "brick", swap)
-        far_near = lax.ppermute(near, "view", turn)
         out = join(estimate.shape, part, ((False, False), (False, True)), (keep, near))
         out = join(estimate.shape, part, ((True, False),), (far,), out)
         return join(estimate.shape, part, ((True, True),), (far_near,), out)

time: 64.7 us -> 60.6 us (0.937)
  the two profiles are of different devices: /device:TPU:16 before, /device:TPU:17 now
where the time goes in v5:
time: 60.6 us; the launch traced here: 60.3 us
  starting transfers between devices  27.1 us (45%)
  Pallas kernels  19.7 us (33%)
  waiting for transfers between devices  12.2 us (20%)
  other arithmetic  0.86 us (1%)
    ppermute x1, starting transfers between devices, shards(): lax.ppermute(lax.dynamic_index_in_dim(across, 1 - core, 0, keepdims=False...  6.79 us
    all_to_all x1, starting transfers between devices, shards(): arrived = lax.all_to_all(packed, ('brick', 'view'), 0, 0, tiled=True)  6.22 us
    pallas_call x1, Pallas kernels, shards(): pl.pallas_call(functools.partial(blur_body, layout), out_shape=[pltpu.VME...  5.23 us
    pallas_call x1, Pallas kernels, shards(): pl.pallas_call(functools.partial(own_body, layout), out_shape=[edged, plt...  4.32 us
    ppermute x1, starting transfers between devices, shards(): after = lax.ppermute(downward, 'brick', down)  4.26 us
    ppermute x1, waiting for transfers between devices, shards(): lax.ppermute(edges, 'brick', [(i, j) for i in range(bricks) for j in [i +...  4.19 us
    ppermute x1, waiting for transfers between devices, shards(): lax.ppermute(send, ('brick', 'view'), [(i * views + j, (i ^ 1) * views +...  3.68 us
    ppermute x1, starting transfers between devices, shards(): lax.ppermute(edges, 'brick', [(i, j) for i in range(bricks) for j in [i +...  3.37 us
  transfers between devices with their start and end apart: 10, of which 5 were waited for; matrix products, arithmetic and copies ran while one was open for 2% of the time, Pallas kernels for 21%

profile of v5, /device:TPU:17, one launch (start us, length us, event | category | flops | bytes accessed | tf_op | source)
XLA Modules:
  0.0 60.3 jit_solution(5189716834568508869)
XLA Ops:
  0.0 0.0 copy-start.1
  0.0 0.0 copy-start
  0.0 0.0 copy-start.2
  0.0 2.1 %pack.1 = (bf16[8,2,2,2,8,512]{5,4,3,2,1,0:T(8,128)(2,1)}, s16[2,8,16,512]{3,2,1,0:T(8,128)(2,1)S(1)}, f32[8,16,512]{2,1,0:T(8,128)S(1)}, f32[8,16,512]{2,1,0:T(8,128)S(1)}) custom-call(s32[16,2,16]{2,1,0:T(2,128)} %bitcast.17, bf16[16,8,2048]{2,1,0:T(8,128)(2,1)} %bitcast.16, f32[8,64,512]{2,1,0:T(8,128)} %estimate.1), custom_call_target="tpu_custom_call" | custom-call | tf_op jit(solution)/shard_map/pack/pallas_call | solution.py:424
  2.1 6.2 %all-to-all-start = ((bf16[32,2,8,512]{3,2,1,0:T(8,128)(2,1)}), bf16[32,2,8,512]{3,2,1,0:T(8,128)(2,1)S(1)}, u32[]{:S(2)}, u32[]{:S(2)}) async-start(bf16[32,2,8,512]{3,2,1,0:T(8,128)(2,1)} %bitcast.7), calls=%async_computation | async-start | bytes 1048576 | tf_op jit(solution)/shard_map/all_to_all | solution.py:443
  8.4 3.4 %collective-permute-start.2 = (s16[2,8,16,512]{3,2,1,0:T(8,128)(2,1)S(1)}, s16[2,8,16,512]{3,2,1,0:T(8,128)(2,1)S(1)}, u32[]{:S(2)}, u32[]{:S(2)}) collective-permute-start(s16[2,8,16,512]{3,2,1,0:T(8,128)(2,1)S(1)} %get-tuple-element.20), channel_id=1, source_target_pairs={{2,4},{4,2},{6,8},{8,6},{10,12},{12,10},{14,16},{16,14},{18,20},{2... | collective-permute-start | bytes 786440 | tf_op jit(solution)/shard_map/ppermute | solution.py:439
  11.8 0.7 %convert_bitcast_fusion = f32[1,2,16]{2,1,0:T(2,128)S(1)} fusion(s32[1,16,16,2]{2,3,1,0:T(2,128)} %param.8, s32[]{:T(128)S(6)} %select_n.21), kind=kLoop, calls=%fused_computation.5 | loop fusion | flops 32 | bytes 260 | tf_op jit(solution)/shard_map/convert_element_type | solution.py:452
  12.4 0.1 convert_element_type.27
  12.5 0.0 copy-done.1
  12.5 0.0 copy-done
  12.5 0.1 copy.10
  12.6 0.1 reshape_squeeze.3
  12.7 0.0 copy-done.2
  12.7 0.1 pad_maximum_fusion.1
  12.8 1.2 %collective-permute-start = (f32[640]{0:T(1024)S(1)}, f32[640]{0:T(1024)S(1)}, u32[]{:S(2)}, u32[]{:S(2)}) collective-permute-start(f32[640]{0:T(1024)S(1)} %pad_maximum_fusion.1), channel_id=1, source_target_pairs={{0,1},{1,0},{2,3},{3,2},{4,5},{5,4},{6,7},{7,6},{8,9},{9,8},{10,11... | collective-permute-start | bytes 7688 | tf_op jit(solution)/shard_map/ppermute | solution.py:454
  14.0 0.4 collective-permute-start.1
  14.4 4.2 %collective-permute-done.2.across = s16[2,8,16,512]{3,2,1,0:T(8,128)(2,1)S(1)} collective-permute-done((s16[2,8,16,512]{3,2,1,0:T(8,128)(2,1)S(1)}, s16[2,8,16,512]{3,2,1,0:T(8,128)(2,1)S(1)}, u32[]{:S(2)}, u32[]{:S(2)}) %collective-permute-start.2) | collective-permute-done | bytes 262176 | tf_op jit(solution)/shard_map/ppermute | solution.py:439
  18.6 6.8 %collective-permute-start.3 = (s16[8,16,512]{2,1,0:T(8,128)(2,1)S(1)}, s16[8,16,512]{2,1,0:T(8,128)(2,1)S(1)}, u32[]{:S(2)}, u32[]{:S(2)}) collective-permute-start(s16[8,16,512]{2,1,0:T(8,128)(2,1)S(1)} %dynamic-slice_bitcast_fusion), channel_id=1, source_target_pairs={{0,2},{2,0},{4,6},{6,4},{8,10},{10,8},{12,14},{14,12},{16,18},{18,... | collective-permute-start | bytes 393224 | tf_op jit(solution)/shard_map/ppermute | solution.py:463
  25.4 0.0 collective-permute-done
  25.4 0.1 broadcast_select_fusion.1
  25.5 0.0 collective-permute-done.1.partner.source
  25.5 0.9 %collective-permute-done.3.passed = s16[8,16,512]{2,1,0:T(8,128)(2,1)S(1)} collective-permute-done((s16[8,16,512]{2,1,0:T(8,128)(2,1)S(1)}, s16[8,16,512]{2,1,0:T(8,128)(2,1)S(1)}, u32[]{:S(2)}, u32[]{:S(2)}) %collective-permute-start.3) | collective-permute-done | bytes 131104 | tf_op jit(solution)/shard_map/ppermute | solution.py:463
  26.4 5.2 %blur.1 = (f32[20,32,512]{2,1,0:T(8,128)S(1)}, f32[9,32,128]{2,1,0:T(8,128)S(1)}, f32[9,32,128]{2,1,0:T(8,128)S(1)}) custom-call(f32[1280]{0:T(1024)S(1)} %pad_maximum_fusion.table, f32[8,16,512]{2,1,0:T(8,128)S(1)} %get-tuple-element.18.mine.source, f32[8,16,512]{2,1,0:T(8,128)S(1)} %collective-permute-done.1.partner.source, ...), custom_call_target="tpu_custom_call" | custom-call | tf_op jit(solution)/shard_map/blur/pallas_call | solution.py:475
  31.6 0.0 all-to-all-done.arrived
  31.6 2.5 %ratio.1 = (f32[3400,128]{1,0:T(8,128)S(1)}, f32[24,32,512]{2,1,0:T(8,128)S(1)}, s16[8,32,512]{2,1,0:T(8,128)(2,1)S(1)}, s16[4,32,512]{2,1,0:T(8,128)(2,1)S(1)}) custom-call(f32[1280]{0:T(1024)S(1)} %pad_maximum_fusion.table, bf16[32,2,8,512]{3,2,1,0:T(8,128)(2,1)S(1)} %all-to-all-done.arrived, f32[20,32,512]{2,1,0:T(8,128)S(1)} %get-tuple-element.21.inverse), custom_call_target="tpu_custom_call" | custom-call | tf_op jit(solution)/shard_map/ratio/pallas_call | solution.py:491
  34.2 1.9 %collective-permute-start.4 = (s16[8,32,512]{2,1,0:T(8,128)(2,1)S(1)}, s16[8,32,512]{2,1,0:T(8,128)(2,1)S(1)}, u32[]{:S(2)}, u32[]{:S(2)}) collective-permute-start(s16[8,32,512]{2,1,0:T(8,128)(2,1)S(1)} %get-tuple-element.27), channel_id=1, source_target_pairs={{0,4},{2,6},{4,8},{6,10},{8,12},{10,14},{12,16},{14,18},{16,20},{1... | collective-permute-start | bytes 786440 | tf_op jit(solution)/shard_map/ppermute | solution.py:506
  36.1 4.3 %collective-permute-start.5 = (s16[4,32,512]{2,1,0:T(8,128)(2,1)S(1)}, s16[4,32,512]{2,1,0:T(8,128)(2,1)S(1)}, u32[]{:S(2)}, u32[]{:S(2)}) collective-permute-start(s16[4,32,512]{2,1,0:T(8,128)(2,1)S(1)} %get-tuple-element.28), channel_id=1, source_target_pairs={{4,0},{6,2},{8,4},{10,6},{12,8},{14,10},{16,12},{18,14},{20,16},{2... | collective-permute-start | bytes 393224 | tf_op jit(solution)/shard_map/ppermute | solution.py:507
  40.4 4.3 %own.1 = (f32[24,32,512]{2,1,0:T(8,128)S(1)}, f32[16,32,512]{2,1,0:T(8,128)S(1)}) custom-call(f32[3400,128]{1,0:T(8,128)S(1)} %get-tuple-element.22.placed, f32[20,32,512]{2,1,0:T(8,128)S(1)} %get-tuple-element.21.inverse, f32[24,32,512]{2,1,0:T(8,128)S(1)} %get-tuple-element.23.edges, ...), custom_call_target="tpu_custom_call", output_to_operand_aliasing={{0}: (2, {})} | custom-call | tf_op jit(solution)/shard_map/own/pallas_call | solution.py:508
  44.7 3.3 %collective-permute-done.5.after = s16[4,32,512]{2,1,0:T(8,128)(2,1)S(1)} collective-permute-done((s16[4,32,512]{2,1,0:T(8,128)(2,1)S(1)}, s16[4,32,512]{2,1,0:T(8,128)(2,1)S(1)}, u32[]{:S(2)}, u32[]{:S(2)}) %collective-permute-start.5) | collective-permute-done | bytes 131104 | tf_op jit(solution)/shard_map/ppermute | solution.py:507
  48.0 0.0 collective-permute-done.4.before
  48.0 1.8 %rest.2 = s16[16,4224]{1,0:T(8,128)(2,1)S(1)} custom-call(f32[16,32,512]{2,1,0:T(8,128)S(1)} %get-tuple-element.26.done, s16[8,32,512]{2,1,0:T(8,128)(2,1)S(1)} %collective-permute-done.4.before, s16[4,32,512]{2,1,0:T(8,128)(2,1)S(1)} %collective-permute-done.5.after, f32[9,32,128]{2,1,0:T(8,128)S(1)} %get-tuple-element.24.wx, ...), custom_call_target="tpu_custom_call" | custom-call | tf_op jit(solution)/shard_map/rest/pallas_call | solution.py:520
  49.8 0.1 collective-permute-start.8
  49.9 1.1 %rest.3.refs_0_ = s16[16,4224]{1,0:T(8,128)(2,1)S(1)} custom-call(f32[16,32,512]{2,1,0:T(8,128)S(1)} %get-tuple-element.26.done, s16[8,32,512]{2,1,0:T(8,128)(2,1)S(1)} %collective-permute-done.4.before, s16[4,32,512]{2,1,0:T(8,128)(2,1)S(1)} %collective-permute-done.5.after, f32[9,32,128]{2,1,0:T(8,128)S(1)} %get-tuple-element.24.wx, ...), custom_call_target="tpu_custom_call" | custom-call | tf_op jit(solution)/shard_map/rest/pallas_call | solution.py:520
  51.1 1.2 %collective-permute-start.7 = (s16[16,4224]{1,0:T(8,128)(2,1)S(1)}, s16[16,4224]{1,0:T(8,128)(2,1)S(1)}, u32[]{:S(2)}, u32[]{:S(2)}) collective-permute-start(s16[16,4224]{1,0:T(8,128)(2,1)S(1)} %rest.3.refs_0_), channel_id=1, source_target_pairs={{0,1},{1,0},{2,3},{3,2},{4,5},{5,4},{6,7},{7,6},{8,9},{9,8},{10,11... | collective-permute-start | bytes 405512 | tf_op jit(solution)/shard_map/ppermute | solution.py:536
  52.3 1.6 %collective-permute-start.6 = (s16[16,4224]{1,0:T(8,128)(2,1)S(1)}, s16[16,4224]{1,0:T(8,128)(2,1)S(1)}, u32[]{:S(2)}, u32[]{:S(2)}) collective-permute-start(s16[16,4224]{1,0:T(8,128)(2,1)S(1)} %rest.2), channel_id=1, source_target_pairs={{0,3},{1,2},{2,1},{3,0},{4,7},{5,6},{6,5},{7,4},{8,11},{9,10},{10,... | collective-permute-start | bytes 405512 | tf_op jit(solution)/shard_map/ppermute | solution.py:538
  53.9 0.0 collective-permute-done.8.refs_1_
  53.9 0.9 %join.3.refs_1_ = f32[8,64,512]{2,1,0:T(8,128)} custom-call(s16[16,4224]{1,0:T(8,128)(2,1)S(1)} %rest.3.refs_0_, s16[16,4224]{1,0:T(8,128)(2,1)S(1)} %collective-permute-done.8.refs_1_), custom_call_target="tpu_custom_call" | custom-call | tf_op jit(solution)/shard_map/join/pallas_call | solution.py:389
  54.8 0.2 collective-permute-done.7.refs_0_
  55.0 0.8 %join.4.refs_1_ = f32[8,64,512]{2,1,0:T(8,128)} custom-call(s16[16,4224]{1,0:T(8,128)(2,1)S(1)} %collective-permute-done.7.refs_0_, f32[8,64,512]{2,1,0:T(8,128)} %join.3.refs_1_), custom_call_target="tpu_custom_call", output_to_operand_aliasing={{}: (1, {})} | custom-call | tf_op jit(solution)/shard_map/join/pallas_call | solution.py:389
  55.8 3.7 %collective-permute-done.6.refs_0_ = s16[16,4224]{1,0:T(8,128)(2,1)S(1)} collective-permute-done((s16[16,4224]{1,0:T(8,128)(2,1)S(1)}, s16[16,4224]{1,0:T(8,128)(2,1)S(1)}, u32[]{:S(2)}, u32[]{:S(2)}) %collective-permute-start.6) | collective-permute-done | bytes 135200 | tf_op jit(solution)/shard_map/ppermute | solution.py:538
  59.5 0.8 %join.5 = f32[8,64,512]{2,1,0:T(8,128)} custom-call(s16[16,4224]{1,0:T(8,128)(2,1)S(1)} %collective-permute-done.6.refs_0_, f32[8,64,512]{2,1,0:T(8,128)} %join.4.refs_1_), custom_call_target="tpu_custom_call", output_to_operand_aliasing={{}: (1, {})} | custom-call | tf_op jit(solution)/shard_map/join/pallas_call | solution.py:389
  (4 shorter events, 0.0 us)
Async XLA Ops:
  0.0 12.5 %copy-start.1 = (s32[1,256]{1,0:T(1,128)S(1)}, s32[1,256]{1,0:T(1,128)}, u32[]{:S(2)}) copy-start(s32[1,256]{1,0:T(1,128)} %param.9) | copy-start | bytes 3076
  0.0 12.5 %copy-start = (f32[1,2,16,9]{2,1,3,0:T(2,128)S(1)}, f32[1,2,16,9]{2,1,3,0:T(2,128)}, u32[]{:S(2)}) copy-start(f32[1,2,16,9]{2,1,3,0:T(2,128)} %param.11) | copy-start | bytes 3460
  0.0 12.7 %copy-start.2 = (s32[1,64]{1,0:T(1,128)S(1)}, s32[1,64]{1,0:T(1,128)}, u32[]{:S(2)}) copy-start(s32[1,64]{1,0:T(1,128)} %param.10) | copy-start | bytes 772
  2.1 29.5 %all-to-all-start = ((bf16[32,2,8,512]{3,2,1,0:T(8,128)(2,1)}), bf16[32,2,8,512]{3,2,1,0:T(8,128)(2,1)S(1)}, u32[]{:S(2)}, u32[]{:S(2)}) async-start(bf16[32,2,8,512]{3,2,1,0:T(8,128)(2,1)} %bitcast.7), calls=%async_computation | async-start | bytes 1048576 | tf_op jit(solution)/shard_map/all_to_all | solution.py:443
  8.4 10.2 %collective-permute-start.2 = (s16[2,8,16,512]{3,2,1,0:T(8,128)(2,1)S(1)}, s16[2,8,16,512]{3,2,1,0:T(8,128)(2,1)S(1)}, u32[]{:S(2)}, u32[]{:S(2)}) collective-permute-start(s16[2,8,16,512]{3,2,1,0:T(8,128)(2,1)S(1)} %get-tuple-element.20), channel_id=1, source_target_pairs={{2,4},{4,2},{6,8},{8,6},{10,12},{12,10},{14,16},{16,14},{18,20},{2... | collective-permute-start | bytes 786440 | tf_op jit(solution)/shard_map/ppermute | solution.py:439
  12.8 12.6 %collective-permute-start = (f32[640]{0:T(1024)S(1)}, f32[640]{0:T(1024)S(1)}, u32[]{:S(2)}, u32[]{:S(2)}) collective-permute-start(f32[640]{0:T(1024)S(1)} %pad_maximum_fusion.1), channel_id=1, source_target_pairs={{0,1},{1,0},{2,3},{3,2},{4,5},{5,4},{6,7},{7,6},{8,9},{9,8},{10,11... | collective-permute-start | bytes 7688 | tf_op jit(solution)/shard_map/ppermute | solution.py:454
  14.0 11.4 %collective-permute-start.1 = (f32[8,16,512]{2,1,0:T(8,128)S(1)}, f32[8,16,512]{2,1,0:T(8,128)S(1)}, u32[]{:S(2)}, u32[]{:S(2)}) collective-permute-start(f32[8,16,512]{2,1,0:T(8,128)S(1)} %get-tuple-element.19), channel_id=1, source_target_pairs={{0,2},{2,0},{4,6},{6,4},{8,10},{10,8},{12,14},{14,12},{16,18},{18,... | collective-permute-start | bytes 786440 | tf_op jit(solution)/shard_map/ppermute | solution.py:442
  18.6 7.8 %collective-permute-start.3 = (s16[8,16,512]{2,1,0:T(8,128)(2,1)S(1)}, s16[8,16,512]{2,1,0:T(8,128)(2,1)S(1)}, u32[]{:S(2)}, u32[]{:S(2)}) collective-permute-start(s16[8,16,512]{2,1,0:T(8,128)(2,1)S(1)} %dynamic-slice_bitcast_fusion), channel_id=1, source_target_pairs={{0,2},{2,0},{4,6},{6,4},{8,10},{10,8},{12,14},{14,12},{16,18},{18,... | collective-permute-start | bytes 393224 | tf_op jit(solution)/shard_map/ppermute | solution.py:463
  34.2 13.9 %collective-permute-start.4 = (s16[8,32,512]{2,1,0:T(8,128)(2,1)S(1)}, s16[8,32,512]{2,1,0:T(8,128)(2,1)S(1)}, u32[]{:S(2)}, u32[]{:S(2)}) collective-permute-start(s16[8,32,512]{2,1,0:T(8,128)(2,1)S(1)} %get-tuple-element.27), channel_id=1, source_target_pairs={{0,4},{2,6},{4,8},{6,10},{8,12},{10,14},{12,16},{14,18},{16,20},{1... | collective-permute-start | bytes 786440 | tf_op jit(solution)/shard_map/ppermute | solution.py:506
  36.1 11.9 %collective-permute-start.5 = (s16[4,32,512]{2,1,0:T(8,128)(2,1)S(1)}, s16[4,32,512]{2,1,0:T(8,128)(2,1)S(1)}, u32[]{:S(2)}, u32[]{:S(2)}) collective-permute-start(s16[4,32,512]{2,1,0:T(8,128)(2,1)S(1)} %get-tuple-element.28), channel_id=1, source_target_pairs={{4,0},{6,2},{8,4},{10,6},{12,8},{14,10},{16,12},{18,14},{20,16},{2... | collective-permute-start | bytes 393224 | tf_op jit(solution)/shard_map/ppermute | solution.py:507
  49.8 4.1 %collective-permute-start.8 = (s16[16,4224]{1,0:T(8,128)(2,1)S(1)}, s16[16,4224]{1,0:T(8,128)(2,1)S(1)}, u32[]{:S(2)}, u32[]{:S(2)}) collective-permute-start(s16[16,4224]{1,0:T(8,128)(2,1)S(1)} %rest.2), channel_id=1, source_target_pairs={{0,2},{2,0},{4,6},{6,4},{8,10},{10,8},{12,14},{14,12},{16,18},{18,... | collective-permute-start | bytes 405512 | tf_op jit(solution)/shard_map/ppermute | solution.py:541
  51.1 3.9 %collective-permute-start.7 = (s16[16,4224]{1,0:T(8,128)(2,1)S(1)}, s16[16,4224]{1,0:T(8,128)(2,1)S(1)}, u32[]{:S(2)}, u32[]{:S(2)}) collective-permute-start(s16[16,4224]{1,0:T(8,128)(2,1)S(1)} %rest.3.refs_0_), channel_id=1, source_target_pairs={{0,1},{1,0},{2,3},{3,2},{4,5},{5,4},{6,7},{7,6},{8,9},{9,8},{10,11... | collective-permute-start | bytes 405512 | tf_op jit(solution)/shard_map/ppermute | solution.py:536
  52.3 7.2 %collective-permute-start.6 = (s16[16,4224]{1,0:T(8,128)(2,1)S(1)}, s16[16,4224]{1,0:T(8,128)(2,1)S(1)}, u32[]{:S(2)}, u32[]{:S(2)}) collective-permute-start(s16[16,4224]{1,0:T(8,128)(2,1)S(1)} %rest.2), channel_id=1, source_target_pairs={{0,3},{1,2},{2,1},{3,0},{4,7},{5,6},{6,5},{7,4},{8,11},{9,10},{10,... | collective-permute-start | bytes 405512 | tf_op jit(solution)/shard_map/ppermute | solution.py:538
